TPU v7x, 256 devices: a whole 4x4x8 slice. The times are simulated.
256 devices in a mesh: own: 2 (over y_hi), space: 128 (over z, x, y_lo, core).
Axes of the slice: x: 4, y: 4 (y_hi: 2, y_lo: 2; y = y_hi * 2 + y_lo), z: 8, core: 2. Of those that a mesh axis runs over, the one named last changes fastest.
Arguments:
- density: bfloat16 [256, 4, 512, 128], P(None, 'own', 'space'), may hold values from -6 to 6
- cotangent: bfloat16 [256, 4, 512, 128], P(None, 'own', 'space'), may hold values from -6 to 6
- pw_one: bfloat16 [256, 256], P('own'), may hold values from -0.375 to 0.375
- pw_two: bfloat16 [256, 256], P('own'), may hold values from -0.375 to 0.375
- dw_one: bfloat16 [27, 256], P(None, 'own'), may hold values from -1.25 to 1.25
- dw_two: bfloat16 [27, 256], P(None, 'own'), may hold values from -1.25 to 1.25
Outputs:
- grad_input: bfloat16 [256, 4, 512, 128], P(None, 'own', 'space')
- grad_pw_one: float32 [256, 256], P('own')
- grad_pw_two: float32 [256, 256], P('own')
- grad_dw_one: float32 [27, 256], P(None, 'own')
- grad_dw_two: float32 [27, 256], P(None, 'own')
All inputs are finite; a program needn't handle non-finite values.
Results may differ from a plain program's by a relative error of at most 0.01.
Values may be sent and summed in bfloat16 or wider, within the bound.
A program may use at most 192 MiB of HBM per device.

v0:
```python
import functools
import math

import jax
import jax.numpy as jnp
from jax import lax
from jax.experimental import pallas as pl
from jax.experimental.pallas import tpu as pltpu
from jax.sharding import PartitionSpec as P

MESH = pl.DeviceIdType.MESH
TILE = 8 * 128

TAP_LIST = [
    (9 * (a + 1) + 3 * (b + 1) + (d + 1), a, b, d)
    for a in (-1, 0, 1)
    for b in (-1, 0, 1)
    for d in (-1, 0, 1)
]


def extended(value, sides, width):
    for axis, dim in sides:
        size, length = (lax.axis_size(axis), value.shape[dim])
        up = [(i, (i + 1) % size) for i in range(size)]
        down = [(j, i) for i, j in up]
        last = lax.slice_in_dim(value, length - width, length, axis=dim)
        first = lax.slice_in_dim(value, 0, width, axis=dim)
        if size == 2:
            theirs = lax.ppermute(jnp.concatenate([first, last], axis=dim), axis, up)
            after = lax.slice_in_dim(theirs, 0, width, axis=dim)
            before = lax.slice_in_dim(theirs, width, 2 * width, axis=dim)
        else:
            before = lax.ppermute(last, axis, up)
            after = lax.ppermute(first, axis, down)
        value = jnp.concatenate([before, value, after], axis=dim)
    return value


def gather_weights(pw_one, pw_two, dw_one, dw_two):
    mine = jnp.concatenate([pw_one.reshape(-1), pw_two.reshape(-1), dw_one.reshape(-1), dw_two.reshape(-1)])
    theirs = lax.ppermute(mine, "own", [(0, 1), (1, 0)])
    first_half = lax.axis_index("own") == 0
    low = jnp.where(first_half, mine, theirs)
    high = jnp.where(first_half, theirs, mine)
    out, offset = [], 0
    for w, dim in ((pw_one, 0), (pw_two, 0), (dw_one, 1), (dw_two, 1)):
        count = w.size
        parts = [h[offset : offset + count].reshape(w.shape) for h in (low, high)]
        out.append(jnp.concatenate(parts, axis=dim))
        offset += count
    return out


def ring_z(padded):
    return jnp.concatenate([padded[..., -1:], padded, padded[..., :1]], axis=3)


def depthwise(padded, weights, extent_x, extent_y, direction):
    extent_z = padded.shape[3]
    wide = ring_z(padded)
    running = jnp.zeros((padded.shape[0], extent_x, extent_y, extent_z), jnp.float32)
    for k, a, b, d in TAP_LIST:
        start_x = 1 + direction * a
        start_y = 1 + direction * b
        start_z = 1 + direction * d
        shifted = wide[:, start_x : start_x + extent_x, start_y : start_y + extent_y, start_z : start_z + extent_z]
        running = running + weights[k].astype(jnp.float32)[:, None, None, None] * shifted.astype(jnp.float32)
    return running


def tap_sums(padded, gradient):
    extent_x, extent_y, extent_z = gradient.shape[1:]
    wide = ring_z(padded)
    grad_float = gradient.astype(jnp.float32)
    columns = []
    for k, a, b, d in TAP_LIST:
        shifted = wide[:, 1 + a : 1 + a + extent_x, 1 + b : 1 + b + extent_y, 1 + d : 1 + d + extent_z]
        columns.append(jnp.sum(shifted.astype(jnp.float32) * grad_float, axis=(1, 2, 3)))
    return jnp.stack(columns, axis=0)


def pointwise(weights, source):
    layout = source.shape
    flattened = source.reshape(layout[0], -1)
    return jnp.dot(weights.T, flattened, preferred_element_type=jnp.float32).reshape(layout)


def backmap(weights, source):
    layout = source.shape
    flattened = source.reshape(layout[0], -1)
    return jnp.dot(weights, flattened, preferred_element_type=jnp.float32).reshape(layout)


def contract_cells(left, right):
    channels = left.shape[0]
    return lax.dot_general(
        left.reshape(channels, -1),
        right.reshape(channels, -1),
        (((1,), (1,)), ((), ())),
        preferred_element_type=jnp.float32,
    )


def reduce_plan(space_size):
    if space_size == 128:
        scatter = ((("own", 0, 2), ("space", 1, 2)), (("space", 2, 2), ("space", 4, 4)))
        return scatter, (("space", 16, 8),)
    factors, stride, rest = [], 1, space_size
    while rest > 2:
        factors.append(("space", stride, 2))
        stride, rest = stride * 2, rest // 2
    scatter = ((("own", 0, 2),) + tuple(factors[:1]),) + tuple((f,) for f in factors[1:])
    return scatter, (("space", stride, rest),)


def group_size(group):
    return math.prod(f[2] for f in group)


def reduce_kernel(plan, x_ref, o_ref, *refs):
    scatter, last = plan
    count = len(scatter)
    bufs = refs[:count]
    recvs = refs[count : 2 * count]
    recv_last, res, send_sem, recv_sem = refs[2 * count :]
    own = lax.axis_index("own")
    space = lax.axis_index("space")

    def coord(factor):
        axis, stride, size = factor
        return own if axis == "own" else (space // stride) % size

    def member(group):
        index = 0
        for factor in group:
            index = index * factor[2] + coord(factor)
        return index

    def device(group, target):
        new_own, new_space = own, space
        for factor in reversed(group):
            axis, stride, size = factor
            value = target % size
            target = target // size
            if axis == "own":
                new_own = value
            else:
                new_space = new_space + (value - coord(factor)) * stride
        return (new_own, new_space)

    barrier = pltpu.get_barrier_semaphore()
    partners = 0
    for group in scatter + (last,):
        size, me = group_size(group), member(group)
        for d in range(1, size):
            pl.semaphore_signal(
                barrier, 1, device_id=device(group, (me + d) % size), device_id_type=MESH
            )
            partners += 1
    pl.semaphore_wait(barrier, partners)

    def exchange(group, base, source_of, dest_of):
        size, me = group_size(group), member(group)
        sends = []
        for d in range(1, size):
            target = (me + d) % size
            copy = pltpu.make_async_remote_copy(
                src_ref=source_of(target),
                dst_ref=dest_of(me),
                send_sem=send_sem.at[base + target],
                recv_sem=recv_sem.at[base + me],
                device_id=device(group, target),
                device_id_type=MESH,
            )
            copy.start()
            sends.append(copy)
        return sends

    def finish(group, base, source_of, dest_of, sends):
        size, me = group_size(group), member(group)
        for d in range(1, size):
            sender = (me + d) % size
            pltpu.make_async_remote_copy(
                src_ref=source_of(sender),
                dst_ref=dest_of(sender),
                send_sem=send_sem.at[base + sender],
                recv_sem=recv_sem.at[base + sender],
                device_id=device(group, sender),
                device_id_type=MESH,
            ).wait_recv()
        for copy in sends:
            copy.wait_send()

    base = 0
    source = x_ref
    for i, group in enumerate(scatter):
        size, me = group_size(group), member(group)
        piece = source.shape[0] // size
        src_of = lambda t, s=source, n=piece: s.at[pl.ds(t * n, n)]
        dst_of = lambda t, r=recvs[i]: r.at[t]
        sends = exchange(group, base, src_of, dst_of)
        finish(group, base, src_of, dst_of, sends)
        total = source[pl.ds(me * piece, piece)]
        for d in range(1, size):
            total = total + recvs[i][(me + d) % size]
        bufs[i][...] = total
        source = bufs[i]
        base += size

    size, me = group_size(last), member(last)
    piece = source.shape[0]
    src_of = lambda t, s=source: s
    dst_of = lambda t: recv_last.at[t]
    sends = exchange(last, base, src_of, dst_of)
    recv_last[me] = source[...]
    finish(last, base, src_of, dst_of, sends)
    total = recv_last[0]
    for k in range(1, size):
        total = total + recv_last[k]
    space_factors = [f for group in scatter for f in group if f[0] != "own"]
    block = 0
    for factor in space_factors:
        block = block * factor[2] + coord(factor)
    res[pl.ds(block * piece, piece)] = total
    base += size

    span = piece
    gathers = [tuple(f for f in group if f[0] != "own") for group in scatter]
    for j in range(len(gathers) - 1, -1, -1):
        group = gathers[j]
        if not group:
            continue
        size, me = group_size(group), member(group)
        prefix = 0
        for earlier in gathers[:j]:
            prefix = prefix * group_size(earlier) + member(earlier)
        start = prefix * size * span
        src_of = lambda t, a=start, n=span: res.at[pl.ds(a + t * n, n)]
        sends = []
        for d in range(1, size):
            target = (me + d) % size
            copy = pltpu.make_async_remote_copy(
                src_ref=src_of(me),
                dst_ref=src_of(me),
                send_sem=send_sem.at[base + target],
                recv_sem=recv_sem.at[base + me],
                device_id=device(group, target),
                device_id_type=MESH,
            )
            copy.start()
            sends.append(copy)
        finish(group, base, src_of, src_of, sends)
        span *= size
        base += size
    o_ref[...] = res[...]


def tree_reduce(packed):
    plan = reduce_plan(lax.axis_size("space"))
    scatter, last = plan
    half = packed.shape[0] // 2
    shapes, length = [], packed.shape[0]
    for group in scatter:
        length //= group_size(group)
        shapes.append((group_size(group), length))
    semaphores = sum(group_size(group) for group in scatter) * 2 + group_size(last)
    scratch = [pltpu.VMEM((n, 8, 128), jnp.float32) for _, n in shapes]
    scratch += [pltpu.VMEM((size, n, 8, 128), jnp.float32) for size, n in shapes]
    scratch += [
        pltpu.VMEM((group_size(last), length, 8, 128), jnp.float32),
        pltpu.VMEM((half, 8, 128), jnp.float32),
        pltpu.SemaphoreType.DMA((semaphores,)),
        pltpu.SemaphoreType.DMA((semaphores,)),
    ]
    return pl.pallas_call(
        functools.partial(reduce_kernel, plan),
        out_shape=jax.ShapeDtypeStruct((half, 8, 128), jnp.float32),
        in_specs=[pl.BlockSpec(memory_space=pltpu.VMEM)],
        out_specs=pl.BlockSpec(memory_space=pltpu.VMEM),
        scratch_shapes=scratch,
        compiler_params=pltpu.CompilerParams(collective_id=0, has_side_effects=True),
        cost_estimate=pl.CostEstimate(
            flops=0, transcendentals=0, bytes_accessed=64 * packed.size * 4
        ),
    )(packed)


def pack_halves(parts, blocks):
    halves = []
    for h in range(2):
        pieces = []
        for p in parts[:2]:
            rows = p.shape[0] // 2
            pieces.append(p[h * rows : (h + 1) * rows].reshape(-1))
        for p in parts[2:]:
            cols = p.shape[1] // 2
            pieces.append(p[:, h * cols : (h + 1) * cols].reshape(-1))
        halves.append(jnp.concatenate(pieces))
    real = halves[0].shape[0]
    tiles = -(-real // (TILE * blocks)) * blocks
    flat = jnp.stack(halves)
    flat = jnp.pad(flat, ((0, 0), (0, tiles * TILE - real)))
    return flat.reshape(2 * tiles, 8, 128), real


def unpack_half(reduced, parts):
    flat = reduced.reshape(-1)
    out, offset = [], 0
    for p in parts[:2]:
        shape = (p.shape[0] // 2, p.shape[1])
        out.append(flat[offset : offset + shape[0] * shape[1]].reshape(shape))
        offset += shape[0] * shape[1]
    for p in parts[2:]:
        shape = (p.shape[0], p.shape[1] // 2)
        out.append(flat[offset : offset + shape[0] * shape[1]].reshape(shape))
        offset += shape[0] * shape[1]
    return out


def shards(density, cotangent, pw_one, pw_two, dw_one, dw_two):
    channels, extent_x, extent_y, extent_z = density.shape
    assert lax.axis_size("own") == 2
    weight_one, weight_two, taps_one, taps_two = gather_weights(pw_one, pw_two, dw_one, dw_two)
    rim_width = 1
    wide_input = extended(density, (("own", 1), ("space", 2)), rim_width)
    first = depthwise(wide_input, taps_one, extent_x, extent_y, 1).astype(jnp.bfloat16)
    pre = pointwise(weight_one, first)
    act = jax.nn.silu(pre).astype(jnp.bfloat16)
    act_padded = extended(act, (("own", 1), ("space", 2)), 1)
    second = depthwise(act_padded, taps_two, extent_x, extent_y, 1).astype(jnp.bfloat16)
    grad_second = backmap(weight_two, cotangent).astype(jnp.bfloat16)
    second_padded = extended(grad_second, (("own", 1), ("space", 2)), 1)
    sigma = jax.nn.sigmoid(pre)
    grad_pre = (
        depthwise(second_padded, taps_two, extent_x, extent_y, -1)
        * (sigma * (1.0 + pre * (1.0 - sigma)))
    ).astype(jnp.bfloat16)
    grad_first = backmap(weight_one, grad_pre).astype(jnp.bfloat16)
    first_padded = extended(grad_first, (("own", 1), ("space", 2)), 1)
    grad_input = (
        cotangent.astype(jnp.float32) + depthwise(first_padded, taps_one, extent_x, extent_y, -1)
    ).astype(jnp.bfloat16)
    total_cells = extent_x * extent_y * extent_z * lax.axis_size("own") * lax.axis_size("space")
    grad_scale = 1.0 / math.sqrt(float(total_cells))
    local_pw_one = contract_cells(first, grad_pre) * grad_scale
    local_pw_two = contract_cells(second, cotangent) * grad_scale
    local_dw_one = tap_sums(wide_input, grad_first) * grad_scale
    local_dw_two = tap_sums(act_padded, grad_second) * grad_scale
    partials = (local_pw_one, local_pw_two, local_dw_one, local_dw_two)
    scatter, _ = reduce_plan(lax.axis_size("space"))
    blocks = math.prod(f[2] for group in scatter for f in group if f[0] != "own")
    packed, _ = pack_halves(partials, blocks)
    result = unpack_half(tree_reduce(packed), partials)
    return (grad_input, result[0], result[1], result[2], result[3])


def solution(mesh):
    in_specs = (
        P(None, "own", "space", None),
        P(None, "own", "space", None),
        P("own", None),
        P("own", None),
        P(None, "own"),
        P(None, "own"),
    )
    out_specs = (
        P(None, "own", "space", None),
        P("own", None),
        P("own", None),
        P(None, "own"),
        P(None, "own"),
    )
    return jax.shard_map(shards, mesh=mesh, in_specs=in_specs, out_specs=out_specs, check_vma=False)
```

profile of v0, /device:TPU:1, one launch (start us, length us, event | category | flops | bytes accessed | tf_op | source)
XLA Modules:
  0.0 174.0 jit_solution(13069155628262151370)
XLA Ops:
  0.6 0.9 copy.30
  1.5 0.9 copy.31
  2.4 0.7 pad_maximum_fusion.60
  3.2 3.8 %collective-permute-start = (bf16[72448]{0:T(1024)(128)(2,1)S(1)}, bf16[72448]{0:T(1024)(128)(2,1)S(1)}, u32[]{:S(2)}, u32[]{:S(2)}) collective-permute-start(bf16[72448]{0:T(1024)(128)(2,1)S(1)} %pad_maximum_fusion.60), channel_id=1, source_target_pairs={{0,128},{128,0},{1,129},{129,1},{2,130},{130,2},{3,131},{131,3},{4... | collective-permute-start | bytes 434696 | tf_op jit(solution)/shard_map/ppermute | solution.py:42
  7.0 1.3 copy.13
  8.4 1.1 collective-permute-done
  9.5 0.8 broadcast_select_fusion.1
  10.3 0.7 fusion.296
  11.0 11.6 %collective-permute-done.4 = bf16[256,2,4,128]{0,3,2,1:T(8,128)(2,1)S(1)} collective-permute-done((bf16[256,2,4,128]{0,3,2,1:T(8,128)(2,1)S(1)}, bf16[256,2,4,128]{0,3,2,1:T(8,128)(2,1)S(1)}, u32[]{:S(2)}, u32[]{:S(2)}) %collective-permute-start.4) | collective-permute-done | bytes 524320 | tf_op jit(solution)/shard_map/ppermute | solution.py:30
  22.7 2.0 %collective-permute-start.5 = (bf16[256,4,1,128]{0,3,2,1:T(8,128)(2,1)S(1)}, bf16[256,4,1,128]{0,3,2,1:T(8,128)(2,1)S(1)}, u32[]{:S(2)}, u32[]{:S(2)}) collective-permute-start(bf16[256,4,1,128]{0,3,2,1:T(8,128)(2,1)S(1)} %get-tuple-element.108), channel_id=1, source_target_pairs={{0,1},{1,2},{2,3},{3,4},{4,5},{5,6},{6,7},{7,8},{8,9},{9,10},{10,1... | collective-permute-start | bytes 786440 | tf_op jit(solution)/shard_map/ppermute | solution.py:34
  24.7 0.6 slice.924
  25.4 0.6 slice.926
  26.2 1.8 %collective-permute-done.5 = bf16[256,4,1,128]{0,3,2,1:T(8,128)(2,1)S(1)} collective-permute-done((bf16[256,4,1,128]{0,3,2,1:T(8,128)(2,1)S(1)}, bf16[256,4,1,128]{0,3,2,1:T(8,128)(2,1)S(1)}, u32[]{:S(2)}, u32[]{:S(2)}) %collective-permute-start.5) | collective-permute-done | bytes 262176 | tf_op jit(solution)/shard_map/ppermute | solution.py:34
  28.0 2.5 %collective-permute-done.6 = bf16[256,4,1,128]{0,3,2,1:T(8,128)(2,1)S(1)} collective-permute-done((bf16[256,4,1,128]{0,3,2,1:T(8,128)(2,1)S(1)}, bf16[256,4,1,128]{0,3,2,1:T(8,128)(2,1)S(1)}, u32[]{:S(2)}, u32[]{:S(2)}) %collective-permute-start.6) | collective-permute-done | bytes 262176 | tf_op jit(solution)/shard_map/ppermute | solution.py:35
  30.8 0.7 fusion.5
  32.0 0.7 copy-done
  32.8 4.2 %fusion.36 = bf16[256,2,4,128]{0,3,2,1:T(8,128)(2,1)S(1)} fusion(bf16[256,2,4,128]{0,3,2,1:T(8,128)(2,1)S(1)} %copy.13, f32[256]{0:T(256)S(1)} %bitcast.227, f32[256]{0:T(256)S(1)} %bitcast.229, f32[256]{0:T(256)S(1)} %bitcast.225, f32[256]{0:T(256)S(1)} %bitcast.223, f32[256]{0:T(256)S(1)} %bitcast.221, f32[256]{0:T(256)S(1)} %bitcast.219, ...), kind=kLoop, calls=%fused_computation.190 | loop fusion | flops 21757952 | bytes 14183424 | tf_op jit(solution)/shard_map/convert_element_type | solution.py:327
  37.1 1.3 multiply_convert_fusion
  38.4 2.3 %collective-permute-start.10 = (bf16[256,2,4,128]{0,3,2,1:T(8,128)(2,1)S(1)}, bf16[256,2,4,128]{0,3,2,1:T(8,128)(2,1)}, u32[]{:S(2)}, u32[]{:S(2)}) collective-permute-start(bf16[256,2,4,128]{0,3,2,1:T(8,128)(2,1)S(1)} %get-tuple-element.194), channel_id=1, source_target_pairs={{0,128},{128,0},{1,129},{129,1},{2,130},{130,2},{3,131},{131,3},{4... | collective-permute-start | bytes 1572872 | tf_op jit(solution)/shard_map/ppermute | solution.py:30
  40.7 1.1 copy.11
  41.9 1.2 reshape.539
  43.0 2.1 %copy.12 = bf16[1024,256]{1,0:T(8,128)(2,1)} copy(bf16[1024,256]{0,1:T(8,128)(2,1)} %bitcast.196) | data formatting | bytes 1048576 | tf_op jit(solution)/shard_map/dot_general | solution.py:92
  45.1 4.0 %collective-permute-done.10 = bf16[256,2,4,128]{0,3,2,1:T(8,128)(2,1)} collective-permute-done((bf16[256,2,4,128]{0,3,2,1:T(8,128)(2,1)S(1)}, bf16[256,2,4,128]{0,3,2,1:T(8,128)(2,1)}, u32[]{:S(2)}, u32[]{:S(2)}) %collective-permute-start.10) | collective-permute-done | bytes 524320 | tf_op jit(solution)/shard_map/ppermute | solution.py:30
  49.0 1.1 fusion.290
  50.1 1.0 pad_maximum_fusion.50
  51.1 3.4 %collective-permute-start.11 = (bf16[256,4,1,128]{0,3,2,1:T(8,128)(2,1)}, bf16[256,4,1,128]{0,3,2,1:T(8,128)(2,1)}, u32[]{:S(2)}, u32[]{:S(2)}) collective-permute-start(bf16[256,4,1,128]{0,3,2,1:T(8,128)(2,1)} %get-tuple-element.96), channel_id=1, source_target_pairs={{0,1},{1,2},{2,3},{3,4},{4,5},{5,6},{6,7},{7,8},{8,9},{9,10},{10,1... | collective-permute-start | bytes 786440 | tf_op jit(solution)/shard_map/ppermute | solution.py:34
  54.5 1.9 %collective-permute-start.12 = (bf16[256,4,1,128]{0,3,2,1:T(8,128)(2,1)}, bf16[256,4,1,128]{0,3,2,1:T(8,128)(2,1)}, u32[]{:S(2)}, u32[]{:S(2)}) collective-permute-start(bf16[256,4,1,128]{0,3,2,1:T(8,128)(2,1)} %get-tuple-element.97), channel_id=1, source_target_pairs={{1,0},{2,1},{3,2},{4,3},{5,4},{6,5},{7,6},{8,7},{9,8},{10,9},{11,1... | collective-permute-start | bytes 786440 | tf_op jit(solution)/shard_map/ppermute | solution.py:35
  56.4 0.6 fusion.266
  57.0 1.5 slice.933
  58.5 1.5 slice.935
  60.2 0.8 collective-permute-done.12
  61.1 1.7 fusion.1
  62.8 1.3 maximum_maximum_fusion.3
  64.2 2.6 %fusion.104 = (f32[256]{0:T(256)}, f32[256]{0:T(256)}, f32[256]{0:T(256)}, f32[256]{0:T(256)}, f32[256]{0:T(256)}, /*index=5*/f32[256]{0:T(256)}, f32[256]{0:T(2...) fusion(bf16[256,4,5,128]{0,3,2,1:T(8,128)(2,1)S(1)} %get-tuple-, ...), kind=kOutput, calls=%fused_computation.258 | convolution fusion | flops 144438272 | bytes 7483392 | tf_op jit(solution)/shard_map/dot_general | solution.py:92
  66.8 2.7 %collective-permute-start.1 = (bf16[256,2,4,128]{0,3,2,1:T(8,128)(2,1)S(1)}, bf16[256,2,4,128]{0,3,2,1:T(8,128)(2,1)}, u32[]{:S(2)}, u32[]{:S(2)}) collective-permute-start(bf16[256,2,4,128]{0,3,2,1:T(8,128)(2,1)S(1)} %get-tuple-element.196), channel_id=1, source_target_pairs={{0,128},{128,0},{1,129},{129,1},{2,130},{130,2},{3,131},{131,3},{4... | collective-permute-start | bytes 1572872 | tf_op jit(solution)/shard_map/ppermute | solution.py:30
  69.5 1.3 fusion
  71.2 5.1 %fusion.8 = f32[256,256]{1,0:T(8,128)} fusion(bf16[256,2,4,128]{0,3,2,1:T(8,128)(2,1)S(1)} %copy-done.10, bf16[256,2,4,128]{0,3,2,1:T(8,128)(2,1)S(1)} %get-tuple-element.194, f32[256]{0:T(256)S(1)} %bitcast.311, f32[256]{0:T(256)S(1)} %bitcast.313, f32[256]{0:T(256)S(1)} %bitcast.309, f32[256]{0:T(256)S(1)} %bitcast.307, f32[256]{0:T(256)S(1)} %bitcast.305, ...), kind=kOutput, calls=%fused_computation.161 | convolution fusion | flops 156041216 | bytes 14445568 | tf_op jit(solution)/shard_map/dot_general | solution.py:97
  76.2 3.2 %fusion.105 = (f32[256]{0:T(256)S(1)}, f32[256]{0:T(256)S(1)}, f32[256]{0:T(256)S(1)}, f32[256]{0:T(256)S(1)}, f32[256]{0:T(256)}, /*index=5*/f32[256]{0:T(256)}...) fusion(bf16[256,2,4,128]{0,3,2,1:T(8,128)(2,1)S(1)} %get-tuple-, ...), kind=kLoop, calls=%fused_computation.259 | loop fusion | flops 12579072 | bytes 7879680 | tf_op jit(solution)/shard_map/reduce_sum | solution.py:79
  79.4 2.9 %stack.232 = f32[27,256]{1,0:T(8,128)S(1)} concatenate(f32[1,256]{1,0:T(1,128)} %bitcast.355, f32[1,256]{1,0:T(1,128)} %bitcast.291, f32[1,256]{1,0:T(1,128)} %bitcast.290, f32[1,256]{1,0:T(1,128)} %bitcast.354, f32[1,256]{1,0:T(1,128)} %bitcast.295, f32[1,256]{1,0:T(1,128)S(1)} %bitcast.283, f32[1,256]{1,0:T(1,128)} %bitcast.361, f32[1,256]{1,0:T(1,128)} %bitcast.352, ...), dimensions={0} | concatenate | bytes 55296 | tf_op jit(solution)/shard_map/stack | solution.py:80
  82.3 1.0 slice_bitcast_fusion.2
  83.3 1.1 fusion.292
  84.5 9.9 %collective-permute-start.3 = (bf16[256,4,1,128]{0,3,2,1:T(8,128)(2,1)S(1)}, bf16[256,4,1,128]{0,3,2,1:T(8,128)(2,1)S(1)}, u32[]{:S(2)}, u32[]{:S(2)}) collective-permute-start(bf16[256,4,1,128]{0,3,2,1:T(8,128)(2,1)S(1)} %get-tuple-element.105), channel_id=1, source_target_pairs={{1,0},{2,1},{3,2},{4,3},{5,4},{6,5},{7,6},{8,7},{9,8},{10,9},{11,1... | collective-permute-start | bytes 786440 | tf_op jit(solution)/shard_map/ppermute | solution.py:35
  94.6 0.6 collective-permute-done.2
  95.1 0.4 collective-permute-done.3
  95.6 0.7 fusion.6
  97.1 0.7 copy-done.14
  98.1 4.8 %fusion.149 = bf16[256,2,4,128]{0,3,2,1:T(8,128)(2,1)S(1)} fusion(f32[256,2,4,128]{0,3,2,1:T(8,128)S(1)} %copy-done.14, bf16[256,2,4,128]{0,3,2,1:T(8,128)(2,1)S(1)} %get-tuple-element.196, bf16[256,4,6,129]{0,3,2,1:T(8,128)(2,1)S(1)} %fusion.6, bf16[256,4,5,128]{0,3,2,1:T(8,128)(2,1)S(1)} %get-tuple-element.103, bf16[256,4,6,129]{0,3,2,1:T(8,128)(2,1)S(1)} %fusion.7, ...), kind=kLoop, calls=%fused_computation.305 | loop fusion | flops 23855104 | bytes 15232000 | tf_op jit(solution)/shard_map/convert_element_type | solution.py:338
  102.9 4.3 %fusion.146 = (f32[256]{0:T(256)S(1)}, f32[256]{0:T(256)S(1)}, f32[256]{0:T(256)S(1)}, f32[256]{0:T(256)S(1)}, f32[256]{0:T(256)S(1)}, /*index=5*/f32[256]{0:T(2...) fusion(bf16[256,4,5,128]{0,3,2,1:T(8,128)(2,1)} %copy-done.9, ...), kind=kOutput, calls=%fused_computation.300 | convolution fusion | flops 144438272 | bytes 7483392 | tf_op jit(solution)/shard_map/dot_general | solution.py:92
  107.6 1.0 copy-done.2
  108.5 2.6 %fusion.147 = (f32[256]{0:T(256)S(1)}, f32[256]{0:T(256)S(1)}, f32[256]{0:T(256)S(1)}, f32[256]{0:T(256)S(1)}, f32[256]{0:T(256)S(1)}, /*index=5*/f32[256]{0:T(2...) fusion(bf16[256,2,4,128]{0,3,2,1:T(8,128)(2,1)S(1)} %get-tuple-, ...), kind=kLoop, calls=%fused_computation.301 | loop fusion | flops 12579072 | bytes 7879680 | tf_op jit(solution)/shard_map/reduce_sum | solution.py:79
  111.1 0.5 collective-permute-start.7
  112.4 0.5 select_maximum_fusion
  112.9 1.4 reshape.550.x_ref
  114.3 44.6 %shard_map.101 = f32[80,8,128]{2,1,0:T(8,128)} custom-call(f32[160,8,128]{2,1,0:T(8,128)} %reshape.550.x_ref), custom_call_target="tpu_custom_call" | custom-call | bytes 41943040 | tf_op jit(solution)/shard_map/pallas_call | solution.py:276
  159.1 0.8 collective-permute-start.8
  160.0 0.7 reshape.552
  160.7 0.7 reshape.551
  161.4 0.6 fusion.294
  162.0 4.1 %collective-permute-done.8 = bf16[256,4,1,128]{0,3,2,1:T(8,128)(2,1)S(1)} collective-permute-done((bf16[256,4,1,128]{0,3,2,1:T(8,128)(2,1)S(1)}, bf16[256,4,1,128]{0,3,2,1:T(8,128)(2,1)S(1)}, u32[]{:S(2)}, u32[]{:S(2)}) %collective-permute-start.8) | collective-permute-done | bytes 262176 | tf_op jit(solution)/shard_map/ppermute | solution.py:34
  166.1 0.7 fusion.2
  166.8 0.3 fusion.3
  167.5 0.6 copy-done.11
  168.3 4.6 %fusion.148 = bf16[256,2,4,128]{0,3,2,1:T(8,128)(2,1)S(1)} fusion(bf16[256,2,4,128]{0,3,2,1:T(8,128)(2,1)S(1)} %get-tuple-element.197, bf16[256,2,4,128]{0,3,2,1:T(8,128)(2,1)S(1)} %copy-done.11, bf16[256,4,6,129]{0,3,2,1:T(8,128)(2,1)S(1)} %fusion.2, bf16[256,4,5,128]{0,3,2,1:T(8,128)(2,1)S(1)} %get-tuple-element.99, ...), kind=kLoop, calls=%fused_computation.304 | loop fusion | flops 22282240 | bytes 14707712 | tf_op jit(solution)/shard_map/convert_element_type | solution.py:343
  172.9 1.1 copy.22
  (268 shorter events, 3.6 us)
Async XLA Ops:
  3.2 6.3 %collective-permute-start = (bf16[72448]{0:T(1024)(128)(2,1)S(1)}, bf16[72448]{0:T(1024)(128)(2,1)S(1)}, u32[]{:S(2)}, u32[]{:S(2)}) collective-permute-start(bf16[72448]{0:T(1024)(128)(2,1)S(1)} %pad_maximum_fusion.60), channel_id=1, source_target_pairs={{0,128},{128,0},{1,129},{129,1},{2,130},{130,2},{3,131},{131,3},{4... | collective-permute-start | bytes 434696 | tf_op jit(solution)/shard_map/ppermute | solution.py:42
  8.3 14.3 %collective-permute-start.4 = (bf16[256,2,4,128]{0,3,2,1:T(8,128)(2,1)S(1)}, bf16[256,2,4,128]{0,3,2,1:T(8,128)(2,1)S(1)}, u32[]{:S(2)}, u32[]{:S(2)}) collective-permute-start(bf16[256,2,4,128]{0,3,2,1:T(8,128)(2,1)S(1)} %copy.13), channel_id=1, source_target_pairs={{0,128},{128,0},{1,129},{129,1},{2,130},{130,2},{3,131},{131,3},{4... | collective-permute-start | bytes 1572872 | tf_op jit(solution)/shard_map/ppermute | solution.py:30
  22.6 9.2 %copy-start.3 = (bf16[256,1,4,128]{0,3,2,1:T(8,128)(2,1)}, bf16[256,1,4,128]{0,3,2,1:T(8,128)(2,1)S(1)}, u32[]{:S(2)}) copy-start(bf16[256,1,4,128]{0,3,2,1:T(8,128)(2,1)S(1)} %get-tuple-element.117) | copy-start | bytes 786436
  22.7 5.3 %collective-permute-start.5 = (bf16[256,4,1,128]{0,3,2,1:T(8,128)(2,1)S(1)}, bf16[256,4,1,128]{0,3,2,1:T(8,128)(2,1)S(1)}, u32[]{:S(2)}, u32[]{:S(2)}) collective-permute-start(bf16[256,4,1,128]{0,3,2,1:T(8,128)(2,1)S(1)} %get-tuple-element.108), channel_id=1, source_target_pairs={{0,1},{1,2},{2,3},{3,4},{4,5},{5,6},{6,7},{7,8},{8,9},{9,10},{10,1... | collective-permute-start | bytes 786440 | tf_op jit(solution)/shard_map/ppermute | solution.py:34
  24.7 5.8 %collective-permute-start.6 = (bf16[256,4,1,128]{0,3,2,1:T(8,128)(2,1)S(1)}, bf16[256,4,1,128]{0,3,2,1:T(8,128)(2,1)S(1)}, u32[]{:S(2)}, u32[]{:S(2)}) collective-permute-start(bf16[256,4,1,128]{0,3,2,1:T(8,128)(2,1)S(1)} %get-tuple-element.109), channel_id=1, source_target_pairs={{1,0},{2,1},{3,2},{4,3},{5,4},{6,5},{7,6},{8,7},{9,8},{10,9},{11,1... | collective-permute-start | bytes 786440 | tf_op jit(solution)/shard_map/ppermute | solution.py:35
  24.7 7.1 %copy-start.24 = (f32[1,256]{1,0:T(1,128)}, f32[1,256]{1,0:T(1,128)S(1)}, u32[]{:S(2)}) copy-start(f32[1,256]{1,0:T(1,128)S(1)} %get-tuple-element.193) | copy-start | bytes 3076
  26.0 5.8 %copy-start.26 = (f32[1,256]{1,0:T(1,128)}, f32[1,256]{1,0:T(1,128)S(1)}, u32[]{:S(2)}) copy-start(f32[1,256]{1,0:T(1,128)S(1)} %get-tuple-element.167) | copy-start | bytes 3076
  26.1 5.8 %copy-start.28 = (f32[1,256]{1,0:T(1,128)}, f32[1,256]{1,0:T(1,128)S(1)}, u32[]{:S(2)}) copy-start(f32[1,256]{1,0:T(1,128)S(1)} %get-tuple-element.168) | copy-start | bytes 3076
  26.1 5.8 %copy-start.30 = (f32[1,256]{1,0:T(1,128)}, f32[1,256]{1,0:T(1,128)S(1)}, u32[]{:S(2)}) copy-start(f32[1,256]{1,0:T(1,128)S(1)} %get-tuple-element.169) | copy-start | bytes 3076
  26.1 5.8 %copy-start.32 = (f32[1,256]{1,0:T(1,128)}, f32[1,256]{1,0:T(1,128)S(1)}, u32[]{:S(2)}) copy-start(f32[1,256]{1,0:T(1,128)S(1)} %get-tuple-element.170) | copy-start | bytes 3076
  26.1 5.8 %copy-start.34 = (f32[1,256]{1,0:T(1,128)}, f32[1,256]{1,0:T(1,128)S(1)}, u32[]{:S(2)}) copy-start(f32[1,256]{1,0:T(1,128)S(1)} %get-tuple-element.171) | copy-start | bytes 3076
  26.1 5.8 %copy-start.36 = (f32[1,256]{1,0:T(1,128)}, f32[1,256]{1,0:T(1,128)S(1)}, u32[]{:S(2)}) copy-start(f32[1,256]{1,0:T(1,128)S(1)} %get-tuple-element.172) | copy-start | bytes 3076
  26.1 5.8 %copy-start.38 = (f32[1,256]{1,0:T(1,128)}, f32[1,256]{1,0:T(1,128)S(1)}, u32[]{:S(2)}) copy-start(f32[1,256]{1,0:T(1,128)S(1)} %get-tuple-element.173) | copy-start | bytes 3076
  26.1 5.8 %copy-start.40 = (f32[1,256]{1,0:T(1,128)}, f32[1,256]{1,0:T(1,128)S(1)}, u32[]{:S(2)}) copy-start(f32[1,256]{1,0:T(1,128)S(1)} %get-tuple-element.174) | copy-start | bytes 3076
  26.1 5.8 %copy-start.42 = (f32[1,256]{1,0:T(1,128)}, f32[1,256]{1,0:T(1,128)S(1)}, u32[]{:S(2)}) copy-start(f32[1,256]{1,0:T(1,128)S(1)} %get-tuple-element.175) | copy-start | bytes 3076
  26.2 5.8 %copy-start.44 = (f32[1,256]{1,0:T(1,128)}, f32[1,256]{1,0:T(1,128)S(1)}, u32[]{:S(2)}) copy-start(f32[1,256]{1,0:T(1,128)S(1)} %get-tuple-element.176) | copy-start | bytes 3076
  26.2 5.8 %copy-start.46 = (f32[1,256]{1,0:T(1,128)}, f32[1,256]{1,0:T(1,128)S(1)}, u32[]{:S(2)}) copy-start(f32[1,256]{1,0:T(1,128)S(1)} %get-tuple-element.177) | copy-start | bytes 3076
  26.2 5.8 %copy-start.48 = (f32[1,256]{1,0:T(1,128)}, f32[1,256]{1,0:T(1,128)S(1)}, u32[]{:S(2)}) copy-start(f32[1,256]{1,0:T(1,128)S(1)} %get-tuple-element.178) | copy-start | bytes 3076
  26.2 5.8 %copy-start.50 = (f32[1,256]{1,0:T(1,128)}, f32[1,256]{1,0:T(1,128)S(1)}, u32[]{:S(2)}) copy-start(f32[1,256]{1,0:T(1,128)S(1)} %get-tuple-element.179) | copy-start | bytes 3076
  26.2 5.8 %copy-start.52 = (f32[1,256]{1,0:T(1,128)}, f32[1,256]{1,0:T(1,128)S(1)}, u32[]{:S(2)}) copy-start(f32[1,256]{1,0:T(1,128)S(1)} %get-tuple-element.180) | copy-start | bytes 3076
  26.2 5.8 %copy-start.54 = (f32[1,256]{1,0:T(1,128)}, f32[1,256]{1,0:T(1,128)S(1)}, u32[]{:S(2)}) copy-start(f32[1,256]{1,0:T(1,128)S(1)} %get-tuple-element.181) | copy-start | bytes 3076
  26.2 5.8 %copy-start.56 = (f32[1,256]{1,0:T(1,128)}, f32[1,256]{1,0:T(1,128)S(1)}, u32[]{:S(2)}) copy-start(f32[1,256]{1,0:T(1,128)S(1)} %get-tuple-element.182) | copy-start | bytes 3076
  26.2 5.8 %copy-start.58 = (f32[1,256]{1,0:T(1,128)}, f32[1,256]{1,0:T(1,128)S(1)}, u32[]{:S(2)}) copy-start(f32[1,256]{1,0:T(1,128)S(1)} %get-tuple-element.183) | copy-start | bytes 3076
  26.2 5.8 %copy-start.60 = (f32[1,256]{1,0:T(1,128)}, f32[1,256]{1,0:T(1,128)S(1)}, u32[]{:S(2)}) copy-start(f32[1,256]{1,0:T(1,128)S(1)} %get-tuple-element.184) | copy-start | bytes 3076
  31.8 5.2 %copy-start.1 = (bf16[256,4,5,128]{0,3,2,1:T(8,128)(2,1)}, bf16[256,4,5,128]{0,3,2,1:T(8,128)(2,1)S(1)}, u32[]{:S(2)}) copy-start(bf16[256,4,5,128]{0,3,2,1:T(8,128)(2,1)S(1)} %get-tuple-element.106) | copy-start | bytes 3932164
  31.8 5.2 %copy-start.9 = (bf16[256,4,5,128]{0,3,2,1:T(8,128)(2,1)}, bf16[256,4,5,128]{0,3,2,1:T(8,128)(2,1)S(1)}, u32[]{:S(2)}) copy-start(bf16[256,4,5,128]{0,3,2,1:T(8,128)(2,1)S(1)} %get-tuple-element.107) | copy-start | bytes 3932164
  38.4 10.6 %collective-permute-start.10 = (bf16[256,2,4,128]{0,3,2,1:T(8,128)(2,1)S(1)}, bf16[256,2,4,128]{0,3,2,1:T(8,128)(2,1)}, u32[]{:S(2)}, u32[]{:S(2)}) collective-permute-start(bf16[256,2,4,128]{0,3,2,1:T(8,128)(2,1)S(1)} %get-tuple-element.194), channel_id=1, source_target_pairs={{0,128},{128,0},{1,129},{129,1},{2,130},{130,2},{3,131},{131,3},{4... | collective-permute-start | bytes 1572872 | tf_op jit(solution)/shard_map/ppermute | solution.py:30
  50.1 12.7 %copy-start.5 = (bf16[256,1,4,128]{0,3,2,1:T(8,128)(2,1)}, bf16[256,1,4,128]{0,3,2,1:T(8,128)(2,1)S(1)}, u32[]{:S(2)}) copy-start(bf16[256,1,4,128]{0,3,2,1:T(8,128)(2,1)S(1)} %get-tuple-element.110) | copy-start | bytes 786436
  50.1 12.7 %copy-start.7 = (bf16[256,1,4,128]{0,3,2,1:T(8,128)(2,1)}, bf16[256,1,4,128]{0,3,2,1:T(8,128)(2,1)S(1)}, u32[]{:S(2)}) copy-start(bf16[256,1,4,128]{0,3,2,1:T(8,128)(2,1)S(1)} %get-tuple-element.111) | copy-start | bytes 786436
  51.1 9.1 %collective-permute-start.11 = (bf16[256,4,1,128]{0,3,2,1:T(8,128)(2,1)}, bf16[256,4,1,128]{0,3,2,1:T(8,128)(2,1)}, u32[]{:S(2)}, u32[]{:S(2)}) collective-permute-start(bf16[256,4,1,128]{0,3,2,1:T(8,128)(2,1)} %get-tuple-element.96), channel_id=1, source_target_pairs={{0,1},{1,2},{2,3},{3,4},{4,5},{5,6},{6,7},{7,8},{8,9},{9,10},{10,1... | collective-permute-start | bytes 786440 | tf_op jit(solution)/shard_map/ppermute | solution.py:34
  54.5 6.6 %collective-permute-start.12 = (bf16[256,4,1,128]{0,3,2,1:T(8,128)(2,1)}, bf16[256,4,1,128]{0,3,2,1:T(8,128)(2,1)}, u32[]{:S(2)}, u32[]{:S(2)}) collective-permute-start(bf16[256,4,1,128]{0,3,2,1:T(8,128)(2,1)} %get-tuple-element.97), channel_id=1, source_target_pairs={{1,0},{2,1},{3,2},{4,3},{5,4},{6,5},{7,6},{8,7},{9,8},{10,9},{11,1... | collective-permute-start | bytes 786440 | tf_op jit(solution)/shard_map/ppermute | solution.py:35
  60.0 10.8 %copy-start.80 = (f32[1,256]{1,0:T(1,128)}, f32[1,256]{1,0:T(1,128)S(1)}, u32[]{:S(2)}) copy-start(f32[1,256]{1,0:T(1,128)S(1)} %get-tuple-element.140) | copy-start | bytes 3076
  60.0 10.8 %copy-start.82 = (f32[1,256]{1,0:T(1,128)}, f32[1,256]{1,0:T(1,128)S(1)}, u32[]{:S(2)}) copy-start(f32[1,256]{1,0:T(1,128)S(1)} %get-tuple-element.141) | copy-start | bytes 3076
  60.1 10.8 %copy-start.84 = (f32[1,256]{1,0:T(1,128)}, f32[1,256]{1,0:T(1,128)S(1)}, u32[]{:S(2)}) copy-start(f32[1,256]{1,0:T(1,128)S(1)} %get-tuple-element.142) | copy-start | bytes 3076
  60.1 10.8 %copy-start.86 = (f32[1,256]{1,0:T(1,128)}, f32[1,256]{1,0:T(1,128)S(1)}, u32[]{:S(2)}) copy-start(f32[1,256]{1,0:T(1,128)S(1)} %get-tuple-element.143) | copy-start | bytes 3076
  60.1 10.8 %copy-start.88 = (f32[1,256]{1,0:T(1,128)}, f32[1,256]{1,0:T(1,128)S(1)}, u32[]{:S(2)}) copy-start(f32[1,256]{1,0:T(1,128)S(1)} %get-tuple-element.144) | copy-start | bytes 3076
  60.1 10.8 %copy-start.90 = (f32[1,256]{1,0:T(1,128)}, f32[1,256]{1,0:T(1,128)S(1)}, u32[]{:S(2)}) copy-start(f32[1,256]{1,0:T(1,128)S(1)} %get-tuple-element.145) | copy-start | bytes 3076
  60.1 10.8 %copy-start.92 = (f32[1,256]{1,0:T(1,128)}, f32[1,256]{1,0:T(1,128)S(1)}, u32[]{:S(2)}) copy-start(f32[1,256]{1,0:T(1,128)S(1)} %get-tuple-element.146) | copy-start | bytes 3076
  60.1 10.8 %copy-start.94 = (f32[1,256]{1,0:T(1,128)}, f32[1,256]{1,0:T(1,128)S(1)}, u32[]{:S(2)}) copy-start(f32[1,256]{1,0:T(1,128)S(1)} %get-tuple-element.147) | copy-start | bytes 3076
  60.1 10.8 %copy-start.96 = (f32[1,256]{1,0:T(1,128)}, f32[1,256]{1,0:T(1,128)S(1)}, u32[]{:S(2)}) copy-start(f32[1,256]{1,0:T(1,128)S(1)} %get-tuple-element.148) | copy-start | bytes 3076
  60.1 10.8 %copy-start.98 = (f32[1,256]{1,0:T(1,128)}, f32[1,256]{1,0:T(1,128)S(1)}, u32[]{:S(2)}) copy-start(f32[1,256]{1,0:T(1,128)S(1)} %get-tuple-element.149) | copy-start | bytes 3076
  60.2 10.8 %copy-start.100 = (f32[1,256]{1,0:T(1,128)}, f32[1,256]{1,0:T(1,128)S(1)}, u32[]{:S(2)}) copy-start(f32[1,256]{1,0:T(1,128)S(1)} %get-tuple-element.150) | copy-start | bytes 3076
  60.2 10.8 %copy-start.102 = (f32[1,256]{1,0:T(1,128)}, f32[1,256]{1,0:T(1,128)S(1)}, u32[]{:S(2)}) copy-start(f32[1,256]{1,0:T(1,128)S(1)} %get-tuple-element.151) | copy-start | bytes 3076
  60.2 10.8 %copy-start.104 = (f32[1,256]{1,0:T(1,128)}, f32[1,256]{1,0:T(1,128)S(1)}, u32[]{:S(2)}) copy-start(f32[1,256]{1,0:T(1,128)S(1)} %get-tuple-element.152) | copy-start | bytes 3076
  60.2 10.8 %copy-start.106 = (f32[1,256]{1,0:T(1,128)}, f32[1,256]{1,0:T(1,128)S(1)}, u32[]{:S(2)}) copy-start(f32[1,256]{1,0:T(1,128)S(1)} %get-tuple-element.153) | copy-start | bytes 3076
  60.2 10.8 %copy-start.108 = (f32[1,256]{1,0:T(1,128)}, f32[1,256]{1,0:T(1,128)S(1)}, u32[]{:S(2)}) copy-start(f32[1,256]{1,0:T(1,128)S(1)} %get-tuple-element.154) | copy-start | bytes 3076
  60.2 10.8 %copy-start.110 = (f32[1,256]{1,0:T(1,128)}, f32[1,256]{1,0:T(1,128)S(1)}, u32[]{:S(2)}) copy-start(f32[1,256]{1,0:T(1,128)S(1)} %get-tuple-element.155) | copy-start | bytes 3076
  60.2 10.8 %copy-start.112 = (f32[1,256]{1,0:T(1,128)}, f32[1,256]{1,0:T(1,128)S(1)}, u32[]{:S(2)}) copy-start(f32[1,256]{1,0:T(1,128)S(1)} %get-tuple-element.156) | copy-start | bytes 3076
  60.2 10.8 %copy-start.114 = (f32[1,256]{1,0:T(1,128)}, f32[1,256]{1,0:T(1,128)S(1)}, u32[]{:S(2)}) copy-start(f32[1,256]{1,0:T(1,128)S(1)} %get-tuple-element.157) | copy-start | bytes 3076
  64.2 5.4 %copy-start.6 = (bf16[256,1,4,128]{0,3,2,1:T(8,128)(2,1)S(1)}, bf16[256,1,4,128]{0,3,2,1:T(8,128)(2,1)}, u32[]{:S(2)}) copy-start(bf16[256,1,4,128]{0,3,2,1:T(8,128)(2,1)} %copy-done.5) | copy-start | bytes 786436
  64.2 5.4 %copy-start.8 = (bf16[256,1,4,128]{0,3,2,1:T(8,128)(2,1)S(1)}, bf16[256,1,4,128]{0,3,2,1:T(8,128)(2,1)}, u32[]{:S(2)}) copy-start(bf16[256,1,4,128]{0,3,2,1:T(8,128)(2,1)} %copy-done.7) | copy-start | bytes 786436
  66.8 4.3 %copy-start.70 = (f32[1,256]{1,0:T(1,128)S(1)}, f32[1,256]{1,0:T(1,128)}, u32[]{:S(2)}) copy-start(f32[1,256]{1,0:T(1,128)} %get-tuple-element.162) | copy-start | bytes 3076
  66.8 4.3 %copy-start.72 = (f32[1,256]{1,0:T(1,128)S(1)}, f32[1,256]{1,0:T(1,128)}, u32[]{:S(2)}) copy-start(f32[1,256]{1,0:T(1,128)} %get-tuple-element.163) | copy-start | bytes 3076
  66.8 4.3 %copy-start.74 = (f32[1,256]{1,0:T(1,128)S(1)}, f32[1,256]{1,0:T(1,128)}, u32[]{:S(2)}) copy-start(f32[1,256]{1,0:T(1,128)} %get-tuple-element.164) | copy-start | bytes 3076
  66.8 4.3 %copy-start.76 = (f32[1,256]{1,0:T(1,128)S(1)}, f32[1,256]{1,0:T(1,128)}, u32[]{:S(2)}) copy-start(f32[1,256]{1,0:T(1,128)} %get-tuple-element.165) | copy-start | bytes 3076
  66.8 16.4 %collective-permute-start.1 = (bf16[256,2,4,128]{0,3,2,1:T(8,128)(2,1)S(1)}, bf16[256,2,4,128]{0,3,2,1:T(8,128)(2,1)}, u32[]{:S(2)}, u32[]{:S(2)}) collective-permute-start(bf16[256,2,4,128]{0,3,2,1:T(8,128)(2,1)S(1)} %get-tuple-element.196), channel_id=1, source_target_pairs={{0,128},{128,0},{1,129},{129,1},{2,130},{130,2},{3,131},{131,3},{4... | collective-permute-start | bytes 1572872 | tf_op jit(solution)/shard_map/ppermute | solution.py:30
  84.4 10.7 %collective-permute-start.2 = (bf16[256,4,1,128]{0,3,2,1:T(8,128)(2,1)S(1)}, bf16[256,4,1,128]{0,3,2,1:T(8,128)(2,1)S(1)}, u32[]{:S(2)}, u32[]{:S(2)}) collective-permute-start(bf16[256,4,1,128]{0,3,2,1:T(8,128)(2,1)S(1)} %get-tuple-element.104), channel_id=1, source_target_pairs={{0,1},{1,2},{2,3},{3,4},{4,5},{5,6},{6,7},{7,8},{8,9},{9,10},{10,1... | collective-permute-start | bytes 786440 | tf_op jit(solution)/shard_map/ppermute | solution.py:34
  84.5 11.1 %collective-permute-start.3 = (bf16[256,4,1,128]{0,3,2,1:T(8,128)(2,1)S(1)}, bf16[256,4,1,128]{0,3,2,1:T(8,128)(2,1)S(1)}, u32[]{:S(2)}, u32[]{:S(2)}) collective-permute-start(bf16[256,4,1,128]{0,3,2,1:T(8,128)(2,1)S(1)} %get-tuple-element.105), channel_id=1, source_target_pairs={{1,0},{2,1},{3,2},{4,3},{5,4},{6,5},{7,6},{8,7},{9,8},{10,9},{11,1... | collective-permute-start | bytes 786440 | tf_op jit(solution)/shard_map/ppermute | solution.py:35
  98.1 4.8 %copy-start.19 = (bf16[128,256]{1,0:T(8,128)(2,1)S(1)}, bf16[128,256]{1,0:T(8,128)(2,1)}, u32[]{:S(2)}) copy-start(bf16[128,256]{1,0:T(8,128)(2,1)} %slice.924) | copy-start | bytes 196612
  98.1 4.8 %copy-start.21 = (bf16[128,256]{1,0:T(8,128)(2,1)S(1)}, bf16[128,256]{1,0:T(8,128)(2,1)}, u32[]{:S(2)}) copy-start(bf16[128,256]{1,0:T(8,128)(2,1)} %slice.926) | copy-start | bytes 196612
  102.9 4.7 %copy-start.4 = (bf16[256,1,4,128]{0,3,2,1:T(8,128)(2,1)S(1)}, bf16[256,1,4,128]{0,3,2,1:T(8,128)(2,1)}, u32[]{:S(2)}) copy-start(bf16[256,1,4,128]{0,3,2,1:T(8,128)(2,1)} %copy-done.3) | copy-start | bytes 786436
  111.1 47.9 %collective-permute-start.7 = (bf16[256,2,4,128]{0,3,2,1:T(8,128)(2,1)S(1)}, bf16[256,2,4,128]{0,3,2,1:T(8,128)(2,1)S(1)}, u32[]{:S(2)}, u32[]{:S(2)}) collective-permute-start(bf16[256,2,4,128]{0,3,2,1:T(8,128)(2,1)S(1)} %get-tuple-element.197), channel_id=1, source_target_pairs={{0,128},{128,0},{1,129},{129,1},{2,130},{130,2},{3,131},{131,3},{4... | collective-permute-start | bytes 1572872 | tf_op jit(solution)/shard_map/ppermute | solution.py:30
  159.1 7.0 %collective-permute-start.8 = (bf16[256,4,1,128]{0,3,2,1:T(8,128)(2,1)S(1)}, bf16[256,4,1,128]{0,3,2,1:T(8,128)(2,1)S(1)}, u32[]{:S(2)}, u32[]{:S(2)}) collective-permute-start(bf16[256,4,1,128]{0,3,2,1:T(8,128)(2,1)S(1)} %get-tuple-element.100), channel_id=1, source_target_pairs={{0,1},{1,2},{2,3},{3,4},{4,5},{5,6},{6,7},{7,8},{8,9},{9,10},{10,1... | collective-permute-start | bytes 786440 | tf_op jit(solution)/shard_map/ppermute | solution.py:34
  159.9 6.1 %collective-permute-start.9 = (bf16[256,4,1,128]{0,3,2,1:T(8,128)(2,1)S(1)}, bf16[256,4,1,128]{0,3,2,1:T(8,128)(2,1)S(1)}, u32[]{:S(2)}, u32[]{:S(2)}) collective-permute-start(bf16[256,4,1,128]{0,3,2,1:T(8,128)(2,1)S(1)} %get-tuple-element.101), channel_id=1, source_target_pairs={{1,0},{2,1},{3,2},{4,3},{5,4},{6,5},{7,6},{8,7},{9,8},{10,9},{11,1... | collective-permute-start | bytes 786440 | tf_op jit(solution)/shard_map/ppermute | solution.py:35
  (65 other events, 105.1 us)
where the time goes:
time: 178 us; the launch traced here: 174 us
  Pallas kernels  44.6 us (25%)
  other arithmetic  31.3 us (18%)
  starting transfers between devices  27.6 us (16%)
  local copies, waits for them, and re-layouts  27.2 us (15%)
  waiting for transfers between devices  26.9 us (15%)
  matrix products  13.6 us (8%)
  between operations  2.66 us (1%)
    pallas_call x1, Pallas kernels, tree_reduce(): pl.pallas_call(functools.partial(reduce_kernel, plan), out_shape=jax.Shap...  44.6 us
    ppermute x4, waiting for transfers between devices, extended(): theirs = lax.ppermute(jnp.concatenate([first, last], axis=dim), axis, up)  15.6 us
    ppermute x4, starting transfers between devices, extended(): after = lax.ppermute(first, axis, down)  11.8 us
    unnamed x243, local copies, waits for them, and re-layouts  10.1 us
    dot_general x2, matrix products, backmap(): jnp.dot(weights, flattened, preferred_element_type=jnp.float32)  6.82 us
    ppermute x4, waiting for transfers between devices, extended(): before = lax.ppermute(last, axis, up)  6.45 us
    ppermute x4, starting transfers between devices, extended(): before = lax.ppermute(last, axis, up)  6.34 us
    concatenate x8, other arithmetic, ring_z(): return jnp.concatenate([padded[..., -1:], padded, padded[..., :1]], axis=3)  6.1 us
  transfers between devices with their start and end apart: 13, of which 9 were waited for; matrix products, arithmetic and copies ran while one was open for 17% of the time, Pallas kernels for 26%

commit v1 on v0

--- a/solution.py
+++ b/solution.py
@@ -35,6 +35,28 @@
             after = lax.ppermute(first, axis, down)
         value = jnp.concatenate([before, value, after], axis=dim)
     return value
+
+
+def extended_at_once(value):
+    count = lax.axis_size("space")
+    up = [(i, (i + 1) % count) for i in range(count)]
+    down = [(j, i) for i, j in up]
+    cross_up = [(o * count + i, (1 - o) * count + j) for o in range(2) for i, j in up]
+    cross_down = [(o * count + i, (1 - o) * count + j) for o in range(2) for i, j in down]
+    first = value[:, :, :1]
+    last = value[:, :, -1:]
+    partner = lax.ppermute(value, "own", [(0, 1), (1, 0)])
+    below = lax.ppermute(last, "space", up)
+    above = lax.ppermute(first, "space", down)
+    corner_below = lax.ppermute(last, ("own", "space"), cross_up)
+    corner_above = lax.ppermute(first, ("own", "space"), cross_down)
+
+    def row(theirs, mine):
+        return jnp.concatenate([theirs[:, -1:], mine, theirs[:, :1]], axis=1)
+
+    return jnp.concatenate(
+        [row(corner_below, below), row(partner, value), row(corner_above, above)], axis=2
+    )
 
 
 def gather_weights(pw_one, pw_two, dw_one, dw_two):
@@ -337,7 +359,7 @@
         * (sigma * (1.0 + pre * (1.0 - sigma)))
     ).astype(jnp.bfloat16)
     grad_first = backmap(weight_one, grad_pre).astype(jnp.bfloat16)
-    first_padded = extended(grad_first, (("own", 1), ("space", 2)), 1)
+    first_padded = extended_at_once(grad_first)
     grad_input = (
         cotangent.astype(jnp.float32) + depthwise(first_padded, taps_one, extent_x, extent_y, -1)
     ).astype(jnp.bfloat16)

time: 178 us -> 188 us (1.056); the launches traced: 174 us -> 187 us
  starting transfers between devices: 27.6 us -> 43.7 us
  Pallas kernels: 44.6 us -> 35.8 us
  other arithmetic: 31.3 us -> 36.4 us
  local copies, waits for them, and re-layouts: 27.2 us -> 31.7 us
  waiting for transfers between devices: 26.9 us -> 22.7 us
    ppermute x0 -> x5, starting transfers between devices: none -> 17.6 us  [the longest x1 8.28 us: extended_at_once(): above = lax.ppermute(first, 'space', down)]
    pallas_call x1, Pallas kernels: 44.6 us -> 35.8 us  [tree_reduce(): pl.pallas_call(functools.partial(reduce_kernel, plan), out_shape=jax.Shap...]
    concatenate x8, other arithmetic: 6.1 us -> 10.5 us  [ring_z(): return jnp.concatenate([padded[..., -1:], padded, padded[..., :1]], axis=3)]
    ppermute x4 -> x3, waiting for transfers between devices: 6.45 us -> 2.31 us  [extended(): before = lax.ppermute(last, axis, up)]
    another operation x2, local copies, waits for them, and re-layouts: 2.97 us -> 5.79 us  [tap_sums(): return jnp.stack(columns, axis=0)]
    ppermute x4 -> x3, starting transfers between devices: 6.34 us -> 5.49 us  [extended(): before = lax.ppermute(last, axis, up)]
    ppermute x4 -> x3, starting transfers between devices: 5.62 us -> 4.95 us  [extended(): theirs = lax.ppermute(jnp.concatenate([first, last], axis=dim), axis, up)]
    unnamed x243 -> x257, local copies, waits for them, and re-layouts: 10.1 us -> 9.94 us
  transfers between devices with their start and end apart: 13 -> 15, of which waited for: 9 -> 8; matrix products, arithmetic and copies ran while one was open for 17% -> 19% of each run, Pallas kernels for 26% -> 19%
where the time goes in v1:
time: 188 us; the launch traced here: 187 us
  starting transfers between devices  43.7 us (23%)
  other arithmetic  36.4 us (19%)
  Pallas kernels  35.8 us (19%)
  local copies, waits for them, and re-layouts  31.7 us (17%)
  waiting for transfers between devices  22.7 us (12%)
  matrix products  14.2 us (8%)
  between operations  2.78 us (1%)
    pallas_call x1, Pallas kernels, tree_reduce(): pl.pallas_call(functools.partial(reduce_kernel, plan), out_shape=jax.Shap...  35.8 us
    ppermute x3, waiting for transfers between devices, extended(): theirs = lax.ppermute(jnp.concatenate([first, last], axis=dim), axis, up)  15.6 us
    ppermute x3, starting transfers between devices, extended(): after = lax.ppermute(first, axis, down)  11.8 us
    concatenate x8, other arithmetic, ring_z(): return jnp.concatenate([padded[..., -1:], padded, padded[..., :1]], axis=3)  10.5 us
    unnamed x257, local copies, waits for them, and re-layouts  9.94 us
    ppermute x1, starting transfers between devices, extended_at_once(): above = lax.ppermute(first, 'space', down)  8.28 us
    ppermute x1, starting transfers between devices, extended_at_once(): corner_above = lax.ppermute(first, ('own', 'space'), cross_down)  8.15 us
    dot_general x2, matrix products, backmap(): jnp.dot(weights, flattened, preferred_element_type=jnp.float32)  7.38 us
  transfers between devices with their start and end apart: 15, of which 8 were waited for; matrix products, arithmetic and copies ran while one was open for 19% of the time, Pallas kernels for 19%

profile of v1, /device:TPU:1, one launch (start us, length us, event | category | flops | bytes accessed | tf_op | source)
XLA Modules:
  0.0 187.3 jit_solution(9208465354299573508)
XLA Ops:
  0.6 0.9 copy.30
  1.5 0.9 copy.31
  2.4 0.7 pad_maximum_fusion.60
  3.2 3.8 %collective-permute-start = (bf16[72448]{0:T(1024)(128)(2,1)S(1)}, bf16[72448]{0:T(1024)(128)(2,1)S(1)}, u32[]{:S(2)}, u32[]{:S(2)}) collective-permute-start(bf16[72448]{0:T(1024)(128)(2,1)S(1)} %pad_maximum_fusion.60), channel_id=1, source_target_pairs={{0,128},{128,0},{1,129},{129,1},{2,130},{130,2},{3,131},{131,3},{4... | collective-permute-start | bytes 434696 | tf_op jit(solution)/shard_map/ppermute | solution.py:64
  7.0 1.3 copy.13
  8.4 1.1 collective-permute-done
  9.5 0.8 broadcast_select_fusion.1
  10.3 0.7 fusion.301
  11.0 11.6 %collective-permute-done.4 = bf16[256,2,4,128]{0,3,2,1:T(8,128)(2,1)S(1)} collective-permute-done((bf16[256,2,4,128]{0,3,2,1:T(8,128)(2,1)S(1)}, bf16[256,2,4,128]{0,3,2,1:T(8,128)(2,1)S(1)}, u32[]{:S(2)}, u32[]{:S(2)}) %collective-permute-start.4) | collective-permute-done | bytes 524320 | tf_op jit(solution)/shard_map/ppermute | solution.py:30
  22.7 2.0 %collective-permute-start.5 = (bf16[256,4,1,128]{0,3,2,1:T(8,128)(2,1)S(1)}, bf16[256,4,1,128]{0,3,2,1:T(8,128)(2,1)S(1)}, u32[]{:S(2)}, u32[]{:S(2)}) collective-permute-start(bf16[256,4,1,128]{0,3,2,1:T(8,128)(2,1)S(1)} %get-tuple-element.106), channel_id=1, source_target_pairs={{0,1},{1,2},{2,3},{3,4},{4,5},{5,6},{6,7},{7,8},{8,9},{9,10},{10,1... | collective-permute-start | bytes 786440 | tf_op jit(solution)/shard_map/ppermute | solution.py:34
  24.8 0.6 slice.933
  25.4 0.6 slice.935
  26.3 1.7 collective-permute-done.5
  28.0 2.5 %collective-permute-done.6 = bf16[256,4,1,128]{0,3,2,1:T(8,128)(2,1)S(1)} collective-permute-done((bf16[256,4,1,128]{0,3,2,1:T(8,128)(2,1)S(1)}, bf16[256,4,1,128]{0,3,2,1:T(8,128)(2,1)S(1)}, u32[]{:S(2)}, u32[]{:S(2)}) %collective-permute-start.6) | collective-permute-done | bytes 262176 | tf_op jit(solution)/shard_map/ppermute | solution.py:35
  30.8 0.7 fusion.9
  32.1 0.7 copy-done
  32.8 4.2 %fusion.40 = bf16[256,2,4,128]{0,3,2,1:T(8,128)(2,1)S(1)} fusion(bf16[256,2,4,128]{0,3,2,1:T(8,128)(2,1)S(1)} %copy.13, f32[256]{0:T(256)S(1)} %bitcast.227, f32[256]{0:T(256)S(1)} %bitcast.229, f32[256]{0:T(256)S(1)} %bitcast.225, f32[256]{0:T(256)S(1)} %bitcast.223, f32[256]{0:T(256)S(1)} %bitcast.221, f32[256]{0:T(256)S(1)} %bitcast.219, ...), kind=kLoop, calls=%fused_computation.198 | loop fusion | flops 21757952 | bytes 14183424 | tf_op jit(solution)/shard_map/convert_element_type | solution.py:349
  37.1 1.4 multiply_convert_fusion
  38.4 2.3 %collective-permute-start.12 = (bf16[256,2,4,128]{0,3,2,1:T(8,128)(2,1)S(1)}, bf16[256,2,4,128]{0,3,2,1:T(8,128)(2,1)}, u32[]{:S(2)}, u32[]{:S(2)}) collective-permute-start(bf16[256,2,4,128]{0,3,2,1:T(8,128)(2,1)S(1)} %get-tuple-element.198), channel_id=1, source_target_pairs={{0,128},{128,0},{1,129},{129,1},{2,130},{130,2},{3,131},{131,3},{4... | collective-permute-start | bytes 1572872 | tf_op jit(solution)/shard_map/ppermute | solution.py:30
  40.8 1.2 copy.11
  41.9 1.2 reshape.539
  43.1 2.1 %copy.12 = bf16[1024,256]{1,0:T(8,128)(2,1)} copy(bf16[1024,256]{0,1:T(8,128)(2,1)} %bitcast.196) | data formatting | bytes 1048576 | tf_op jit(solution)/shard_map/dot_general | solution.py:114
  45.1 3.9 %collective-permute-done.12 = bf16[256,2,4,128]{0,3,2,1:T(8,128)(2,1)} collective-permute-done((bf16[256,2,4,128]{0,3,2,1:T(8,128)(2,1)S(1)}, bf16[256,2,4,128]{0,3,2,1:T(8,128)(2,1)}, u32[]{:S(2)}, u32[]{:S(2)}) %collective-permute-start.12) | collective-permute-done | bytes 524320 | tf_op jit(solution)/shard_map/ppermute | solution.py:30
  49.1 1.1 fusion.294
  50.2 1.0 pad_maximum_fusion.53
  51.1 3.4 %collective-permute-start.13 = (bf16[256,4,1,128]{0,3,2,1:T(8,128)(2,1)}, bf16[256,4,1,128]{0,3,2,1:T(8,128)(2,1)}, u32[]{:S(2)}, u32[]{:S(2)}) collective-permute-start(bf16[256,4,1,128]{0,3,2,1:T(8,128)(2,1)} %get-tuple-element.96), channel_id=1, source_target_pairs={{0,1},{1,2},{2,3},{3,4},{4,5},{5,6},{6,7},{7,8},{8,9},{9,10},{10,1... | collective-permute-start | bytes 786440 | tf_op jit(solution)/shard_map/ppermute | solution.py:34
  54.5 1.9 %collective-permute-start.14 = (bf16[256,4,1,128]{0,3,2,1:T(8,128)(2,1)}, bf16[256,4,1,128]{0,3,2,1:T(8,128)(2,1)}, u32[]{:S(2)}, u32[]{:S(2)}) collective-permute-start(bf16[256,4,1,128]{0,3,2,1:T(8,128)(2,1)} %get-tuple-element.97), channel_id=1, source_target_pairs={{1,0},{2,1},{3,2},{4,3},{5,4},{6,5},{7,6},{8,7},{9,8},{10,9},{11,1... | collective-permute-start | bytes 786440 | tf_op jit(solution)/shard_map/ppermute | solution.py:35
  56.4 0.6 fusion.270
  57.1 1.5 slice.942
  58.6 1.5 slice.944
  60.3 0.8 collective-permute-done.14
  61.1 1.7 fusion.1
  62.8 1.3 maximum_maximum_fusion.4
  64.2 2.5 %fusion.108 = (f32[256]{0:T(256)}, f32[256]{0:T(256)}, f32[256]{0:T(256)}, f32[256]{0:T(256)}, f32[256]{0:T(256)}, /*index=5*/f32[256]{0:T(256)}, f32[256]{0:T(2...) fusion(bf16[256,4,5,128]{0,3,2,1:T(8,128)(2,1)S(1)} %get-tuple-, ...), kind=kOutput, calls=%fused_computation.266 | convolution fusion | flops 144438272 | bytes 7483392 | tf_op jit(solution)/shard_map/dot_general | solution.py:114
  66.8 2.5 %collective-permute-start.1 = (bf16[256,2,4,128]{0,3,2,1:T(8,128)(2,1)S(1)}, bf16[256,2,4,128]{0,3,2,1:T(8,128)(2,1)}, u32[]{:S(2)}, u32[]{:S(2)}) collective-permute-start(bf16[256,2,4,128]{0,3,2,1:T(8,128)(2,1)S(1)} %get-tuple-element.200), channel_id=1, source_target_pairs={{0,128},{128,0},{1,129},{129,1},{2,130},{130,2},{3,131},{131,3},{4... | collective-permute-start | bytes 1572872 | tf_op jit(solution)/shard_map/ppermute | solution.py:30
  69.3 1.3 fusion
  70.9 5.1 %fusion.12 = f32[256,256]{1,0:T(8,128)} fusion(bf16[256,2,4,128]{0,3,2,1:T(8,128)(2,1)S(1)} %copy-done.10, bf16[256,2,4,128]{0,3,2,1:T(8,128)(2,1)S(1)} %get-tuple-element.198, f32[256]{0:T(256)S(1)} %bitcast.311, f32[256]{0:T(256)S(1)} %bitcast.313, f32[256]{0:T(256)S(1)} %bitcast.309, f32[256]{0:T(256)S(1)} %bitcast.307, f32[256]{0:T(256)S(1)} %bitcast.305, ...), kind=kOutput, calls=%fused_computation.169 | convolution fusion | flops 156041216 | bytes 14445568 | tf_op jit(solution)/shard_map/dot_general | solution.py:119
  76.0 3.2 %fusion.109 = (f32[256]{0:T(256)S(1)}, f32[256]{0:T(256)S(1)}, f32[256]{0:T(256)S(1)}, f32[256]{0:T(256)S(1)}, f32[256]{0:T(256)S(1)}, /*index=5*/f32[256]{0:T(2...) fusion(bf16[256,2,4,128]{0,3,2,1:T(8,128)(2,1)S(1)} %get-tuple-, ...), kind=kLoop, calls=%fused_computation.267 | loop fusion | flops 12579072 | bytes 7879680 | tf_op jit(solution)/shard_map/reduce_sum | solution.py:101
  79.2 2.9 %stack.232 = f32[27,256]{1,0:T(8,128)S(1)} concatenate(f32[1,256]{1,0:T(1,128)} %bitcast.367, f32[1,256]{1,0:T(1,128)} %bitcast.291, f32[1,256]{1,0:T(1,128)} %bitcast.290, f32[1,256]{1,0:T(1,128)} %bitcast.366, f32[1,256]{1,0:T(1,128)} %bitcast.295, f32[1,256]{1,0:T(1,128)S(1)} %bitcast.283, f32[1,256]{1,0:T(1,128)} %bitcast.373, f32[1,256]{1,0:T(1,128)} %bitcast.364, ...), dimensions={0} | concatenate | bytes 55296 | tf_op jit(solution)/shard_map/stack | solution.py:102
  82.1 1.0 slice_bitcast_fusion.2
  83.1 1.1 fusion.297
  84.3 9.9 %collective-permute-start.3 = (bf16[256,4,1,128]{0,3,2,1:T(8,128)(2,1)S(1)}, bf16[256,4,1,128]{0,3,2,1:T(8,128)(2,1)S(1)}, u32[]{:S(2)}, u32[]{:S(2)}) collective-permute-start(bf16[256,4,1,128]{0,3,2,1:T(8,128)(2,1)S(1)} %get-tuple-element.103), channel_id=1, source_target_pairs={{1,0},{2,1},{3,2},{4,3},{5,4},{6,5},{7,6},{8,7},{9,8},{10,9},{11,1... | collective-permute-start | bytes 786440 | tf_op jit(solution)/shard_map/ppermute | solution.py:35
  94.4 0.6 collective-permute-done.2
  95.4 0.7 fusion.10
  96.9 0.7 copy-done.13
  97.9 4.8 %fusion.153 = bf16[256,2,4,128]{0,3,2,1:T(8,128)(2,1)S(1)} fusion(f32[256,2,4,128]{0,3,2,1:T(8,128)S(1)} %copy-done.13, bf16[256,2,4,128]{0,3,2,1:T(8,128)(2,1)S(1)} %get-tuple-element.200, bf16[256,4,6,129]{0,3,2,1:T(8,128)(2,1)S(1)} %fusion.10, bf16[256,4,5,128]{0,3,2,1:T(8,128)(2,1)S(1)} %get-tuple-element.101, bf16[256,4,6,129]{0,3,2,1:T(8,128)(2,1)S(1)} %fusion.11, ...), kind=kLoop, calls=%fused_computation.313 | loop fusion | flops 23855104 | bytes 15232000 | tf_op jit(solution)/shard_map/convert_element_type | solution.py:360
  102.7 4.8 %fusion.150 = (f32[256]{0:T(256)}, f32[256]{0:T(256)}, f32[256]{0:T(256)}, f32[256]{0:T(256)}, f32[256]{0:T(256)}, /*index=5*/f32[256]{0:T(256)}, f32[256]{0:T(2...) fusion(bf16[256,4,5,128]{0,3,2,1:T(8,128)(2,1)} %copy-done.9, ...), kind=kOutput, calls=%fused_computation.308 | convolution fusion | flops 144438272 | bytes 7483392 | tf_op jit(solution)/shard_map/dot_general | solution.py:114
  107.9 1.0 copy-done.2
  108.9 3.2 %fusion.151 = (f32[256]{0:T(256)}, f32[256]{0:T(256)}, f32[256]{0:T(256)}, f32[256]{0:T(256)}, f32[256]{0:T(256)}, /*index=5*/f32[256]{0:T(256)}, f32[256]{0:T(2...) fusion(bf16[256,2,4,128]{0,3,2,1:T(8,128)(2,1)S(1)} %get-tuple-, ...), kind=kLoop, calls=%fused_computation.309 | loop fusion | flops 12579072 | bytes 7879680 | tf_op jit(solution)/shard_map/reduce_sum | solution.py:101
  112.6 8.3 %collective-permute-start.11 = (bf16[256,2,1,128]{0,3,2,1:T(8,128)(2,1)S(1)}, bf16[256,2,1,128]{0,3,2,1:T(8,128)(2,1)S(1)}, u32[]{:S(2)}, u32[]{:S(2)}) collective-permute-start(bf16[256,2,1,128]{0,3,2,1:T(8,128)(2,1)S(1)} %get-tuple-element.113), channel_id=1, source_target_pairs={{1,0},{2,1},{3,2},{4,3},{5,4},{6,5},{7,6},{8,7},{9,8},{10,9},{11,1... | collective-permute-start | bytes 393224 | tf_op jit(solution)/shard_map/ppermute | solution.py:50
  120.9 8.2 %collective-permute-start.10 = (bf16[256,2,1,128]{0,3,2,1:T(8,128)(2,1)S(1)}, bf16[256,2,1,128]{0,3,2,1:T(8,128)(2,1)S(1)}, u32[]{:S(2)}, u32[]{:S(2)}) collective-permute-start(bf16[256,2,1,128]{0,3,2,1:T(8,128)(2,1)S(1)} %get-tuple-element.113), channel_id=1, source_target_pairs={{1,128},{2,129},{3,130},{4,131},{5,132},{6,133},{7,134},{8,135},{9... | collective-permute-start | bytes 393224 | tf_op jit(solution)/shard_map/ppermute | solution.py:52
  129.1 0.7 collective-permute-start.9
  129.8 2.9 %stack.204 = f32[27,256]{1,0:T(8,128)S(1)} concatenate(f32[1,256]{1,0:T(1,128)} %bitcast.354, f32[1,256]{1,0:T(1,128)} %bitcast.276, f32[1,256]{1,0:T(1,128)} %bitcast.275, f32[1,256]{1,0:T(1,128)} %bitcast.355, f32[1,256]{1,0:T(1,128)} %bitcast.280, f32[1,256]{1,0:T(1,128)} %bitcast.268, f32[1,256]{1,0:T(1,128)} %bitcast.361, f32[1,256]{1,0:T(1,128)} %bitcast.352, ...), dimensions={0} | concatenate | bytes 55296 | tf_op jit(solution)/shard_map/stack | solution.py:102
  133.3 0.5 select_maximum_fusion
  133.9 1.4 reshape.550.x_ref
  135.3 35.8 %shard_map.101 = f32[80,8,128]{2,1,0:T(8,128)} custom-call(f32[160,8,128]{2,1,0:T(8,128)} %reshape.550.x_ref), custom_call_target="tpu_custom_call" | custom-call | bytes 41943040 | tf_op jit(solution)/shard_map/pallas_call | solution.py:298
  171.1 1.0 fusion.300
  172.1 1.4 fusion.299
  173.5 0.7 reshape.552
  174.2 0.7 reshape.551
  175.0 2.2 %fusion.3 = bf16[256,4,6,129]{0,3,2,1:T(8,128)(2,1)S(1)} fusion(bf16[256,1,1,128]{0,3,2,1:T(8,128)(2,1)S(1)} %get-tuple-element.139, bf16[256,2,1,128]{0,3,2,1:T(8,128)(2,1)S(1)} %collective-permute-done.11, bf16[256,1,1,128]{0,3,2,1:T(8,128)(2,1)S(1)} %get-tuple-element.138, bf16[256,1,4,128]{0,3,2,1:T(8,128)(2,1)S(1)} %get-tuple-element.111, ...), kind=kLoop, calls=%fused_computation.68 | loop fusion | flops 28532736 | bytes 3158016 | tf_op jit(solution)/shard_map/concatenate | solution.py:78
  177.2 3.2 %fusion.6 = bf16[256,4,6,129]{0,3,2,1:T(8,128)(2,1)S(1)} fusion(bf16[256,1,1,128]{0,3,2,1:T(8,128)(2,1)S(1)} %get-tuple-element.139, bf16[256,2,1,128]{0,3,2,1:T(8,128)(2,1)S(1)} %collective-permute-done.11, bf16[256,1,1,128]{0,3,2,1:T(8,128)(2,1)S(1)} %get-tuple-element.138, bf16[256,1,4,128]{0,3,2,1:T(8,128)(2,1)S(1)} %get-tuple-element.111, ...), kind=kLoop, calls=%fused_computation.77 | loop fusion | flops 28532736 | bytes 3158016 | tf_op jit(solution)/shard_map/concatenate | solution.py:78
  181.7 4.6 %fusion.152 = bf16[256,2,4,128]{0,3,2,1:T(8,128)(2,1)S(1)} fusion(bf16[256,2,4,128]{0,3,2,1:T(8,128)(2,1)S(1)} %get-tuple-element.201, bf16[256,2,4,128]{0,3,2,1:T(8,128)(2,1)S(1)} %copy-done.11, bf16[256,4,6,129]{0,3,2,1:T(8,128)(2,1)S(1)} %fusion.3, bf16[256,4,5,128]{0,3,2,1:T(8,128)(2,1)S(1)} %get-tuple-element.99, ...), kind=kLoop, calls=%fused_computation.312 | loop fusion | flops 22282240 | bytes 14707712 | tf_op jit(solution)/shard_map/convert_element_type | solution.py:365
  186.3 1.1 copy.22
  (288 shorter events, 5.0 us)
Async XLA Ops:
  3.2 6.3 %collective-permute-start = (bf16[72448]{0:T(1024)(128)(2,1)S(1)}, bf16[72448]{0:T(1024)(128)(2,1)S(1)}, u32[]{:S(2)}, u32[]{:S(2)}) collective-permute-start(bf16[72448]{0:T(1024)(128)(2,1)S(1)} %pad_maximum_fusion.60), channel_id=1, source_target_pairs={{0,128},{128,0},{1,129},{129,1},{2,130},{130,2},{3,131},{131,3},{4... | collective-permute-start | bytes 434696 | tf_op jit(solution)/shard_map/ppermute | solution.py:64
  8.3 14.3 %collective-permute-start.4 = (bf16[256,2,4,128]{0,3,2,1:T(8,128)(2,1)S(1)}, bf16[256,2,4,128]{0,3,2,1:T(8,128)(2,1)S(1)}, u32[]{:S(2)}, u32[]{:S(2)}) collective-permute-start(bf16[256,2,4,128]{0,3,2,1:T(8,128)(2,1)S(1)} %copy.13), channel_id=1, source_target_pairs={{0,128},{128,0},{1,129},{129,1},{2,130},{130,2},{3,131},{131,3},{4... | collective-permute-start | bytes 1572872 | tf_op jit(solution)/shard_map/ppermute | solution.py:30
  22.6 9.2 %copy-start.3 = (bf16[256,1,4,128]{0,3,2,1:T(8,128)(2,1)}, bf16[256,1,4,128]{0,3,2,1:T(8,128)(2,1)S(1)}, u32[]{:S(2)}) copy-start(bf16[256,1,4,128]{0,3,2,1:T(8,128)(2,1)S(1)} %get-tuple-element.117) | copy-start | bytes 786436
  22.7 5.3 %collective-permute-start.5 = (bf16[256,4,1,128]{0,3,2,1:T(8,128)(2,1)S(1)}, bf16[256,4,1,128]{0,3,2,1:T(8,128)(2,1)S(1)}, u32[]{:S(2)}, u32[]{:S(2)}) collective-permute-start(bf16[256,4,1,128]{0,3,2,1:T(8,128)(2,1)S(1)} %get-tuple-element.106), channel_id=1, source_target_pairs={{0,1},{1,2},{2,3},{3,4},{4,5},{5,6},{6,7},{7,8},{8,9},{9,10},{10,1... | collective-permute-start | bytes 786440 | tf_op jit(solution)/shard_map/ppermute | solution.py:34
  24.7 5.8 %collective-permute-start.6 = (bf16[256,4,1,128]{0,3,2,1:T(8,128)(2,1)S(1)}, bf16[256,4,1,128]{0,3,2,1:T(8,128)(2,1)S(1)}, u32[]{:S(2)}, u32[]{:S(2)}) collective-permute-start(bf16[256,4,1,128]{0,3,2,1:T(8,128)(2,1)S(1)} %get-tuple-element.107), channel_id=1, source_target_pairs={{1,0},{2,1},{3,2},{4,3},{5,4},{6,5},{7,6},{8,7},{9,8},{10,9},{11,1... | collective-permute-start | bytes 786440 | tf_op jit(solution)/shard_map/ppermute | solution.py:35
  24.7 7.1 %copy-start.23 = (f32[1,256]{1,0:T(1,128)}, f32[1,256]{1,0:T(1,128)S(1)}, u32[]{:S(2)}) copy-start(f32[1,256]{1,0:T(1,128)S(1)} %get-tuple-element.193) | copy-start | bytes 3076
  24.7 7.1 %copy-start.25 = (f32[1,256]{1,0:T(1,128)}, f32[1,256]{1,0:T(1,128)S(1)}, u32[]{:S(2)}) copy-start(f32[1,256]{1,0:T(1,128)S(1)} %get-tuple-element.194) | copy-start | bytes 3076
  24.8 7.1 %copy-start.27 = (f32[1,256]{1,0:T(1,128)}, f32[1,256]{1,0:T(1,128)S(1)}, u32[]{:S(2)}) copy-start(f32[1,256]{1,0:T(1,128)S(1)} %get-tuple-element.195) | copy-start | bytes 3076
  24.8 7.1 %copy-start.29 = (f32[1,256]{1,0:T(1,128)}, f32[1,256]{1,0:T(1,128)S(1)}, u32[]{:S(2)}) copy-start(f32[1,256]{1,0:T(1,128)S(1)} %get-tuple-element.196) | copy-start | bytes 3076
  24.8 7.1 %copy-start.31 = (f32[1,256]{1,0:T(1,128)}, f32[1,256]{1,0:T(1,128)S(1)}, u32[]{:S(2)}) copy-start(f32[1,256]{1,0:T(1,128)S(1)} %get-tuple-element.197) | copy-start | bytes 3076
  26.1 5.8 %copy-start.33 = (f32[1,256]{1,0:T(1,128)}, f32[1,256]{1,0:T(1,128)S(1)}, u32[]{:S(2)}) copy-start(f32[1,256]{1,0:T(1,128)S(1)} %get-tuple-element.171) | copy-start | bytes 3076
  26.1 5.8 %copy-start.35 = (f32[1,256]{1,0:T(1,128)}, f32[1,256]{1,0:T(1,128)S(1)}, u32[]{:S(2)}) copy-start(f32[1,256]{1,0:T(1,128)S(1)} %get-tuple-element.172) | copy-start | bytes 3076
  26.1 5.8 %copy-start.37 = (f32[1,256]{1,0:T(1,128)}, f32[1,256]{1,0:T(1,128)S(1)}, u32[]{:S(2)}) copy-start(f32[1,256]{1,0:T(1,128)S(1)} %get-tuple-element.173) | copy-start | bytes 3076
  26.1 5.8 %copy-start.39 = (f32[1,256]{1,0:T(1,128)}, f32[1,256]{1,0:T(1,128)S(1)}, u32[]{:S(2)}) copy-start(f32[1,256]{1,0:T(1,128)S(1)} %get-tuple-element.174) | copy-start | bytes 3076
  26.1 5.8 %copy-start.41 = (f32[1,256]{1,0:T(1,128)}, f32[1,256]{1,0:T(1,128)S(1)}, u32[]{:S(2)}) copy-start(f32[1,256]{1,0:T(1,128)S(1)} %get-tuple-element.175) | copy-start | bytes 3076
  26.1 5.8 %copy-start.43 = (f32[1,256]{1,0:T(1,128)}, f32[1,256]{1,0:T(1,128)S(1)}, u32[]{:S(2)}) copy-start(f32[1,256]{1,0:T(1,128)S(1)} %get-tuple-element.176) | copy-start | bytes 3076
  26.1 5.8 %copy-start.45 = (f32[1,256]{1,0:T(1,128)}, f32[1,256]{1,0:T(1,128)S(1)}, u32[]{:S(2)}) copy-start(f32[1,256]{1,0:T(1,128)S(1)} %get-tuple-element.177) | copy-start | bytes 3076
  26.2 5.8 %copy-start.47 = (f32[1,256]{1,0:T(1,128)}, f32[1,256]{1,0:T(1,128)S(1)}, u32[]{:S(2)}) copy-start(f32[1,256]{1,0:T(1,128)S(1)} %get-tuple-element.178) | copy-start | bytes 3076
  26.2 5.8 %copy-start.49 = (f32[1,256]{1,0:T(1,128)}, f32[1,256]{1,0:T(1,128)S(1)}, u32[]{:S(2)}) copy-start(f32[1,256]{1,0:T(1,128)S(1)} %get-tuple-element.179) | copy-start | bytes 3076
  26.2 5.8 %copy-start.51 = (f32[1,256]{1,0:T(1,128)}, f32[1,256]{1,0:T(1,128)S(1)}, u32[]{:S(2)}) copy-start(f32[1,256]{1,0:T(1,128)S(1)} %get-tuple-element.180) | copy-start | bytes 3076
  26.2 5.8 %copy-start.53 = (f32[1,256]{1,0:T(1,128)}, f32[1,256]{1,0:T(1,128)S(1)}, u32[]{:S(2)}) copy-start(f32[1,256]{1,0:T(1,128)S(1)} %get-tuple-element.181) | copy-start | bytes 3076
  26.2 5.8 %copy-start.55 = (f32[1,256]{1,0:T(1,128)}, f32[1,256]{1,0:T(1,128)S(1)}, u32[]{:S(2)}) copy-start(f32[1,256]{1,0:T(1,128)S(1)} %get-tuple-element.182) | copy-start | bytes 3076
  26.2 5.8 %copy-start.57 = (f32[1,256]{1,0:T(1,128)}, f32[1,256]{1,0:T(1,128)S(1)}, u32[]{:S(2)}) copy-start(f32[1,256]{1,0:T(1,128)S(1)} %get-tuple-element.183) | copy-start | bytes 3076
  26.2 5.8 %copy-start.59 = (f32[1,256]{1,0:T(1,128)}, f32[1,256]{1,0:T(1,128)S(1)}, u32[]{:S(2)}) copy-start(f32[1,256]{1,0:T(1,128)S(1)} %get-tuple-element.184) | copy-start | bytes 3076
  26.2 5.8 %copy-start.61 = (f32[1,256]{1,0:T(1,128)}, f32[1,256]{1,0:T(1,128)S(1)}, u32[]{:S(2)}) copy-start(f32[1,256]{1,0:T(1,128)S(1)} %get-tuple-element.185) | copy-start | bytes 3076
  26.3 5.8 %copy-start.63 = (f32[1,256]{1,0:T(1,128)}, f32[1,256]{1,0:T(1,128)S(1)}, u32[]{:S(2)}) copy-start(f32[1,256]{1,0:T(1,128)S(1)} %get-tuple-element.186) | copy-start | bytes 3076
  26.3 5.8 %copy-start.65 = (f32[1,256]{1,0:T(1,128)}, f32[1,256]{1,0:T(1,128)S(1)}, u32[]{:S(2)}) copy-start(f32[1,256]{1,0:T(1,128)S(1)} %get-tuple-element.187) | copy-start | bytes 3076
  26.3 5.8 %copy-start.67 = (f32[1,256]{1,0:T(1,128)}, f32[1,256]{1,0:T(1,128)S(1)}, u32[]{:S(2)}) copy-start(f32[1,256]{1,0:T(1,128)S(1)} %get-tuple-element.188) | copy-start | bytes 3076
  31.8 5.2 %copy-start.1 = (bf16[256,4,5,128]{0,3,2,1:T(8,128)(2,1)}, bf16[256,4,5,128]{0,3,2,1:T(8,128)(2,1)S(1)}, u32[]{:S(2)}) copy-start(bf16[256,4,5,128]{0,3,2,1:T(8,128)(2,1)S(1)} %get-tuple-element.104) | copy-start | bytes 3932164
  38.4 10.6 %collective-permute-start.12 = (bf16[256,2,4,128]{0,3,2,1:T(8,128)(2,1)S(1)}, bf16[256,2,4,128]{0,3,2,1:T(8,128)(2,1)}, u32[]{:S(2)}, u32[]{:S(2)}) collective-permute-start(bf16[256,2,4,128]{0,3,2,1:T(8,128)(2,1)S(1)} %get-tuple-element.198), channel_id=1, source_target_pairs={{0,128},{128,0},{1,129},{129,1},{2,130},{130,2},{3,131},{131,3},{4... | collective-permute-start | bytes 1572872 | tf_op jit(solution)/shard_map/ppermute | solution.py:30
  50.1 12.7 %copy-start.5 = (bf16[256,1,4,128]{0,3,2,1:T(8,128)(2,1)}, bf16[256,1,4,128]{0,3,2,1:T(8,128)(2,1)S(1)}, u32[]{:S(2)}) copy-start(bf16[256,1,4,128]{0,3,2,1:T(8,128)(2,1)S(1)} %get-tuple-element.108) | copy-start | bytes 786436
  50.1 12.7 %copy-start.7 = (bf16[256,1,4,128]{0,3,2,1:T(8,128)(2,1)}, bf16[256,1,4,128]{0,3,2,1:T(8,128)(2,1)S(1)}, u32[]{:S(2)}) copy-start(bf16[256,1,4,128]{0,3,2,1:T(8,128)(2,1)S(1)} %get-tuple-element.109) | copy-start | bytes 786436
  51.1 9.1 %collective-permute-start.13 = (bf16[256,4,1,128]{0,3,2,1:T(8,128)(2,1)}, bf16[256,4,1,128]{0,3,2,1:T(8,128)(2,1)}, u32[]{:S(2)}, u32[]{:S(2)}) collective-permute-start(bf16[256,4,1,128]{0,3,2,1:T(8,128)(2,1)} %get-tuple-element.96), channel_id=1, source_target_pairs={{0,1},{1,2},{2,3},{3,4},{4,5},{5,6},{6,7},{7,8},{8,9},{9,10},{10,1... | collective-permute-start | bytes 786440 | tf_op jit(solution)/shard_map/ppermute | solution.py:34
  54.5 6.6 %collective-permute-start.14 = (bf16[256,4,1,128]{0,3,2,1:T(8,128)(2,1)}, bf16[256,4,1,128]{0,3,2,1:T(8,128)(2,1)}, u32[]{:S(2)}, u32[]{:S(2)}) collective-permute-start(bf16[256,4,1,128]{0,3,2,1:T(8,128)(2,1)} %get-tuple-element.97), channel_id=1, source_target_pairs={{1,0},{2,1},{3,2},{4,3},{5,4},{6,5},{7,6},{8,7},{9,8},{10,9},{11,1... | collective-permute-start | bytes 786440 | tf_op jit(solution)/shard_map/ppermute | solution.py:35
  57.0 13.6 %copy-start.69 = (f32[1,256]{1,0:T(1,128)}, f32[1,256]{1,0:T(1,128)S(1)}, u32[]{:S(2)}) copy-start(f32[1,256]{1,0:T(1,128)S(1)} %get-tuple-element.162) | copy-start | bytes 3076
  57.0 13.6 %copy-start.71 = (f32[1,256]{1,0:T(1,128)}, f32[1,256]{1,0:T(1,128)S(1)}, u32[]{:S(2)}) copy-start(f32[1,256]{1,0:T(1,128)S(1)} %get-tuple-element.163) | copy-start | bytes 3076
  57.0 13.6 %copy-start.73 = (f32[1,256]{1,0:T(1,128)}, f32[1,256]{1,0:T(1,128)S(1)}, u32[]{:S(2)}) copy-start(f32[1,256]{1,0:T(1,128)S(1)} %get-tuple-element.164) | copy-start | bytes 3076
  57.0 13.6 %copy-start.75 = (f32[1,256]{1,0:T(1,128)}, f32[1,256]{1,0:T(1,128)S(1)}, u32[]{:S(2)}) copy-start(f32[1,256]{1,0:T(1,128)S(1)} %get-tuple-element.165) | copy-start | bytes 3076
  60.1 10.6 %copy-start.87 = (f32[1,256]{1,0:T(1,128)}, f32[1,256]{1,0:T(1,128)S(1)}, u32[]{:S(2)}) copy-start(f32[1,256]{1,0:T(1,128)S(1)} %get-tuple-element.144) | copy-start | bytes 3076
  60.1 10.6 %copy-start.89 = (f32[1,256]{1,0:T(1,128)}, f32[1,256]{1,0:T(1,128)S(1)}, u32[]{:S(2)}) copy-start(f32[1,256]{1,0:T(1,128)S(1)} %get-tuple-element.145) | copy-start | bytes 3076
  60.1 10.6 %copy-start.91 = (f32[1,256]{1,0:T(1,128)}, f32[1,256]{1,0:T(1,128)S(1)}, u32[]{:S(2)}) copy-start(f32[1,256]{1,0:T(1,128)S(1)} %get-tuple-element.146) | copy-start | bytes 3076
  60.1 10.6 %copy-start.93 = (f32[1,256]{1,0:T(1,128)}, f32[1,256]{1,0:T(1,128)S(1)}, u32[]{:S(2)}) copy-start(f32[1,256]{1,0:T(1,128)S(1)} %get-tuple-element.147) | copy-start | bytes 3076
  60.1 10.6 %copy-start.95 = (f32[1,256]{1,0:T(1,128)}, f32[1,256]{1,0:T(1,128)S(1)}, u32[]{:S(2)}) copy-start(f32[1,256]{1,0:T(1,128)S(1)} %get-tuple-element.148) | copy-start | bytes 3076
  60.1 10.6 %copy-start.97 = (f32[1,256]{1,0:T(1,128)}, f32[1,256]{1,0:T(1,128)S(1)}, u32[]{:S(2)}) copy-start(f32[1,256]{1,0:T(1,128)S(1)} %get-tuple-element.149) | copy-start | bytes 3076
  60.1 10.6 %copy-start.99 = (f32[1,256]{1,0:T(1,128)}, f32[1,256]{1,0:T(1,128)S(1)}, u32[]{:S(2)}) copy-start(f32[1,256]{1,0:T(1,128)S(1)} %get-tuple-element.150) | copy-start | bytes 3076
  60.1 10.6 %copy-start.101 = (f32[1,256]{1,0:T(1,128)}, f32[1,256]{1,0:T(1,128)S(1)}, u32[]{:S(2)}) copy-start(f32[1,256]{1,0:T(1,128)S(1)} %get-tuple-element.151) | copy-start | bytes 3076
  60.1 10.6 %copy-start.103 = (f32[1,256]{1,0:T(1,128)}, f32[1,256]{1,0:T(1,128)S(1)}, u32[]{:S(2)}) copy-start(f32[1,256]{1,0:T(1,128)S(1)} %get-tuple-element.152) | copy-start | bytes 3076
  60.2 10.6 %copy-start.105 = (f32[1,256]{1,0:T(1,128)}, f32[1,256]{1,0:T(1,128)S(1)}, u32[]{:S(2)}) copy-start(f32[1,256]{1,0:T(1,128)S(1)} %get-tuple-element.153) | copy-start | bytes 3076
  60.2 10.6 %copy-start.107 = (f32[1,256]{1,0:T(1,128)}, f32[1,256]{1,0:T(1,128)S(1)}, u32[]{:S(2)}) copy-start(f32[1,256]{1,0:T(1,128)S(1)} %get-tuple-element.154) | copy-start | bytes 3076
  60.2 10.6 %copy-start.109 = (f32[1,256]{1,0:T(1,128)}, f32[1,256]{1,0:T(1,128)S(1)}, u32[]{:S(2)}) copy-start(f32[1,256]{1,0:T(1,128)S(1)} %get-tuple-element.155) | copy-start | bytes 3076
  60.2 10.6 %copy-start.111 = (f32[1,256]{1,0:T(1,128)}, f32[1,256]{1,0:T(1,128)S(1)}, u32[]{:S(2)}) copy-start(f32[1,256]{1,0:T(1,128)S(1)} %get-tuple-element.156) | copy-start | bytes 3076
  60.2 10.6 %copy-start.113 = (f32[1,256]{1,0:T(1,128)}, f32[1,256]{1,0:T(1,128)S(1)}, u32[]{:S(2)}) copy-start(f32[1,256]{1,0:T(1,128)S(1)} %get-tuple-element.157) | copy-start | bytes 3076
  60.2 10.6 %copy-start.115 = (f32[1,256]{1,0:T(1,128)}, f32[1,256]{1,0:T(1,128)S(1)}, u32[]{:S(2)}) copy-start(f32[1,256]{1,0:T(1,128)S(1)} %get-tuple-element.158) | copy-start | bytes 3076
  60.2 10.6 %copy-start.117 = (f32[1,256]{1,0:T(1,128)}, f32[1,256]{1,0:T(1,128)S(1)}, u32[]{:S(2)}) copy-start(f32[1,256]{1,0:T(1,128)S(1)} %get-tuple-element.159) | copy-start | bytes 3076
  60.2 10.6 %copy-start.119 = (f32[1,256]{1,0:T(1,128)}, f32[1,256]{1,0:T(1,128)S(1)}, u32[]{:S(2)}) copy-start(f32[1,256]{1,0:T(1,128)S(1)} %get-tuple-element.160) | copy-start | bytes 3076
  60.2 10.6 %copy-start.121 = (f32[1,256]{1,0:T(1,128)}, f32[1,256]{1,0:T(1,128)S(1)}, u32[]{:S(2)}) copy-start(f32[1,256]{1,0:T(1,128)S(1)} %get-tuple-element.161) | copy-start | bytes 3076
  66.8 16.3 %collective-permute-start.1 = (bf16[256,2,4,128]{0,3,2,1:T(8,128)(2,1)S(1)}, bf16[256,2,4,128]{0,3,2,1:T(8,128)(2,1)}, u32[]{:S(2)}, u32[]{:S(2)}) collective-permute-start(bf16[256,2,4,128]{0,3,2,1:T(8,128)(2,1)S(1)} %get-tuple-element.200), channel_id=1, source_target_pairs={{0,128},{128,0},{1,129},{129,1},{2,130},{130,2},{3,131},{131,3},{4... | collective-permute-start | bytes 1572872 | tf_op jit(solution)/shard_map/ppermute | solution.py:30
  84.2 10.7 %collective-permute-start.2 = (bf16[256,4,1,128]{0,3,2,1:T(8,128)(2,1)S(1)}, bf16[256,4,1,128]{0,3,2,1:T(8,128)(2,1)S(1)}, u32[]{:S(2)}, u32[]{:S(2)}) collective-permute-start(bf16[256,4,1,128]{0,3,2,1:T(8,128)(2,1)S(1)} %get-tuple-element.102), channel_id=1, source_target_pairs={{0,1},{1,2},{2,3},{3,4},{4,5},{5,6},{6,7},{7,8},{8,9},{9,10},{10,1... | collective-permute-start | bytes 786440 | tf_op jit(solution)/shard_map/ppermute | solution.py:34
  84.3 11.1 %collective-permute-start.3 = (bf16[256,4,1,128]{0,3,2,1:T(8,128)(2,1)S(1)}, bf16[256,4,1,128]{0,3,2,1:T(8,128)(2,1)S(1)}, u32[]{:S(2)}, u32[]{:S(2)}) collective-permute-start(bf16[256,4,1,128]{0,3,2,1:T(8,128)(2,1)S(1)} %get-tuple-element.103), channel_id=1, source_target_pairs={{1,0},{2,1},{3,2},{4,3},{5,4},{6,5},{7,6},{8,7},{9,8},{10,9},{11,1... | collective-permute-start | bytes 786440 | tf_op jit(solution)/shard_map/ppermute | solution.py:35
  112.1 62.9 %collective-permute-start.8 = (bf16[256,2,1,128]{0,3,2,1:T(8,128)(2,1)S(1)}, bf16[256,2,1,128]{0,3,2,1:T(8,128)(2,1)S(1)}, u32[]{:S(2)}, u32[]{:S(2)}) collective-permute-start(bf16[256,2,1,128]{0,3,2,1:T(8,128)(2,1)S(1)} %get-tuple-element.112), channel_id=1, source_target_pairs={{0,1},{1,2},{2,3},{3,4},{4,5},{5,6},{6,7},{7,8},{8,9},{9,10},{10,1... | collective-permute-start | bytes 393224 | tf_op jit(solution)/shard_map/ppermute | solution.py:49
  112.2 62.7 %collective-permute-start.7 = (bf16[256,2,1,128]{0,3,2,1:T(8,128)(2,1)S(1)}, bf16[256,2,1,128]{0,3,2,1:T(8,128)(2,1)S(1)}, u32[]{:S(2)}, u32[]{:S(2)}) collective-permute-start(bf16[256,2,1,128]{0,3,2,1:T(8,128)(2,1)S(1)} %get-tuple-element.112), channel_id=1, source_target_pairs={{0,129},{1,130},{2,131},{3,132},{4,133},{5,134},{6,135},{7,136},{8... | collective-permute-start | bytes 393224 | tf_op jit(solution)/shard_map/ppermute | solution.py:51
  112.6 62.4 %collective-permute-start.11 = (bf16[256,2,1,128]{0,3,2,1:T(8,128)(2,1)S(1)}, bf16[256,2,1,128]{0,3,2,1:T(8,128)(2,1)S(1)}, u32[]{:S(2)}, u32[]{:S(2)}) collective-permute-start(bf16[256,2,1,128]{0,3,2,1:T(8,128)(2,1)S(1)} %get-tuple-element.113), channel_id=1, source_target_pairs={{1,0},{2,1},{3,2},{4,3},{5,4},{6,5},{7,6},{8,7},{9,8},{10,9},{11,1... | collective-permute-start | bytes 393224 | tf_op jit(solution)/shard_map/ppermute | solution.py:50
  120.9 54.0 %collective-permute-start.10 = (bf16[256,2,1,128]{0,3,2,1:T(8,128)(2,1)S(1)}, bf16[256,2,1,128]{0,3,2,1:T(8,128)(2,1)S(1)}, u32[]{:S(2)}, u32[]{:S(2)}) collective-permute-start(bf16[256,2,1,128]{0,3,2,1:T(8,128)(2,1)S(1)} %get-tuple-element.113), channel_id=1, source_target_pairs={{1,128},{2,129},{3,130},{4,131},{5,132},{6,133},{7,134},{8,135},{9... | collective-permute-start | bytes 393224 | tf_op jit(solution)/shard_map/ppermute | solution.py:52
  129.1 45.9 %collective-permute-start.9 = (bf16[256,2,4,128]{0,3,2,1:T(8,128)(2,1)S(1)}, bf16[256,2,4,128]{0,3,2,1:T(8,128)(2,1)S(1)}, u32[]{:S(2)}, u32[]{:S(2)}) collective-permute-start(bf16[256,2,4,128]{0,3,2,1:T(8,128)(2,1)S(1)} %get-tuple-element.201), channel_id=1, source_target_pairs={{0,128},{128,0},{1,129},{129,1},{2,130},{130,2},{3,131},{131,3},{4... | collective-permute-start | bytes 1572872 | tf_op jit(solution)/shard_map/ppermute | solution.py:48
  (74 other events, 138.0 us)

commit v2 on v0

--- a/solution.py
+++ b/solution.py
@@ -226,7 +226,7 @@
     base += size
 
     span = piece
-    gathers = [tuple(f for f in group if f[0] != "own") for group in scatter]
+    gathers = [tuple(f for group in scatter for f in group if f[0] != "own")]
     for j in range(len(gathers) - 1, -1, -1):
         group = gathers[j]
         if not group:
@@ -264,7 +264,9 @@
     for group in scatter:
         length //= group_size(group)
         shapes.append((group_size(group), length))
-    semaphores = sum(group_size(group) for group in scatter) * 2 + group_size(last)
+    semaphores = sum(group_size(group) for group in scatter) + group_size(last) + math.prod(
+        f[2] for group in scatter for f in group if f[0] != "own"
+    )
     scratch = [pltpu.VMEM((n, 8, 128), jnp.float32) for _, n in shapes]
     scratch += [pltpu.VMEM((size, n, 8, 128), jnp.float32) for size, n in shapes]
     scratch += [

time: 178 us -> 177 us (level)
  transfers between devices with their start and end apart: 13 -> 13, of which waited for: 9 -> 9; matrix products, arithmetic and copies ran while one was open for 17% -> 17% of each run, Pallas kernels for 26% -> 25%
where the time goes in v2:
time: 177 us; the launch traced here: 174 us
  Pallas kernels  43.2 us (24%)
  other arithmetic  31.3 us (18%)
  starting transfers between devices  29 us (16%)
  local copies, waits for them, and re-layouts  27.2 us (15%)
  waiting for transfers between devices  26.9 us (15%)
  matrix products  13.6 us (8%)
  between operations  2.66 us (2%)
    pallas_call x1, Pallas kernels, tree_reduce(): pl.pallas_call(functools.partial(reduce_kernel, plan), out_shape=jax.Shap...  43.2 us
    ppermute x4, waiting for transfers between devices, extended(): theirs = lax.ppermute(jnp.concatenate([first, last], axis=dim), axis, up)  15.6 us
    ppermute x4, starting transfers between devices, extended(): after = lax.ppermute(first, axis, down)  11.8 us
    unnamed x243, local copies, waits for them, and re-layouts  10.1 us
    ppermute x4, starting transfers between devices, extended(): before = lax.ppermute(last, axis, up)  7.74 us
    dot_general x2, matrix products, backmap(): jnp.dot(weights, flattened, preferred_element_type=jnp.float32)  6.82 us
    ppermute x4, waiting for transfers between devices, extended(): before = lax.ppermute(last, axis, up)  6.45 us
    concatenate x8, other arithmetic, ring_z(): return jnp.concatenate([padded[..., -1:], padded, padded[..., :1]], axis=3)  6.1 us
  transfers between devices with their start and end apart: 13, of which 9 were waited for; matrix products, arithmetic and copies ran while one was open for 17% of the time, Pallas kernels for 25%

profile of v2, /device:TPU:1, one launch (start us, length us, event | category | flops | bytes accessed | tf_op | source)
XLA Modules:
  0.0 173.9 jit_solution(12306957812756845908)
XLA Ops:
  0.6 0.9 copy.30
  1.5 0.9 copy.31
  2.4 0.7 pad_maximum_fusion.60
  3.2 3.8 %collective-permute-start = (bf16[72448]{0:T(1024)(128)(2,1)S(1)}, bf16[72448]{0:T(1024)(128)(2,1)S(1)}, u32[]{:S(2)}, u32[]{:S(2)}) collective-permute-start(bf16[72448]{0:T(1024)(128)(2,1)S(1)} %pad_maximum_fusion.60), channel_id=1, source_target_pairs={{0,128},{128,0},{1,129},{129,1},{2,130},{130,2},{3,131},{131,3},{4... | collective-permute-start | bytes 434696 | tf_op jit(solution)/shard_map/ppermute | solution.py:42
  7.0 1.3 copy.13
  8.4 1.1 collective-permute-done
  9.5 0.8 broadcast_select_fusion.1
  10.3 0.7 fusion.296
  11.0 11.6 %collective-permute-done.4 = bf16[256,2,4,128]{0,3,2,1:T(8,128)(2,1)S(1)} collective-permute-done((bf16[256,2,4,128]{0,3,2,1:T(8,128)(2,1)S(1)}, bf16[256,2,4,128]{0,3,2,1:T(8,128)(2,1)S(1)}, u32[]{:S(2)}, u32[]{:S(2)}) %collective-permute-start.4) | collective-permute-done | bytes 524320 | tf_op jit(solution)/shard_map/ppermute | solution.py:30
  22.7 2.0 %collective-permute-start.5 = (bf16[256,4,1,128]{0,3,2,1:T(8,128)(2,1)S(1)}, bf16[256,4,1,128]{0,3,2,1:T(8,128)(2,1)S(1)}, u32[]{:S(2)}, u32[]{:S(2)}) collective-permute-start(bf16[256,4,1,128]{0,3,2,1:T(8,128)(2,1)S(1)} %get-tuple-element.108), channel_id=1, source_target_pairs={{0,1},{1,2},{2,3},{3,4},{4,5},{5,6},{6,7},{7,8},{8,9},{9,10},{10,1... | collective-permute-start | bytes 786440 | tf_op jit(solution)/shard_map/ppermute | solution.py:34
  24.7 0.6 slice.924
  25.4 0.6 slice.926
  26.2 1.8 %collective-permute-done.5 = bf16[256,4,1,128]{0,3,2,1:T(8,128)(2,1)S(1)} collective-permute-done((bf16[256,4,1,128]{0,3,2,1:T(8,128)(2,1)S(1)}, bf16[256,4,1,128]{0,3,2,1:T(8,128)(2,1)S(1)}, u32[]{:S(2)}, u32[]{:S(2)}) %collective-permute-start.5) | collective-permute-done | bytes 262176 | tf_op jit(solution)/shard_map/ppermute | solution.py:34
  28.0 2.5 %collective-permute-done.6 = bf16[256,4,1,128]{0,3,2,1:T(8,128)(2,1)S(1)} collective-permute-done((bf16[256,4,1,128]{0,3,2,1:T(8,128)(2,1)S(1)}, bf16[256,4,1,128]{0,3,2,1:T(8,128)(2,1)S(1)}, u32[]{:S(2)}, u32[]{:S(2)}) %collective-permute-start.6) | collective-permute-done | bytes 262176 | tf_op jit(solution)/shard_map/ppermute | solution.py:35
  30.8 0.7 fusion.5
  32.0 0.7 copy-done
  32.8 4.2 %fusion.36 = bf16[256,2,4,128]{0,3,2,1:T(8,128)(2,1)S(1)} fusion(bf16[256,2,4,128]{0,3,2,1:T(8,128)(2,1)S(1)} %copy.13, f32[256]{0:T(256)S(1)} %bitcast.227, f32[256]{0:T(256)S(1)} %bitcast.229, f32[256]{0:T(256)S(1)} %bitcast.225, f32[256]{0:T(256)S(1)} %bitcast.223, f32[256]{0:T(256)S(1)} %bitcast.221, f32[256]{0:T(256)S(1)} %bitcast.219, ...), kind=kLoop, calls=%fused_computation.190 | loop fusion | flops 21757952 | bytes 14183424 | tf_op jit(solution)/shard_map/convert_element_type | solution.py:329
  37.1 1.3 multiply_convert_fusion
  38.4 2.3 %collective-permute-start.10 = (bf16[256,2,4,128]{0,3,2,1:T(8,128)(2,1)S(1)}, bf16[256,2,4,128]{0,3,2,1:T(8,128)(2,1)}, u32[]{:S(2)}, u32[]{:S(2)}) collective-permute-start(bf16[256,2,4,128]{0,3,2,1:T(8,128)(2,1)S(1)} %get-tuple-element.194), channel_id=1, source_target_pairs={{0,128},{128,0},{1,129},{129,1},{2,130},{130,2},{3,131},{131,3},{4... | collective-permute-start | bytes 1572872 | tf_op jit(solution)/shard_map/ppermute | solution.py:30
  40.7 1.1 copy.11
  41.9 1.2 reshape.539
  43.0 2.1 %copy.12 = bf16[1024,256]{1,0:T(8,128)(2,1)} copy(bf16[1024,256]{0,1:T(8,128)(2,1)} %bitcast.196) | data formatting | bytes 1048576 | tf_op jit(solution)/shard_map/dot_general | solution.py:92
  45.1 4.0 %collective-permute-done.10 = bf16[256,2,4,128]{0,3,2,1:T(8,128)(2,1)} collective-permute-done((bf16[256,2,4,128]{0,3,2,1:T(8,128)(2,1)S(1)}, bf16[256,2,4,128]{0,3,2,1:T(8,128)(2,1)}, u32[]{:S(2)}, u32[]{:S(2)}) %collective-permute-start.10) | collective-permute-done | bytes 524320 | tf_op jit(solution)/shard_map/ppermute | solution.py:30
  49.0 1.1 fusion.290
  50.1 1.0 pad_maximum_fusion.50
  51.1 3.4 %collective-permute-start.11 = (bf16[256,4,1,128]{0,3,2,1:T(8,128)(2,1)}, bf16[256,4,1,128]{0,3,2,1:T(8,128)(2,1)}, u32[]{:S(2)}, u32[]{:S(2)}) collective-permute-start(bf16[256,4,1,128]{0,3,2,1:T(8,128)(2,1)} %get-tuple-element.96), channel_id=1, source_target_pairs={{0,1},{1,2},{2,3},{3,4},{4,5},{5,6},{6,7},{7,8},{8,9},{9,10},{10,1... | collective-permute-start | bytes 786440 | tf_op jit(solution)/shard_map/ppermute | solution.py:34
  54.5 1.9 %collective-permute-start.12 = (bf16[256,4,1,128]{0,3,2,1:T(8,128)(2,1)}, bf16[256,4,1,128]{0,3,2,1:T(8,128)(2,1)}, u32[]{:S(2)}, u32[]{:S(2)}) collective-permute-start(bf16[256,4,1,128]{0,3,2,1:T(8,128)(2,1)} %get-tuple-element.97), channel_id=1, source_target_pairs={{1,0},{2,1},{3,2},{4,3},{5,4},{6,5},{7,6},{8,7},{9,8},{10,9},{11,1... | collective-permute-start | bytes 786440 | tf_op jit(solution)/shard_map/ppermute | solution.py:35
  56.4 0.6 fusion.266
  57.0 1.5 slice.933
  58.5 1.5 slice.935
  60.2 0.8 collective-permute-done.12
  61.1 1.7 fusion.1
  62.8 1.3 maximum_maximum_fusion.3
  64.2 2.6 %fusion.104 = (f32[256]{0:T(256)}, f32[256]{0:T(256)}, f32[256]{0:T(256)}, f32[256]{0:T(256)}, f32[256]{0:T(256)}, /*index=5*/f32[256]{0:T(256)}, f32[256]{0:T(2...) fusion(bf16[256,4,5,128]{0,3,2,1:T(8,128)(2,1)S(1)} %get-tuple-, ...), kind=kOutput, calls=%fused_computation.258 | convolution fusion | flops 144438272 | bytes 7483392 | tf_op jit(solution)/shard_map/dot_general | solution.py:92
  66.8 2.7 %collective-permute-start.1 = (bf16[256,2,4,128]{0,3,2,1:T(8,128)(2,1)S(1)}, bf16[256,2,4,128]{0,3,2,1:T(8,128)(2,1)}, u32[]{:S(2)}, u32[]{:S(2)}) collective-permute-start(bf16[256,2,4,128]{0,3,2,1:T(8,128)(2,1)S(1)} %get-tuple-element.196), channel_id=1, source_target_pairs={{0,128},{128,0},{1,129},{129,1},{2,130},{130,2},{3,131},{131,3},{4... | collective-permute-start | bytes 1572872 | tf_op jit(solution)/shard_map/ppermute | solution.py:30
  69.5 1.3 fusion
  71.2 5.1 %fusion.8 = f32[256,256]{1,0:T(8,128)} fusion(bf16[256,2,4,128]{0,3,2,1:T(8,128)(2,1)S(1)} %copy-done.10, bf16[256,2,4,128]{0,3,2,1:T(8,128)(2,1)S(1)} %get-tuple-element.194, f32[256]{0:T(256)S(1)} %bitcast.311, f32[256]{0:T(256)S(1)} %bitcast.313, f32[256]{0:T(256)S(1)} %bitcast.309, f32[256]{0:T(256)S(1)} %bitcast.307, f32[256]{0:T(256)S(1)} %bitcast.305, ...), kind=kOutput, calls=%fused_computation.161 | convolution fusion | flops 156041216 | bytes 14445568 | tf_op jit(solution)/shard_map/dot_general | solution.py:97
  76.2 3.2 %fusion.105 = (f32[256]{0:T(256)S(1)}, f32[256]{0:T(256)S(1)}, f32[256]{0:T(256)S(1)}, f32[256]{0:T(256)S(1)}, f32[256]{0:T(256)}, /*index=5*/f32[256]{0:T(256)}...) fusion(bf16[256,2,4,128]{0,3,2,1:T(8,128)(2,1)S(1)} %get-tuple-, ...), kind=kLoop, calls=%fused_computation.259 | loop fusion | flops 12579072 | bytes 7879680 | tf_op jit(solution)/shard_map/reduce_sum | solution.py:79
  79.4 2.9 %stack.232 = f32[27,256]{1,0:T(8,128)S(1)} concatenate(f32[1,256]{1,0:T(1,128)} %bitcast.355, f32[1,256]{1,0:T(1,128)} %bitcast.291, f32[1,256]{1,0:T(1,128)} %bitcast.290, f32[1,256]{1,0:T(1,128)} %bitcast.354, f32[1,256]{1,0:T(1,128)} %bitcast.295, f32[1,256]{1,0:T(1,128)S(1)} %bitcast.283, f32[1,256]{1,0:T(1,128)} %bitcast.361, f32[1,256]{1,0:T(1,128)} %bitcast.352, ...), dimensions={0} | concatenate | bytes 55296 | tf_op jit(solution)/shard_map/stack | solution.py:80
  82.3 1.0 slice_bitcast_fusion.2
  83.3 1.1 fusion.292
  84.5 9.9 %collective-permute-start.3 = (bf16[256,4,1,128]{0,3,2,1:T(8,128)(2,1)S(1)}, bf16[256,4,1,128]{0,3,2,1:T(8,128)(2,1)S(1)}, u32[]{:S(2)}, u32[]{:S(2)}) collective-permute-start(bf16[256,4,1,128]{0,3,2,1:T(8,128)(2,1)S(1)} %get-tuple-element.105), channel_id=1, source_target_pairs={{1,0},{2,1},{3,2},{4,3},{5,4},{6,5},{7,6},{8,7},{9,8},{10,9},{11,1... | collective-permute-start | bytes 786440 | tf_op jit(solution)/shard_map/ppermute | solution.py:35
  94.6 0.6 collective-permute-done.2
  95.1 0.4 collective-permute-done.3
  95.6 0.7 fusion.6
  97.1 0.7 copy-done.14
  98.1 4.8 %fusion.149 = bf16[256,2,4,128]{0,3,2,1:T(8,128)(2,1)S(1)} fusion(f32[256,2,4,128]{0,3,2,1:T(8,128)S(1)} %copy-done.14, bf16[256,2,4,128]{0,3,2,1:T(8,128)(2,1)S(1)} %get-tuple-element.196, bf16[256,4,6,129]{0,3,2,1:T(8,128)(2,1)S(1)} %fusion.6, bf16[256,4,5,128]{0,3,2,1:T(8,128)(2,1)S(1)} %get-tuple-element.103, bf16[256,4,6,129]{0,3,2,1:T(8,128)(2,1)S(1)} %fusion.7, ...), kind=kLoop, calls=%fused_computation.305 | loop fusion | flops 23855104 | bytes 15232000 | tf_op jit(solution)/shard_map/convert_element_type | solution.py:340
  102.9 4.3 %fusion.146 = (f32[256]{0:T(256)S(1)}, f32[256]{0:T(256)S(1)}, f32[256]{0:T(256)S(1)}, f32[256]{0:T(256)S(1)}, f32[256]{0:T(256)S(1)}, /*index=5*/f32[256]{0:T(2...) fusion(bf16[256,4,5,128]{0,3,2,1:T(8,128)(2,1)} %copy-done.9, ...), kind=kOutput, calls=%fused_computation.300 | convolution fusion | flops 144438272 | bytes 7483392 | tf_op jit(solution)/shard_map/dot_general | solution.py:92
  107.6 1.0 copy-done.2
  108.5 2.6 %fusion.147 = (f32[256]{0:T(256)S(1)}, f32[256]{0:T(256)S(1)}, f32[256]{0:T(256)S(1)}, f32[256]{0:T(256)S(1)}, f32[256]{0:T(256)S(1)}, /*index=5*/f32[256]{0:T(2...) fusion(bf16[256,2,4,128]{0,3,2,1:T(8,128)(2,1)S(1)} %get-tuple-, ...), kind=kLoop, calls=%fused_computation.301 | loop fusion | flops 12579072 | bytes 7879680 | tf_op jit(solution)/shard_map/reduce_sum | solution.py:79
  111.1 0.5 collective-permute-start.7
  112.4 0.5 select_maximum_fusion
  112.9 1.4 reshape.550.x_ref
  114.3 43.2 %shard_map.101 = f32[80,8,128]{2,1,0:T(8,128)} custom-call(f32[160,8,128]{2,1,0:T(8,128)} %reshape.550.x_ref), custom_call_target="tpu_custom_call" | custom-call | bytes 41943040 | tf_op jit(solution)/shard_map/pallas_call | solution.py:278
  157.7 2.2 %collective-permute-start.8 = (bf16[256,4,1,128]{0,3,2,1:T(8,128)(2,1)S(1)}, bf16[256,4,1,128]{0,3,2,1:T(8,128)(2,1)S(1)}, u32[]{:S(2)}, u32[]{:S(2)}) collective-permute-start(bf16[256,4,1,128]{0,3,2,1:T(8,128)(2,1)S(1)} %get-tuple-element.100), channel_id=1, source_target_pairs={{0,1},{1,2},{2,3},{3,4},{4,5},{5,6},{6,7},{7,8},{8,9},{9,10},{10,1... | collective-permute-start | bytes 786440 | tf_op jit(solution)/shard_map/ppermute | solution.py:34
  159.9 0.7 reshape.552
  160.6 0.7 reshape.551
  161.3 0.6 fusion.294
  161.9 4.1 %collective-permute-done.8 = bf16[256,4,1,128]{0,3,2,1:T(8,128)(2,1)S(1)} collective-permute-done((bf16[256,4,1,128]{0,3,2,1:T(8,128)(2,1)S(1)}, bf16[256,4,1,128]{0,3,2,1:T(8,128)(2,1)S(1)}, u32[]{:S(2)}, u32[]{:S(2)}) %collective-permute-start.8) | collective-permute-done | bytes 262176 | tf_op jit(solution)/shard_map/ppermute | solution.py:34
  166.0 0.7 fusion.2
  166.7 0.3 fusion.3
  167.5 0.6 copy-done.11
  168.3 4.6 %fusion.148 = bf16[256,2,4,128]{0,3,2,1:T(8,128)(2,1)S(1)} fusion(bf16[256,2,4,128]{0,3,2,1:T(8,128)(2,1)S(1)} %get-tuple-element.197, bf16[256,2,4,128]{0,3,2,1:T(8,128)(2,1)S(1)} %copy-done.11, bf16[256,4,6,129]{0,3,2,1:T(8,128)(2,1)S(1)} %fusion.2, bf16[256,4,5,128]{0,3,2,1:T(8,128)(2,1)S(1)} %get-tuple-element.99, ...), kind=kLoop, calls=%fused_computation.304 | loop fusion | flops 22282240 | bytes 14707712 | tf_op jit(solution)/shard_map/convert_element_type | solution.py:345
  172.9 1.1 copy.22
  (268 shorter events, 3.6 us)
Async XLA Ops:
  3.2 6.3 %collective-permute-start = (bf16[72448]{0:T(1024)(128)(2,1)S(1)}, bf16[72448]{0:T(1024)(128)(2,1)S(1)}, u32[]{:S(2)}, u32[]{:S(2)}) collective-permute-start(bf16[72448]{0:T(1024)(128)(2,1)S(1)} %pad_maximum_fusion.60), channel_id=1, source_target_pairs={{0,128},{128,0},{1,129},{129,1},{2,130},{130,2},{3,131},{131,3},{4... | collective-permute-start | bytes 434696 | tf_op jit(solution)/shard_map/ppermute | solution.py:42
  8.3 14.3 %collective-permute-start.4 = (bf16[256,2,4,128]{0,3,2,1:T(8,128)(2,1)S(1)}, bf16[256,2,4,128]{0,3,2,1:T(8,128)(2,1)S(1)}, u32[]{:S(2)}, u32[]{:S(2)}) collective-permute-start(bf16[256,2,4,128]{0,3,2,1:T(8,128)(2,1)S(1)} %copy.13), channel_id=1, source_target_pairs={{0,128},{128,0},{1,129},{129,1},{2,130},{130,2},{3,131},{131,3},{4... | collective-permute-start | bytes 1572872 | tf_op jit(solution)/shard_map/ppermute | solution.py:30
  22.6 9.2 %copy-start.3 = (bf16[256,1,4,128]{0,3,2,1:T(8,128)(2,1)}, bf16[256,1,4,128]{0,3,2,1:T(8,128)(2,1)S(1)}, u32[]{:S(2)}) copy-start(bf16[256,1,4,128]{0,3,2,1:T(8,128)(2,1)S(1)} %get-tuple-element.117) | copy-start | bytes 786436
  22.7 5.3 %collective-permute-start.5 = (bf16[256,4,1,128]{0,3,2,1:T(8,128)(2,1)S(1)}, bf16[256,4,1,128]{0,3,2,1:T(8,128)(2,1)S(1)}, u32[]{:S(2)}, u32[]{:S(2)}) collective-permute-start(bf16[256,4,1,128]{0,3,2,1:T(8,128)(2,1)S(1)} %get-tuple-element.108), channel_id=1, source_target_pairs={{0,1},{1,2},{2,3},{3,4},{4,5},{5,6},{6,7},{7,8},{8,9},{9,10},{10,1... | collective-permute-start | bytes 786440 | tf_op jit(solution)/shard_map/ppermute | solution.py:34
  24.7 5.8 %collective-permute-start.6 = (bf16[256,4,1,128]{0,3,2,1:T(8,128)(2,1)S(1)}, bf16[256,4,1,128]{0,3,2,1:T(8,128)(2,1)S(1)}, u32[]{:S(2)}, u32[]{:S(2)}) collective-permute-start(bf16[256,4,1,128]{0,3,2,1:T(8,128)(2,1)S(1)} %get-tuple-element.109), channel_id=1, source_target_pairs={{1,0},{2,1},{3,2},{4,3},{5,4},{6,5},{7,6},{8,7},{9,8},{10,9},{11,1... | collective-permute-start | bytes 786440 | tf_op jit(solution)/shard_map/ppermute | solution.py:35
  24.7 7.1 %copy-start.24 = (f32[1,256]{1,0:T(1,128)}, f32[1,256]{1,0:T(1,128)S(1)}, u32[]{:S(2)}) copy-start(f32[1,256]{1,0:T(1,128)S(1)} %get-tuple-element.193) | copy-start | bytes 3076
  26.0 5.8 %copy-start.26 = (f32[1,256]{1,0:T(1,128)}, f32[1,256]{1,0:T(1,128)S(1)}, u32[]{:S(2)}) copy-start(f32[1,256]{1,0:T(1,128)S(1)} %get-tuple-element.167) | copy-start | bytes 3076
  26.1 5.8 %copy-start.28 = (f32[1,256]{1,0:T(1,128)}, f32[1,256]{1,0:T(1,128)S(1)}, u32[]{:S(2)}) copy-start(f32[1,256]{1,0:T(1,128)S(1)} %get-tuple-element.168) | copy-start | bytes 3076
  26.1 5.8 %copy-start.30 = (f32[1,256]{1,0:T(1,128)}, f32[1,256]{1,0:T(1,128)S(1)}, u32[]{:S(2)}) copy-start(f32[1,256]{1,0:T(1,128)S(1)} %get-tuple-element.169) | copy-start | bytes 3076
  26.1 5.8 %copy-start.32 = (f32[1,256]{1,0:T(1,128)}, f32[1,256]{1,0:T(1,128)S(1)}, u32[]{:S(2)}) copy-start(f32[1,256]{1,0:T(1,128)S(1)} %get-tuple-element.170) | copy-start | bytes 3076
  26.1 5.8 %copy-start.34 = (f32[1,256]{1,0:T(1,128)}, f32[1,256]{1,0:T(1,128)S(1)}, u32[]{:S(2)}) copy-start(f32[1,256]{1,0:T(1,128)S(1)} %get-tuple-element.171) | copy-start | bytes 3076
  26.1 5.8 %copy-start.36 = (f32[1,256]{1,0:T(1,128)}, f32[1,256]{1,0:T(1,128)S(1)}, u32[]{:S(2)}) copy-start(f32[1,256]{1,0:T(1,128)S(1)} %get-tuple-element.172) | copy-start | bytes 3076
  26.1 5.8 %copy-start.38 = (f32[1,256]{1,0:T(1,128)}, f32[1,256]{1,0:T(1,128)S(1)}, u32[]{:S(2)}) copy-start(f32[1,256]{1,0:T(1,128)S(1)} %get-tuple-element.173) | copy-start | bytes 3076
  26.1 5.8 %copy-start.40 = (f32[1,256]{1,0:T(1,128)}, f32[1,256]{1,0:T(1,128)S(1)}, u32[]{:S(2)}) copy-start(f32[1,256]{1,0:T(1,128)S(1)} %get-tuple-element.174) | copy-start | bytes 3076
  26.1 5.8 %copy-start.42 = (f32[1,256]{1,0:T(1,128)}, f32[1,256]{1,0:T(1,128)S(1)}, u32[]{:S(2)}) copy-start(f32[1,256]{1,0:T(1,128)S(1)} %get-tuple-element.175) | copy-start | bytes 3076
  26.2 5.8 %copy-start.44 = (f32[1,256]{1,0:T(1,128)}, f32[1,256]{1,0:T(1,128)S(1)}, u32[]{:S(2)}) copy-start(f32[1,256]{1,0:T(1,128)S(1)} %get-tuple-element.176) | copy-start | bytes 3076
  26.2 5.8 %copy-start.46 = (f32[1,256]{1,0:T(1,128)}, f32[1,256]{1,0:T(1,128)S(1)}, u32[]{:S(2)}) copy-start(f32[1,256]{1,0:T(1,128)S(1)} %get-tuple-element.177) | copy-start | bytes 3076
  26.2 5.8 %copy-start.48 = (f32[1,256]{1,0:T(1,128)}, f32[1,256]{1,0:T(1,128)S(1)}, u32[]{:S(2)}) copy-start(f32[1,256]{1,0:T(1,128)S(1)} %get-tuple-element.178) | copy-start | bytes 3076
  26.2 5.8 %copy-start.50 = (f32[1,256]{1,0:T(1,128)}, f32[1,256]{1,0:T(1,128)S(1)}, u32[]{:S(2)}) copy-start(f32[1,256]{1,0:T(1,128)S(1)} %get-tuple-element.179) | copy-start | bytes 3076
  26.2 5.8 %copy-start.52 = (f32[1,256]{1,0:T(1,128)}, f32[1,256]{1,0:T(1,128)S(1)}, u32[]{:S(2)}) copy-start(f32[1,256]{1,0:T(1,128)S(1)} %get-tuple-element.180) | copy-start | bytes 3076
  26.2 5.8 %copy-start.54 = (f32[1,256]{1,0:T(1,128)}, f32[1,256]{1,0:T(1,128)S(1)}, u32[]{:S(2)}) copy-start(f32[1,256]{1,0:T(1,128)S(1)} %get-tuple-element.181) | copy-start | bytes 3076
  26.2 5.8 %copy-start.56 = (f32[1,256]{1,0:T(1,128)}, f32[1,256]{1,0:T(1,128)S(1)}, u32[]{:S(2)}) copy-start(f32[1,256]{1,0:T(1,128)S(1)} %get-tuple-element.182) | copy-start | bytes 3076
  26.2 5.8 %copy-start.58 = (f32[1,256]{1,0:T(1,128)}, f32[1,256]{1,0:T(1,128)S(1)}, u32[]{:S(2)}) copy-start(f32[1,256]{1,0:T(1,128)S(1)} %get-tuple-element.183) | copy-start | bytes 3076
  26.2 5.8 %copy-start.60 = (f32[1,256]{1,0:T(1,128)}, f32[1,256]{1,0:T(1,128)S(1)}, u32[]{:S(2)}) copy-start(f32[1,256]{1,0:T(1,128)S(1)} %get-tuple-element.184) | copy-start | bytes 3076
  31.8 5.2 %copy-start.1 = (bf16[256,4,5,128]{0,3,2,1:T(8,128)(2,1)}, bf16[256,4,5,128]{0,3,2,1:T(8,128)(2,1)S(1)}, u32[]{:S(2)}) copy-start(bf16[256,4,5,128]{0,3,2,1:T(8,128)(2,1)S(1)} %get-tuple-element.106) | copy-start | bytes 3932164
  31.8 5.2 %copy-start.9 = (bf16[256,4,5,128]{0,3,2,1:T(8,128)(2,1)}, bf16[256,4,5,128]{0,3,2,1:T(8,128)(2,1)S(1)}, u32[]{:S(2)}) copy-start(bf16[256,4,5,128]{0,3,2,1:T(8,128)(2,1)S(1)} %get-tuple-element.107) | copy-start | bytes 3932164
  38.4 10.6 %collective-permute-start.10 = (bf16[256,2,4,128]{0,3,2,1:T(8,128)(2,1)S(1)}, bf16[256,2,4,128]{0,3,2,1:T(8,128)(2,1)}, u32[]{:S(2)}, u32[]{:S(2)}) collective-permute-start(bf16[256,2,4,128]{0,3,2,1:T(8,128)(2,1)S(1)} %get-tuple-element.194), channel_id=1, source_target_pairs={{0,128},{128,0},{1,129},{129,1},{2,130},{130,2},{3,131},{131,3},{4... | collective-permute-start | bytes 1572872 | tf_op jit(solution)/shard_map/ppermute | solution.py:30
  50.1 12.7 %copy-start.5 = (bf16[256,1,4,128]{0,3,2,1:T(8,128)(2,1)}, bf16[256,1,4,128]{0,3,2,1:T(8,128)(2,1)S(1)}, u32[]{:S(2)}) copy-start(bf16[256,1,4,128]{0,3,2,1:T(8,128)(2,1)S(1)} %get-tuple-element.110) | copy-start | bytes 786436
  50.1 12.7 %copy-start.7 = (bf16[256,1,4,128]{0,3,2,1:T(8,128)(2,1)}, bf16[256,1,4,128]{0,3,2,1:T(8,128)(2,1)S(1)}, u32[]{:S(2)}) copy-start(bf16[256,1,4,128]{0,3,2,1:T(8,128)(2,1)S(1)} %get-tuple-element.111) | copy-start | bytes 786436
  51.1 9.1 %collective-permute-start.11 = (bf16[256,4,1,128]{0,3,2,1:T(8,128)(2,1)}, bf16[256,4,1,128]{0,3,2,1:T(8,128)(2,1)}, u32[]{:S(2)}, u32[]{:S(2)}) collective-permute-start(bf16[256,4,1,128]{0,3,2,1:T(8,128)(2,1)} %get-tuple-element.96), channel_id=1, source_target_pairs={{0,1},{1,2},{2,3},{3,4},{4,5},{5,6},{6,7},{7,8},{8,9},{9,10},{10,1... | collective-permute-start | bytes 786440 | tf_op jit(solution)/shard_map/ppermute | solution.py:34
  54.5 6.6 %collective-permute-start.12 = (bf16[256,4,1,128]{0,3,2,1:T(8,128)(2,1)}, bf16[256,4,1,128]{0,3,2,1:T(8,128)(2,1)}, u32[]{:S(2)}, u32[]{:S(2)}) collective-permute-start(bf16[256,4,1,128]{0,3,2,1:T(8,128)(2,1)} %get-tuple-element.97), channel_id=1, source_target_pairs={{1,0},{2,1},{3,2},{4,3},{5,4},{6,5},{7,6},{8,7},{9,8},{10,9},{11,1... | collective-permute-start | bytes 786440 | tf_op jit(solution)/shard_map/ppermute | solution.py:35
  60.0 10.8 %copy-start.80 = (f32[1,256]{1,0:T(1,128)}, f32[1,256]{1,0:T(1,128)S(1)}, u32[]{:S(2)}) copy-start(f32[1,256]{1,0:T(1,128)S(1)} %get-tuple-element.140) | copy-start | bytes 3076
  60.0 10.8 %copy-start.82 = (f32[1,256]{1,0:T(1,128)}, f32[1,256]{1,0:T(1,128)S(1)}, u32[]{:S(2)}) copy-start(f32[1,256]{1,0:T(1,128)S(1)} %get-tuple-element.141) | copy-start | bytes 3076
  60.1 10.8 %copy-start.84 = (f32[1,256]{1,0:T(1,128)}, f32[1,256]{1,0:T(1,128)S(1)}, u32[]{:S(2)}) copy-start(f32[1,256]{1,0:T(1,128)S(1)} %get-tuple-element.142) | copy-start | bytes 3076
  60.1 10.8 %copy-start.86 = (f32[1,256]{1,0:T(1,128)}, f32[1,256]{1,0:T(1,128)S(1)}, u32[]{:S(2)}) copy-start(f32[1,256]{1,0:T(1,128)S(1)} %get-tuple-element.143) | copy-start | bytes 3076
  60.1 10.8 %copy-start.88 = (f32[1,256]{1,0:T(1,128)}, f32[1,256]{1,0:T(1,128)S(1)}, u32[]{:S(2)}) copy-start(f32[1,256]{1,0:T(1,128)S(1)} %get-tuple-element.144) | copy-start | bytes 3076
  60.1 10.8 %copy-start.90 = (f32[1,256]{1,0:T(1,128)}, f32[1,256]{1,0:T(1,128)S(1)}, u32[]{:S(2)}) copy-start(f32[1,256]{1,0:T(1,128)S(1)} %get-tuple-element.145) | copy-start | bytes 3076
  60.1 10.8 %copy-start.92 = (f32[1,256]{1,0:T(1,128)}, f32[1,256]{1,0:T(1,128)S(1)}, u32[]{:S(2)}) copy-start(f32[1,256]{1,0:T(1,128)S(1)} %get-tuple-element.146) | copy-start | bytes 3076
  60.1 10.8 %copy-start.94 = (f32[1,256]{1,0:T(1,128)}, f32[1,256]{1,0:T(1,128)S(1)}, u32[]{:S(2)}) copy-start(f32[1,256]{1,0:T(1,128)S(1)} %get-tuple-element.147) | copy-start | bytes 3076
  60.1 10.8 %copy-start.96 = (f32[1,256]{1,0:T(1,128)}, f32[1,256]{1,0:T(1,128)S(1)}, u32[]{:S(2)}) copy-start(f32[1,256]{1,0:T(1,128)S(1)} %get-tuple-element.148) | copy-start | bytes 3076
  60.1 10.8 %copy-start.98 = (f32[1,256]{1,0:T(1,128)}, f32[1,256]{1,0:T(1,128)S(1)}, u32[]{:S(2)}) copy-start(f32[1,256]{1,0:T(1,128)S(1)} %get-tuple-element.149) | copy-start | bytes 3076
  60.2 10.8 %copy-start.100 = (f32[1,256]{1,0:T(1,128)}, f32[1,256]{1,0:T(1,128)S(1)}, u32[]{:S(2)}) copy-start(f32[1,256]{1,0:T(1,128)S(1)} %get-tuple-element.150) | copy-start | bytes 3076
  60.2 10.8 %copy-start.102 = (f32[1,256]{1,0:T(1,128)}, f32[1,256]{1,0:T(1,128)S(1)}, u32[]{:S(2)}) copy-start(f32[1,256]{1,0:T(1,128)S(1)} %get-tuple-element.151) | copy-start | bytes 3076
  60.2 10.8 %copy-start.104 = (f32[1,256]{1,0:T(1,128)}, f32[1,256]{1,0:T(1,128)S(1)}, u32[]{:S(2)}) copy-start(f32[1,256]{1,0:T(1,128)S(1)} %get-tuple-element.152) | copy-start | bytes 3076
  60.2 10.8 %copy-start.106 = (f32[1,256]{1,0:T(1,128)}, f32[1,256]{1,0:T(1,128)S(1)}, u32[]{:S(2)}) copy-start(f32[1,256]{1,0:T(1,128)S(1)} %get-tuple-element.153) | copy-start | bytes 3076
  60.2 10.8 %copy-start.108 = (f32[1,256]{1,0:T(1,128)}, f32[1,256]{1,0:T(1,128)S(1)}, u32[]{:S(2)}) copy-start(f32[1,256]{1,0:T(1,128)S(1)} %get-tuple-element.154) | copy-start | bytes 3076
  60.2 10.8 %copy-start.110 = (f32[1,256]{1,0:T(1,128)}, f32[1,256]{1,0:T(1,128)S(1)}, u32[]{:S(2)}) copy-start(f32[1,256]{1,0:T(1,128)S(1)} %get-tuple-element.155) | copy-start | bytes 3076
  60.2 10.8 %copy-start.112 = (f32[1,256]{1,0:T(1,128)}, f32[1,256]{1,0:T(1,128)S(1)}, u32[]{:S(2)}) copy-start(f32[1,256]{1,0:T(1,128)S(1)} %get-tuple-element.156) | copy-start | bytes 3076
  60.2 10.8 %copy-start.114 = (f32[1,256]{1,0:T(1,128)}, f32[1,256]{1,0:T(1,128)S(1)}, u32[]{:S(2)}) copy-start(f32[1,256]{1,0:T(1,128)S(1)} %get-tuple-element.157) | copy-start | bytes 3076
  64.2 5.4 %copy-start.6 = (bf16[256,1,4,128]{0,3,2,1:T(8,128)(2,1)S(1)}, bf16[256,1,4,128]{0,3,2,1:T(8,128)(2,1)}, u32[]{:S(2)}) copy-start(bf16[256,1,4,128]{0,3,2,1:T(8,128)(2,1)} %copy-done.5) | copy-start | bytes 786436
  64.2 5.4 %copy-start.8 = (bf16[256,1,4,128]{0,3,2,1:T(8,128)(2,1)S(1)}, bf16[256,1,4,128]{0,3,2,1:T(8,128)(2,1)}, u32[]{:S(2)}) copy-start(bf16[256,1,4,128]{0,3,2,1:T(8,128)(2,1)} %copy-done.7) | copy-start | bytes 786436
  66.8 4.3 %copy-start.70 = (f32[1,256]{1,0:T(1,128)S(1)}, f32[1,256]{1,0:T(1,128)}, u32[]{:S(2)}) copy-start(f32[1,256]{1,0:T(1,128)} %get-tuple-element.162) | copy-start | bytes 3076
  66.8 4.3 %copy-start.72 = (f32[1,256]{1,0:T(1,128)S(1)}, f32[1,256]{1,0:T(1,128)}, u32[]{:S(2)}) copy-start(f32[1,256]{1,0:T(1,128)} %get-tuple-element.163) | copy-start | bytes 3076
  66.8 4.3 %copy-start.74 = (f32[1,256]{1,0:T(1,128)S(1)}, f32[1,256]{1,0:T(1,128)}, u32[]{:S(2)}) copy-start(f32[1,256]{1,0:T(1,128)} %get-tuple-element.164) | copy-start | bytes 3076
  66.8 4.3 %copy-start.76 = (f32[1,256]{1,0:T(1,128)S(1)}, f32[1,256]{1,0:T(1,128)}, u32[]{:S(2)}) copy-start(f32[1,256]{1,0:T(1,128)} %get-tuple-element.165) | copy-start | bytes 3076
  66.8 16.4 %collective-permute-start.1 = (bf16[256,2,4,128]{0,3,2,1:T(8,128)(2,1)S(1)}, bf16[256,2,4,128]{0,3,2,1:T(8,128)(2,1)}, u32[]{:S(2)}, u32[]{:S(2)}) collective-permute-start(bf16[256,2,4,128]{0,3,2,1:T(8,128)(2,1)S(1)} %get-tuple-element.196), channel_id=1, source_target_pairs={{0,128},{128,0},{1,129},{129,1},{2,130},{130,2},{3,131},{131,3},{4... | collective-permute-start | bytes 1572872 | tf_op jit(solution)/shard_map/ppermute | solution.py:30
  84.4 10.7 %collective-permute-start.2 = (bf16[256,4,1,128]{0,3,2,1:T(8,128)(2,1)S(1)}, bf16[256,4,1,128]{0,3,2,1:T(8,128)(2,1)S(1)}, u32[]{:S(2)}, u32[]{:S(2)}) collective-permute-start(bf16[256,4,1,128]{0,3,2,1:T(8,128)(2,1)S(1)} %get-tuple-element.104), channel_id=1, source_target_pairs={{0,1},{1,2},{2,3},{3,4},{4,5},{5,6},{6,7},{7,8},{8,9},{9,10},{10,1... | collective-permute-start | bytes 786440 | tf_op jit(solution)/shard_map/ppermute | solution.py:34
  84.5 11.1 %collective-permute-start.3 = (bf16[256,4,1,128]{0,3,2,1:T(8,128)(2,1)S(1)}, bf16[256,4,1,128]{0,3,2,1:T(8,128)(2,1)S(1)}, u32[]{:S(2)}, u32[]{:S(2)}) collective-permute-start(bf16[256,4,1,128]{0,3,2,1:T(8,128)(2,1)S(1)} %get-tuple-element.105), channel_id=1, source_target_pairs={{1,0},{2,1},{3,2},{4,3},{5,4},{6,5},{7,6},{8,7},{9,8},{10,9},{11,1... | collective-permute-start | bytes 786440 | tf_op jit(solution)/shard_map/ppermute | solution.py:35
  98.1 4.8 %copy-start.19 = (bf16[128,256]{1,0:T(8,128)(2,1)S(1)}, bf16[128,256]{1,0:T(8,128)(2,1)}, u32[]{:S(2)}) copy-start(bf16[128,256]{1,0:T(8,128)(2,1)} %slice.924) | copy-start | bytes 196612
  98.1 4.8 %copy-start.21 = (bf16[128,256]{1,0:T(8,128)(2,1)S(1)}, bf16[128,256]{1,0:T(8,128)(2,1)}, u32[]{:S(2)}) copy-start(bf16[128,256]{1,0:T(8,128)(2,1)} %slice.926) | copy-start | bytes 196612
  102.9 4.7 %copy-start.4 = (bf16[256,1,4,128]{0,3,2,1:T(8,128)(2,1)S(1)}, bf16[256,1,4,128]{0,3,2,1:T(8,128)(2,1)}, u32[]{:S(2)}) copy-start(bf16[256,1,4,128]{0,3,2,1:T(8,128)(2,1)} %copy-done.3) | copy-start | bytes 786436
  111.1 46.4 %collective-permute-start.7 = (bf16[256,2,4,128]{0,3,2,1:T(8,128)(2,1)S(1)}, bf16[256,2,4,128]{0,3,2,1:T(8,128)(2,1)S(1)}, u32[]{:S(2)}, u32[]{:S(2)}) collective-permute-start(bf16[256,2,4,128]{0,3,2,1:T(8,128)(2,1)S(1)} %get-tuple-element.197), channel_id=1, source_target_pairs={{0,128},{128,0},{1,129},{129,1},{2,130},{130,2},{3,131},{131,3},{4... | collective-permute-start | bytes 1572872 | tf_op jit(solution)/shard_map/ppermute | solution.py:30
  157.7 8.4 %collective-permute-start.8 = (bf16[256,4,1,128]{0,3,2,1:T(8,128)(2,1)S(1)}, bf16[256,4,1,128]{0,3,2,1:T(8,128)(2,1)S(1)}, u32[]{:S(2)}, u32[]{:S(2)}) collective-permute-start(bf16[256,4,1,128]{0,3,2,1:T(8,128)(2,1)S(1)} %get-tuple-element.100), channel_id=1, source_target_pairs={{0,1},{1,2},{2,3},{3,4},{4,5},{5,6},{6,7},{7,8},{8,9},{9,10},{10,1... | collective-permute-start | bytes 786440 | tf_op jit(solution)/shard_map/ppermute | solution.py:34
  159.9 6.1 %collective-permute-start.9 = (bf16[256,4,1,128]{0,3,2,1:T(8,128)(2,1)S(1)}, bf16[256,4,1,128]{0,3,2,1:T(8,128)(2,1)S(1)}, u32[]{:S(2)}, u32[]{:S(2)}) collective-permute-start(bf16[256,4,1,128]{0,3,2,1:T(8,128)(2,1)S(1)} %get-tuple-element.101), channel_id=1, source_target_pairs={{1,0},{2,1},{3,2},{4,3},{5,4},{6,5},{7,6},{8,7},{9,8},{10,9},{11,1... | collective-permute-start | bytes 786440 | tf_op jit(solution)/shard_map/ppermute | solution.py:35
  (65 other events, 106.5 us)

commit v3 on v2

--- a/solution.py
+++ b/solution.py
@@ -77,7 +77,7 @@
     for k, a, b, d in TAP_LIST:
         shifted = wide[:, 1 + a : 1 + a + extent_x, 1 + b : 1 + b + extent_y, 1 + d : 1 + d + extent_z]
         columns.append(jnp.sum(shifted.astype(jnp.float32) * grad_float, axis=(1, 2, 3)))
-    return jnp.stack(columns, axis=0)
+    return columns
 
 
 def pointwise(weights, source):
@@ -295,9 +295,9 @@
         for p in parts[:2]:
             rows = p.shape[0] // 2
             pieces.append(p[h * rows : (h + 1) * rows].reshape(-1))
-        for p in parts[2:]:
-            cols = p.shape[1] // 2
-            pieces.append(p[:, h * cols : (h + 1) * cols].reshape(-1))
+        for columns in parts[2:]:
+            cols = columns[0].shape[0] // 2
+            pieces.extend(column[h * cols : (h + 1) * cols] for column in columns)
         halves.append(jnp.concatenate(pieces))
     real = halves[0].shape[0]
     tiles = -(-real // (TILE * blocks)) * blocks
@@ -313,8 +313,8 @@
         shape = (p.shape[0] // 2, p.shape[1])
         out.append(flat[offset : offset + shape[0] * shape[1]].reshape(shape))
         offset += shape[0] * shape[1]
-    for p in parts[2:]:
-        shape = (p.shape[0], p.shape[1] // 2)
+    for columns in parts[2:]:
+        shape = (len(columns), columns[0].shape[0] // 2)
         out.append(flat[offset : offset + shape[0] * shape[1]].reshape(shape))
         offset += shape[0] * shape[1]
     return out
@@ -347,8 +347,8 @@
     grad_scale = 1.0 / math.sqrt(float(total_cells))
     local_pw_one = contract_cells(first, grad_pre) * grad_scale
     local_pw_two = contract_cells(second, cotangent) * grad_scale
-    local_dw_one = tap_sums(wide_input, grad_first) * grad_scale
-    local_dw_two = tap_sums(act_padded, grad_second) * grad_scale
+    local_dw_one = [column * grad_scale for column in tap_sums(wide_input, grad_first)]
+    local_dw_two = [column * grad_scale for column in tap_sums(act_padded, grad_second)]
     partials = (local_pw_one, local_pw_two, local_dw_one, local_dw_two)
     scatter, _ = reduce_plan(lax.axis_size("space"))
     blocks = math.prod(f[2] for group in scatter for f in group if f[0] != "own")

time: 177 us -> 153 us (0.86); the launches traced: 174 us -> 153 us
  local copies, waits for them, and re-layouts: 27.2 us -> 11.8 us
  other arithmetic: 31.3 us -> 23.7 us
  starting transfers between devices: 29 us -> 36.3 us
  Pallas kernels: 43.2 us -> 36.4 us
  waiting for transfers between devices: 26.9 us -> 31.7 us
  matrix products: 13.6 us -> 10.9 us
    ppermute x4, waiting for transfers between devices: 15.6 us -> 29.8 us  [extended(): theirs = lax.ppermute(jnp.concatenate([first, last], axis=dim), axis, up)]
    ppermute x4, starting transfers between devices: 11.8 us -> 20.2 us  [extended(): after = lax.ppermute(first, axis, down)]
    pallas_call x1, Pallas kernels: 43.2 us -> 36.4 us  [tree_reduce(): pl.pallas_call(functools.partial(reduce_kernel, plan), out_shape=jax.Shap...]
    ppermute x4, waiting for transfers between devices: 6.45 us -> 1.61 us  [extended(): before = lax.ppermute(last, axis, up)]
    slice x6, local copies, waits for them, and re-layouts: 4.94 us -> 0.14 us  [gather_weights(): parts = [h[offset:offset + count].reshape(w.shape) for h in (low, high)]]
    unnamed x243 -> x74, local copies, waits for them, and re-layouts: 10.1 us -> 5.4 us
    dot_general x2, matrix products: 6.82 us -> 2.26 us  [backmap(): jnp.dot(weights, flattened, preferred_element_type=jnp.float32)]
    convert_element_type x1, other arithmetic: 4.79 us -> 0.28 us  [shards(): act = jax.nn.silu(pre).astype(jnp.bfloat16)]
  transfers between devices with their start and end apart: 13 -> 13, of which waited for: 9 -> 6; matrix products, arithmetic and copies ran while one was open for 17% -> 15% of each run, Pallas kernels for 25% -> 0%
where the time goes in v3:
time: 153 us
  Pallas kernels  36.4 us (24%)
  starting transfers between devices  36.3 us (24%)
  waiting for transfers between devices  31.7 us (21%)
  other arithmetic  23.7 us (15%)
  local copies, waits for them, and re-layouts  11.8 us (8%)
  matrix products  10.9 us (7%)
  between operations  1.96 us (1%)
    pallas_call x1, Pallas kernels, tree_reduce(): pl.pallas_call(functools.partial(reduce_kernel, plan), out_shape=jax.Shap...  36.4 us
    ppermute x4, waiting for transfers between devices, extended(): theirs = lax.ppermute(jnp.concatenate([first, last], axis=dim), axis, up)  29.8 us
    ppermute x4, starting transfers between devices, extended(): after = lax.ppermute(first, axis, down)  20.2 us
    ppermute x4, starting transfers between devices, extended(): theirs = lax.ppermute(jnp.concatenate([first, last], axis=dim), axis, up)  7.22 us
    reduce_sum x3, other arithmetic, tap_sums(): jnp.sum(shifted.astype(jnp.float32) * grad_float, axis=(1, 2, 3))  6.46 us
    unnamed x74, local copies, waits for them, and re-layouts  5.4 us
    ppermute x4, starting transfers between devices, extended(): before = lax.ppermute(last, axis, up)  5.03 us
    convert_element_type x1, other arithmetic, shards(): grad_input = (cotangent.astype(jnp.float32) + depthwise(first_padded, tap...  4.83 us
  transfers between devices with their start and end apart: 13, of which 6 were waited for; matrix products, arithmetic and copies ran while one was open for 15% of the time, Pallas kernels for 0%

profile of v3, /device:TPU:1, one launch (start us, length us, event | category | flops | bytes accessed | tf_op | source)
XLA Modules:
  0.0 152.8 jit_solution(18075997525364312332)
XLA Ops:
  0.6 0.9 copy.31
  1.6 0.9 copy.30
  2.5 0.7 pad_maximum_fusion.58
  3.2 3.8 %collective-permute-start = (bf16[72448]{0:T(1024)(128)(2,1)S(1)}, bf16[72448]{0:T(1024)(128)(2,1)}, u32[]{:S(2)}, u32[]{:S(2)}) collective-permute-start(bf16[72448]{0:T(1024)(128)(2,1)S(1)} %pad_maximum_fusion.58), channel_id=1, source_target_pairs={{0,128},{128,0},{1,129},{129,1},{2,130},{130,2},{3,131},{131,3},{4... | collective-permute-start | bytes 434696 | tf_op jit(solution)/shard_map/ppermute | solution.py:42
  7.1 1.3 copy.13
  8.4 0.1 collective-permute-start.4
  8.5 0.4 reshape.527
  8.9 0.3 copy.11
  9.2 0.2 copy.12
  9.4 0.2 collective-permute-done
  9.7 1.0 broadcast_select_fusion.1
  10.8 0.3 convolution_convert_fusion.1
  11.1 3.8 %collective-permute-start.1 = (bf16[256,2,4,128]{0,3,2,1:T(8,128)(2,1)S(1)}, bf16[256,2,4,128]{0,3,2,1:T(8,128)(2,1)S(1)}, u32[]{:S(2)}, u32[]{:S(2)}) collective-permute-start(bf16[256,2,4,128]{0,3,2,1:T(8,128)(2,1)S(1)} %convolution_convert_fusion.1), channel_id=1, source_target_pairs={{0,128},{128,0},{1,129},{129,1},{2,130},{130,2},{3,131},{131,3},{4... | collective-permute-start | bytes 1572872 | tf_op jit(solution)/shard_map/ppermute | solution.py:30
  15.0 7.6 %collective-permute-done.4 = bf16[256,2,4,128]{0,3,2,1:T(8,128)(2,1)S(1)} collective-permute-done((bf16[256,2,4,128]{0,3,2,1:T(8,128)(2,1)S(1)}, bf16[256,2,4,128]{0,3,2,1:T(8,128)(2,1)S(1)}, u32[]{:S(2)}, u32[]{:S(2)}) %collective-permute-start.4) | collective-permute-done | bytes 524320 | tf_op jit(solution)/shard_map/ppermute | solution.py:30
  22.7 0.1 pad_maximum_fusion.54
  22.7 3.5 %collective-permute-start.5 = (bf16[256,4,1,128]{0,3,2,1:T(8,128)(2,1)S(1)}, bf16[256,4,1,128]{0,3,2,1:T(8,128)(2,1)S(1)}, u32[]{:S(2)}, u32[]{:S(2)}) collective-permute-start(bf16[256,4,1,128]{0,3,2,1:T(8,128)(2,1)S(1)} %get-tuple-element.108), channel_id=1, source_target_pairs={{0,1},{1,2},{2,3},{3,4},{4,5},{5,6},{6,7},{7,8},{8,9},{9,10},{10,1... | collective-permute-start | bytes 786440 | tf_op jit(solution)/shard_map/ppermute | solution.py:34
  26.3 10.4 %collective-permute-done.1 = bf16[256,2,4,128]{0,3,2,1:T(8,128)(2,1)S(1)} collective-permute-done((bf16[256,2,4,128]{0,3,2,1:T(8,128)(2,1)S(1)}, bf16[256,2,4,128]{0,3,2,1:T(8,128)(2,1)S(1)}, u32[]{:S(2)}, u32[]{:S(2)}) %collective-permute-start.1) | collective-permute-done | bytes 524320 | tf_op jit(solution)/shard_map/ppermute | solution.py:30
  36.7 0.1 pad_maximum_fusion.57
  36.8 3.3 %collective-permute-start.3 = (bf16[256,4,1,128]{0,3,2,1:T(8,128)(2,1)S(1)}, bf16[256,4,1,128]{0,3,2,1:T(8,128)(2,1)S(1)}, u32[]{:S(2)}, u32[]{:S(2)}) collective-permute-start(bf16[256,4,1,128]{0,3,2,1:T(8,128)(2,1)S(1)} %get-tuple-element.105), channel_id=1, source_target_pairs={{1,0},{2,1},{3,2},{4,3},{5,4},{6,5},{7,6},{8,7},{9,8},{10,9},{11,1... | collective-permute-start | bytes 786440 | tf_op jit(solution)/shard_map/ppermute | solution.py:35
  40.0 0.2 maximum_maximum_fusion.1
  40.3 0.7 fusion.5
  41.0 0.3 fusion.4
  41.3 4.3 %fusion.36 = bf16[256,2,4,128]{0,3,2,1:T(8,128)(2,1)S(1)} fusion(bf16[256,2,4,128]{0,3,2,1:T(8,128)(2,1)S(1)} %copy.13, f32[256]{0:T(256)S(1)} %bitcast.163, f32[256]{0:T(256)S(1)} %bitcast.165, f32[256]{0:T(256)S(1)} %bitcast.161, f32[256]{0:T(256)S(1)} %bitcast.159, f32[256]{0:T(256)S(1)} %bitcast.157, f32[256]{0:T(256)S(1)} %bitcast.155, ...), kind=kLoop, calls=%fused_computation.190 | loop fusion | flops 21757952 | bytes 14183424 | tf_op jit(solution)/shard_map/convert_element_type | solution.py:329
  45.7 0.5 collective-permute-done.2
  46.2 0.7 fusion.6
  46.9 0.2 pad_maximum_fusion.32
  47.1 0.3 fusion.7
  47.4 3.9 %fusion.149 = (bf16[256,2,4,128]{0,3,2,1:T(8,128)(2,1)S(1)}, f32[256,2,4,128]{0,3,2,1:T(8,128)S(1)}) fusion(bf16[256,2,4,128]{0,3,2,1:T(8,128)(2,1)S(1)} %convolution_convert_fusion.1, bf16[256,4,6,129]{0,3,2,1:T(8,128)(2,1)S(1)} %fusion.6, bf16[256,4,5,128]{0,3,2,1:T(8,128)(2,1)S(1)} %get-tuple-element.103, bf16[256,4,6,129]{0,3,2,1:T(8,128)(2,1)S(1)} %fusion.7, ...), kind=kOutput, calls=%fused_computation.305 | convolution fusion | flops 158334976 | bytes 15887360 | tf_op jit(solution)/shard_map/dot_general | solution.py:86
  51.3 1.9 %fusion.146 = (f32[256]{0:T(256)S(1)}, f32[256]{0:T(256)S(1)}, f32[256]{0:T(256)S(1)}, f32[256]{0:T(256)S(1)}, f32[256]{0:T(256)S(1)}, /*index=5*/f32[256]{0:T(2...) fusion(bf16[256,4,5,128]{0,3,2,1:T(8,128)(2,1)S(1)} %get-tuple-, ...), kind=kOutput, calls=%fused_computation.300 | convolution fusion | flops 144438272 | bytes 7483392 | tf_op jit(solution)/shard_map/dot_general | solution.py:92
  53.3 0.3 fusion.9
  53.6 3.0 %collective-permute-start.7 = (bf16[256,2,4,128]{0,3,2,1:T(8,128)(2,1)S(1)}, bf16[256,2,4,128]{0,3,2,1:T(8,128)(2,1)S(1)}, u32[]{:S(2)}, u32[]{:S(2)}) collective-permute-start(bf16[256,2,4,128]{0,3,2,1:T(8,128)(2,1)S(1)} %get-tuple-element.300), channel_id=1, source_target_pairs={{0,128},{128,0},{1,129},{129,1},{2,130},{130,2},{3,131},{131,3},{4... | collective-permute-start | bytes 1572872 | tf_op jit(solution)/shard_map/ppermute | solution.py:30
  56.6 2.6 %fusion.147 = (f32[256]{0:T(256)S(1)}, f32[256]{0:T(256)S(1)}, f32[256]{0:T(256)S(1)}, f32[256]{0:T(256)S(1)}, f32[256]{0:T(256)S(1)}, /*index=5*/f32[256]{0:T(2...) fusion(bf16[256,2,4,128]{0,3,2,1:T(8,128)(2,1)S(1)} %get-tuple-, ...), kind=kLoop, calls=%fused_computation.301 | loop fusion | flops 12579072 | bytes 7879680 | tf_op jit(solution)/shard_map/reduce_sum | solution.py:79
  59.2 0.1 copy.32
  59.3 0.3 multiply_convert_fusion
  59.6 0.4 collective-permute-start.10
  60.0 0.1 copy.34
  60.3 11.8 %collective-permute-done.10 = bf16[256,2,4,128]{0,3,2,1:T(8,128)(2,1)S(1)} collective-permute-done((bf16[256,2,4,128]{0,3,2,1:T(8,128)(2,1)S(1)}, bf16[256,2,4,128]{0,3,2,1:T(8,128)(2,1)S(1)}, u32[]{:S(2)}, u32[]{:S(2)}) %collective-permute-start.10) | collective-permute-done | bytes 524320 | tf_op jit(solution)/shard_map/ppermute | solution.py:30
  72.2 0.1 pad_maximum_fusion.48
  72.3 9.3 %collective-permute-start.12 = (bf16[256,4,1,128]{0,3,2,1:T(8,128)(2,1)S(1)}, bf16[256,4,1,128]{0,3,2,1:T(8,128)(2,1)S(1)}, u32[]{:S(2)}, u32[]{:S(2)}) collective-permute-start(bf16[256,4,1,128]{0,3,2,1:T(8,128)(2,1)S(1)} %get-tuple-element.97), channel_id=1, source_target_pairs={{1,0},{2,1},{3,2},{4,3},{5,4},{6,5},{7,6},{8,7},{9,8},{10,9},{11,1... | collective-permute-start | bytes 786440 | tf_op jit(solution)/shard_map/ppermute | solution.py:35
  81.5 1.5 collective-permute-start.11
  83.2 7.7 %collective-permute-start.9 = (bf16[256,4,1,128]{0,3,2,1:T(8,128)(2,1)S(1)}, bf16[256,4,1,128]{0,3,2,1:T(8,128)(2,1)S(1)}, u32[]{:S(2)}, u32[]{:S(2)}) collective-permute-start(bf16[256,4,1,128]{0,3,2,1:T(8,128)(2,1)S(1)} %get-tuple-element.101), channel_id=1, source_target_pairs={{1,0},{2,1},{3,2},{4,3},{5,4},{6,5},{7,6},{8,7},{9,8},{10,9},{11,1... | collective-permute-start | bytes 786440 | tf_op jit(solution)/shard_map/ppermute | solution.py:35
  90.8 1.1 collective-permute-done.11
  92.0 0.3 fusion
  92.3 0.2 maximum_maximum_fusion.3
  92.5 2.6 %fusion.105 = (f32[256]{0:T(256)S(1)}, f32[256]{0:T(256)S(1)}, f32[256]{0:T(256)S(1)}, f32[256]{0:T(256)S(1)}, f32[256]{0:T(256)S(1)}, /*index=5*/f32[256]{0:T(2...) fusion(bf16[256,2,4,128]{0,3,2,1:T(8,128)(2,1)S(1)} %convolutio, ...), kind=kLoop, calls=%fused_computation.259 | loop fusion | flops 12579072 | bytes 7879680 | tf_op jit(solution)/shard_map/reduce_sum | solution.py:79
  95.1 0.7 fusion.1
  95.8 4.4 %fusion.8 = f32[256,256]{1,0:T(8,128)S(1)} fusion(bf16[256,2,4,128]{0,3,2,1:T(8,128)(2,1)S(1)} %copy.11, bf16[256,2,4,128]{0,3,2,1:T(8,128)(2,1)S(1)} %multiply_convert_fusion, f32[256]{0:T(256)S(1)} %bitcast.218, f32[256]{0:T(256)S(1)} %bitcast.220, f32[256]{0:T(256)S(1)} %bitcast.216, f32[256]{0:T(256)S(1)} %bitcast.214, f32[256]{0:T(256)S(1)} %bitcast.212, ...), kind=kOutput, calls=%fused_computation.161 | convolution fusion | flops 156041216 | bytes 14445568 | tf_op jit(solution)/shard_map/dot_general | solution.py:97
  100.3 1.3 fusion.104
  101.6 0.7 fusion.2
  102.3 0.2 pad_maximum_fusion.34
  102.6 0.3 fusion.3
  102.9 4.8 %fusion.148 = bf16[256,2,4,128]{0,3,2,1:T(8,128)(2,1)S(1)} fusion(bf16[256,2,4,128]{0,3,2,1:T(8,128)(2,1)S(1)} %get-tuple-element.300, bf16[256,2,4,128]{0,3,2,1:T(8,128)(2,1)S(1)} %copy.11, bf16[256,4,6,129]{0,3,2,1:T(8,128)(2,1)S(1)} %fusion.2, bf16[256,4,5,128]{0,3,2,1:T(8,128)(2,1)S(1)} %get-tuple-element.99, bf16[256,4,6,129]{0,3,2,1:T(8,128)(2,1)S(1)} %fusion.3, ...), kind=kLoop, calls=%fused_computation.304 | loop fusion | flops 22282240 | bytes 14707712 | tf_op jit(solution)/shard_map/convert_element_type | solution.py:345
  107.8 1.1 copy.22
  108.9 0.1 copy.33
  108.9 0.1 copy.35
  110.2 0.2 stack.10
  110.4 0.2 stack.9
  110.6 0.5 select_maximum_fusion
  111.2 1.4 reshape.534.x_ref
  112.6 36.4 %shard_map.101 = f32[80,8,128]{2,1,0:T(8,128)} custom-call(f32[160,8,128]{2,1,0:T(8,128)} %reshape.534.x_ref), custom_call_target="tpu_custom_call" | custom-call | bytes 41943040 | tf_op jit(solution)/shard_map/pallas_call | solution.py:278
  149.1 1.0 fusion.295
  150.0 0.7 reshape.535
  150.7 0.7 reshape.536
  151.4 1.4 fusion.294
  (147 shorter events, 1.2 us)
Async XLA Ops:
  0.6 7.9 %copy-start = (bf16[256,2,4,128]{3,2,1,0:T(4,128)(2,1)S(1)}, bf16[256,2,4,128]{3,2,1,0:T(4,128)(2,1)}, u32[]{:S(2)}) copy-start(bf16[256,2,4,128]{3,2,1,0:T(4,128)(2,1)} %param.7) | copy-start | bytes 1572868
  3.2 6.4 %collective-permute-start = (bf16[72448]{0:T(1024)(128)(2,1)S(1)}, bf16[72448]{0:T(1024)(128)(2,1)}, u32[]{:S(2)}, u32[]{:S(2)}) collective-permute-start(bf16[72448]{0:T(1024)(128)(2,1)S(1)} %pad_maximum_fusion.58), channel_id=1, source_target_pairs={{0,128},{128,0},{1,129},{129,1},{2,130},{130,2},{3,131},{131,3},{4... | collective-permute-start | bytes 434696 | tf_op jit(solution)/shard_map/ppermute | solution.py:42
  8.4 1.3 copy-start.1
  8.4 1.3 copy-start.2
  8.4 14.2 %collective-permute-start.4 = (bf16[256,2,4,128]{0,3,2,1:T(8,128)(2,1)S(1)}, bf16[256,2,4,128]{0,3,2,1:T(8,128)(2,1)S(1)}, u32[]{:S(2)}, u32[]{:S(2)}) collective-permute-start(bf16[256,2,4,128]{0,3,2,1:T(8,128)(2,1)S(1)} %copy.13), channel_id=1, source_target_pairs={{0,128},{128,0},{1,129},{129,1},{2,130},{130,2},{3,131},{131,3},{4... | collective-permute-start | bytes 1572872 | tf_op jit(solution)/shard_map/ppermute | solution.py:30
  11.1 25.6 %collective-permute-start.1 = (bf16[256,2,4,128]{0,3,2,1:T(8,128)(2,1)S(1)}, bf16[256,2,4,128]{0,3,2,1:T(8,128)(2,1)S(1)}, u32[]{:S(2)}, u32[]{:S(2)}) collective-permute-start(bf16[256,2,4,128]{0,3,2,1:T(8,128)(2,1)S(1)} %convolution_convert_fusion.1), channel_id=1, source_target_pairs={{0,128},{128,0},{1,129},{129,1},{2,130},{130,2},{3,131},{131,3},{4... | collective-permute-start | bytes 1572872 | tf_op jit(solution)/shard_map/ppermute | solution.py:30
  22.7 17.3 %collective-permute-start.5 = (bf16[256,4,1,128]{0,3,2,1:T(8,128)(2,1)S(1)}, bf16[256,4,1,128]{0,3,2,1:T(8,128)(2,1)S(1)}, u32[]{:S(2)}, u32[]{:S(2)}) collective-permute-start(bf16[256,4,1,128]{0,3,2,1:T(8,128)(2,1)S(1)} %get-tuple-element.108), channel_id=1, source_target_pairs={{0,1},{1,2},{2,3},{3,4},{4,5},{5,6},{6,7},{7,8},{8,9},{9,10},{10,1... | collective-permute-start | bytes 786440 | tf_op jit(solution)/shard_map/ppermute | solution.py:34
  26.3 13.8 %collective-permute-start.6 = (bf16[256,4,1,128]{0,3,2,1:T(8,128)(2,1)S(1)}, bf16[256,4,1,128]{0,3,2,1:T(8,128)(2,1)S(1)}, u32[]{:S(2)}, u32[]{:S(2)}) collective-permute-start(bf16[256,4,1,128]{0,3,2,1:T(8,128)(2,1)S(1)} %get-tuple-element.109), channel_id=1, source_target_pairs={{1,0},{2,1},{3,2},{4,3},{5,4},{6,5},{7,6},{8,7},{9,8},{10,9},{11,1... | collective-permute-start | bytes 786440 | tf_op jit(solution)/shard_map/ppermute | solution.py:35
  36.8 8.9 %collective-permute-start.3 = (bf16[256,4,1,128]{0,3,2,1:T(8,128)(2,1)S(1)}, bf16[256,4,1,128]{0,3,2,1:T(8,128)(2,1)S(1)}, u32[]{:S(2)}, u32[]{:S(2)}) collective-permute-start(bf16[256,4,1,128]{0,3,2,1:T(8,128)(2,1)S(1)} %get-tuple-element.105), channel_id=1, source_target_pairs={{1,0},{2,1},{3,2},{4,3},{5,4},{6,5},{7,6},{8,7},{9,8},{10,9},{11,1... | collective-permute-start | bytes 786440 | tf_op jit(solution)/shard_map/ppermute | solution.py:35
  40.0 6.1 %collective-permute-start.2 = (bf16[256,4,1,128]{0,3,2,1:T(8,128)(2,1)S(1)}, bf16[256,4,1,128]{0,3,2,1:T(8,128)(2,1)S(1)}, u32[]{:S(2)}, u32[]{:S(2)}) collective-permute-start(bf16[256,4,1,128]{0,3,2,1:T(8,128)(2,1)S(1)} %get-tuple-element.104), channel_id=1, source_target_pairs={{0,1},{1,2},{2,3},{3,4},{4,5},{5,6},{6,7},{7,8},{8,9},{9,10},{10,1... | collective-permute-start | bytes 786440 | tf_op jit(solution)/shard_map/ppermute | solution.py:34
  53.6 29.4 %collective-permute-start.7 = (bf16[256,2,4,128]{0,3,2,1:T(8,128)(2,1)S(1)}, bf16[256,2,4,128]{0,3,2,1:T(8,128)(2,1)S(1)}, u32[]{:S(2)}, u32[]{:S(2)}) collective-permute-start(bf16[256,2,4,128]{0,3,2,1:T(8,128)(2,1)S(1)} %get-tuple-element.300), channel_id=1, source_target_pairs={{0,128},{128,0},{1,129},{129,1},{2,130},{130,2},{3,131},{131,3},{4... | collective-permute-start | bytes 1572872 | tf_op jit(solution)/shard_map/ppermute | solution.py:30
  59.6 12.6 %collective-permute-start.10 = (bf16[256,2,4,128]{0,3,2,1:T(8,128)(2,1)S(1)}, bf16[256,2,4,128]{0,3,2,1:T(8,128)(2,1)S(1)}, u32[]{:S(2)}, u32[]{:S(2)}) collective-permute-start(bf16[256,2,4,128]{0,3,2,1:T(8,128)(2,1)S(1)} %multiply_convert_fusion), channel_id=1, source_target_pairs={{0,128},{128,0},{1,129},{129,1},{2,130},{130,2},{3,131},{131,3},{4... | collective-permute-start | bytes 1572872 | tf_op jit(solution)/shard_map/ppermute | solution.py:30
  72.3 18.6 %collective-permute-start.12 = (bf16[256,4,1,128]{0,3,2,1:T(8,128)(2,1)S(1)}, bf16[256,4,1,128]{0,3,2,1:T(8,128)(2,1)S(1)}, u32[]{:S(2)}, u32[]{:S(2)}) collective-permute-start(bf16[256,4,1,128]{0,3,2,1:T(8,128)(2,1)S(1)} %get-tuple-element.97), channel_id=1, source_target_pairs={{1,0},{2,1},{3,2},{4,3},{5,4},{6,5},{7,6},{8,7},{9,8},{10,9},{11,1... | collective-permute-start | bytes 786440 | tf_op jit(solution)/shard_map/ppermute | solution.py:35
  81.5 10.4 %collective-permute-start.11 = (bf16[256,4,1,128]{0,3,2,1:T(8,128)(2,1)S(1)}, bf16[256,4,1,128]{0,3,2,1:T(8,128)(2,1)S(1)}, u32[]{:S(2)}, u32[]{:S(2)}) collective-permute-start(bf16[256,4,1,128]{0,3,2,1:T(8,128)(2,1)S(1)} %get-tuple-element.96), channel_id=1, source_target_pairs={{0,1},{1,2},{2,3},{3,4},{4,5},{5,6},{6,7},{7,8},{8,9},{9,10},{10,1... | collective-permute-start | bytes 786440 | tf_op jit(solution)/shard_map/ppermute | solution.py:34
  83.2 18.5 %collective-permute-start.9 = (bf16[256,4,1,128]{0,3,2,1:T(8,128)(2,1)S(1)}, bf16[256,4,1,128]{0,3,2,1:T(8,128)(2,1)S(1)}, u32[]{:S(2)}, u32[]{:S(2)}) collective-permute-start(bf16[256,4,1,128]{0,3,2,1:T(8,128)(2,1)S(1)} %get-tuple-element.101), channel_id=1, source_target_pairs={{1,0},{2,1},{3,2},{4,3},{5,4},{6,5},{7,6},{8,7},{9,8},{10,9},{11,1... | collective-permute-start | bytes 786440 | tf_op jit(solution)/shard_map/ppermute | solution.py:35
  90.8 10.8 %collective-permute-start.8 = (bf16[256,4,1,128]{0,3,2,1:T(8,128)(2,1)S(1)}, bf16[256,4,1,128]{0,3,2,1:T(8,128)(2,1)S(1)}, u32[]{:S(2)}, u32[]{:S(2)}) collective-permute-start(bf16[256,4,1,128]{0,3,2,1:T(8,128)(2,1)S(1)} %get-tuple-element.100), channel_id=1, source_target_pairs={{0,1},{1,2},{2,3},{3,4},{4,5},{5,6},{6,7},{7,8},{8,9},{9,10},{10,1... | collective-permute-start | bytes 786440 | tf_op jit(solution)/shard_map/ppermute | solution.py:34

commit v4 on v3

--- a/solution.py
+++ b/solution.py
@@ -288,31 +288,43 @@
     )(packed)
 
 
+def tiled(block):
+    rows, cols = block.shape
+    return block.reshape(rows // 8, 8, cols // 128, 128).transpose(0, 2, 1, 3).reshape(-1, 8, 128)
+
+
+def untiled(tiles, rows, cols):
+    return tiles.reshape(rows // 8, cols // 128, 8, 128).transpose(0, 2, 1, 3).reshape(rows, cols)
+
+
 def pack_halves(parts, blocks):
     halves = []
     for h in range(2):
-        pieces = []
+        tiles = []
         for p in parts[:2]:
             rows = p.shape[0] // 2
-            pieces.append(p[h * rows : (h + 1) * rows].reshape(-1))
+            tiles.append(tiled(p[h * rows : (h + 1) * rows]))
+        tail = []
         for columns in parts[2:]:
             cols = columns[0].shape[0] // 2
-            pieces.extend(column[h * cols : (h + 1) * cols] for column in columns)
-        halves.append(jnp.concatenate(pieces))
-    real = halves[0].shape[0]
-    tiles = -(-real // (TILE * blocks)) * blocks
-    flat = jnp.stack(halves)
-    flat = jnp.pad(flat, ((0, 0), (0, tiles * TILE - real)))
-    return flat.reshape(2 * tiles, 8, 128), real
+            tail.extend(column[h * cols : (h + 1) * cols] for column in columns)
+        tail = jnp.concatenate(tail)
+        head = sum(t.shape[0] for t in tiles)
+        total = -(-(head + -(-tail.shape[0] // TILE)) // blocks) * blocks
+        tail = jnp.pad(tail, (0, (total - head) * TILE - tail.shape[0]))
+        halves.append(jnp.concatenate(tiles + [tail.reshape(-1, 8, 128)]))
+    return jnp.concatenate(halves), None
 
 
 def unpack_half(reduced, parts):
-    flat = reduced.reshape(-1)
     out, offset = [], 0
     for p in parts[:2]:
-        shape = (p.shape[0] // 2, p.shape[1])
-        out.append(flat[offset : offset + shape[0] * shape[1]].reshape(shape))
-        offset += shape[0] * shape[1]
+        rows, cols = p.shape[0] // 2, p.shape[1]
+        count = rows * cols // TILE
+        out.append(untiled(reduced[offset : offset + count], rows, cols))
+        offset += count
+    flat = reduced[offset:].reshape(-1)
+    offset = 0
     for columns in parts[2:]:
         shape = (len(columns), columns[0].shape[0] // 2)
         out.append(flat[offset : offset + shape[0] * shape[1]].reshape(shape))

time: 153 us -> 153 us (level)
  waiting for transfers between devices: 31.7 us -> 29 us
  matrix products: 10.9 us -> 12.5 us
    reshape x3 -> x0, local copies, waits for them, and re-layouts: 2.78 us -> none  [the longest x1 1.4 us: pack_halves(): return (flat.reshape(2 * tiles, 8, 128), real)]
    unnamed x74 -> x235, local copies, waits for them, and re-layouts: 5.4 us -> 7.14 us
    slice x0 -> x3, local copies, waits for them, and re-layouts: none -> 1.72 us  [the longest x1 1.68 us: unpack_half(): out.append(untiled(reduced[offset:offset + count], rows, cols))]
    ppermute x4, waiting for transfers between devices: 29.8 us -> 28.3 us  [extended(): theirs = lax.ppermute(jnp.concatenate([first, last], axis=dim), axis, up)]
  transfers between devices with their start and end apart: 13 -> 13, of which waited for: 6 -> 6; matrix products, arithmetic and copies ran while one was open for 15% -> 18% of each run, Pallas kernels for 0% -> 24%
where the time goes in v4:
time: 153 us; the launch traced here: 152 us
  starting transfers between devices  36.8 us (24%)
  Pallas kernels  35.9 us (23%)
  waiting for transfers between devices  29 us (19%)
  other arithmetic  23.9 us (16%)
  matrix products  12.5 us (8%)
  local copies, waits for them, and re-layouts  11.2 us (7%)
  between operations  2.97 us (2%)
    pallas_call x1, Pallas kernels, tree_reduce(): pl.pallas_call(functools.partial(reduce_kernel, plan), out_shape=jax.Shap...  35.9 us
    ppermute x4, waiting for transfers between devices, extended(): theirs = lax.ppermute(jnp.concatenate([first, last], axis=dim), axis, up)  28.3 us
    ppermute x4, starting transfers between devices, extended(): after = lax.ppermute(first, axis, down)  20.4 us
    ppermute x4, starting transfers between devices, extended(): theirs = lax.ppermute(jnp.concatenate([first, last], axis=dim), axis, up)  7.22 us
    unnamed x235, local copies, waits for them, and re-layouts  7.14 us
    reduce_sum x3, other arithmetic, tap_sums(): jnp.sum(shifted.astype(jnp.float32) * grad_float, axis=(1, 2, 3))  6.46 us
    dot_general x2, matrix products, contract_cells(): lax.dot_general(left.reshape(channels, -1), right.reshape(channels, -1),...  5.58 us
    ppermute x4, starting transfers between devices, extended(): before = lax.ppermute(last, axis, up)  5.36 us
  transfers between devices with their start and end apart: 13, of which 6 were waited for; matrix products, arithmetic and copies ran while one was open for 18% of the time, Pallas kernels for 24%

profile of v4, /device:TPU:1, one launch (start us, length us, event | category | flops | bytes accessed | tf_op | source)
XLA Modules:
  0.0 152.1 jit_solution(17136571092461347141)
XLA Ops:
  0.6 0.9 copy.31
  1.6 0.9 copy.30
  2.5 0.7 pad_maximum_fusion.58
  3.2 3.8 %collective-permute-start = (bf16[72448]{0:T(1024)(128)(2,1)S(1)}, bf16[72448]{0:T(1024)(128)(2,1)S(1)}, u32[]{:S(2)}, u32[]{:S(2)}) collective-permute-start(bf16[72448]{0:T(1024)(128)(2,1)S(1)} %pad_maximum_fusion.58), channel_id=1, source_target_pairs={{0,128},{128,0},{1,129},{129,1},{2,130},{130,2},{3,131},{131,3},{4... | collective-permute-start | bytes 434696 | tf_op jit(solution)/shard_map/ppermute | solution.py:42
  7.1 1.3 copy.13
  8.4 0.1 collective-permute-start.4
  8.5 0.4 reshape.544
  8.9 0.3 copy.11
  9.2 0.2 copy.12
  9.5 0.1 collective-permute-done
  9.6 0.1 broadcast_select_fusion.1
  9.7 0.3 convolution_convert_fusion.1
  10.1 3.7 %collective-permute-start.1 = (bf16[256,2,4,128]{0,3,2,1:T(8,128)(2,1)S(1)}, bf16[256,2,4,128]{0,3,2,1:T(8,128)(2,1)S(1)}, u32[]{:S(2)}, u32[]{:S(2)}) collective-permute-start(bf16[256,2,4,128]{0,3,2,1:T(8,128)(2,1)S(1)} %convolution_convert_fusion.1), channel_id=1, source_target_pairs={{0,128},{128,0},{1,129},{129,1},{2,130},{130,2},{3,131},{131,3},{4... | collective-permute-start | bytes 1572872 | tf_op jit(solution)/shard_map/ppermute | solution.py:30
  13.9 0.6 fusion.275
  14.5 0.6 fusion.284
  15.5 7.1 %collective-permute-done.4 = bf16[256,2,4,128]{0,3,2,1:T(8,128)(2,1)S(1)} collective-permute-done((bf16[256,2,4,128]{0,3,2,1:T(8,128)(2,1)S(1)}, bf16[256,2,4,128]{0,3,2,1:T(8,128)(2,1)S(1)}, u32[]{:S(2)}, u32[]{:S(2)}) %collective-permute-start.4) | collective-permute-done | bytes 524320 | tf_op jit(solution)/shard_map/ppermute | solution.py:30
  22.7 0.1 pad_maximum_fusion.54
  22.7 3.5 %collective-permute-start.5 = (bf16[256,4,1,128]{0,3,2,1:T(8,128)(2,1)S(1)}, bf16[256,4,1,128]{0,3,2,1:T(8,128)(2,1)S(1)}, u32[]{:S(2)}, u32[]{:S(2)}) collective-permute-start(bf16[256,4,1,128]{0,3,2,1:T(8,128)(2,1)S(1)} %get-tuple-element.108), channel_id=1, source_target_pairs={{0,1},{1,2},{2,3},{3,4},{4,5},{5,6},{6,7},{7,8},{8,9},{9,10},{10,1... | collective-permute-start | bytes 786440 | tf_op jit(solution)/shard_map/ppermute | solution.py:34
  26.3 10.4 %collective-permute-done.1 = bf16[256,2,4,128]{0,3,2,1:T(8,128)(2,1)S(1)} collective-permute-done((bf16[256,2,4,128]{0,3,2,1:T(8,128)(2,1)S(1)}, bf16[256,2,4,128]{0,3,2,1:T(8,128)(2,1)S(1)}, u32[]{:S(2)}, u32[]{:S(2)}) %collective-permute-start.1) | collective-permute-done | bytes 524320 | tf_op jit(solution)/shard_map/ppermute | solution.py:30
  36.7 0.1 pad_maximum_fusion.57
  36.8 3.3 %collective-permute-start.3 = (bf16[256,4,1,128]{0,3,2,1:T(8,128)(2,1)S(1)}, bf16[256,4,1,128]{0,3,2,1:T(8,128)(2,1)S(1)}, u32[]{:S(2)}, u32[]{:S(2)}) collective-permute-start(bf16[256,4,1,128]{0,3,2,1:T(8,128)(2,1)S(1)} %get-tuple-element.105), channel_id=1, source_target_pairs={{1,0},{2,1},{3,2},{4,3},{5,4},{6,5},{7,6},{8,7},{9,8},{10,9},{11,1... | collective-permute-start | bytes 786440 | tf_op jit(solution)/shard_map/ppermute | solution.py:35
  40.0 0.2 maximum_maximum_fusion.1
  40.3 0.7 fusion.5
  41.0 0.3 fusion.4
  41.6 4.3 %fusion.36 = bf16[256,2,4,128]{0,3,2,1:T(8,128)(2,1)S(1)} fusion(bf16[256,2,4,128]{0,3,2,1:T(8,128)(2,1)S(1)} %copy.13, f32[256]{0:T(256)S(1)} %bitcast.187, f32[256]{0:T(256)S(1)} %bitcast.189, f32[256]{0:T(256)S(1)} %bitcast.185, f32[256]{0:T(256)S(1)} %bitcast.183, f32[256]{0:T(256)S(1)} %bitcast.181, f32[256]{0:T(256)S(1)} %bitcast.179, ...), kind=kLoop, calls=%fused_computation.190 | loop fusion | flops 21757952 | bytes 14183424 | tf_op jit(solution)/shard_map/convert_element_type | solution.py:341
  45.9 0.3 collective-permute-done.2
  46.2 0.7 fusion.6
  46.9 0.2 pad_maximum_fusion.32
  47.1 0.3 fusion.7
  47.6 4.6 %fusion.149 = (bf16[256,2,4,128]{0,3,2,1:T(8,128)(2,1)S(1)}, f32[256,2,4,128]{0,3,2,1:T(8,128)S(1)}) fusion(bf16[256,2,4,128]{0,3,2,1:T(8,128)(2,1)S(1)} %convolution_convert_fusion.1, bf16[256,4,6,129]{0,3,2,1:T(8,128)(2,1)S(1)} %fusion.6, bf16[256,4,5,128]{0,3,2,1:T(8,128)(2,1)S(1)} %get-tuple-element.103, bf16[256,4,6,129]{0,3,2,1:T(8,128)(2,1)S(1)} %fusion.7, ...), kind=kOutput, calls=%fused_computation.305 | convolution fusion | flops 158334976 | bytes 15887360 | tf_op jit(solution)/shard_map/dot_general | solution.py:86
  52.2 1.9 %fusion.146 = (f32[256]{0:T(256)S(1)}, f32[256]{0:T(256)S(1)}, f32[256]{0:T(256)S(1)}, f32[256]{0:T(256)S(1)}, f32[256]{0:T(256)S(1)}, /*index=5*/f32[256]{0:T(2...) fusion(bf16[256,4,5,128]{0,3,2,1:T(8,128)(2,1)S(1)} %get-tuple-, ...), kind=kOutput, calls=%fused_computation.300 | convolution fusion | flops 144438272 | bytes 7483392 | tf_op jit(solution)/shard_map/dot_general | solution.py:92
  54.2 0.3 fusion.9
  54.5 3.0 %collective-permute-start.7 = (bf16[256,2,4,128]{0,3,2,1:T(8,128)(2,1)S(1)}, bf16[256,2,4,128]{0,3,2,1:T(8,128)(2,1)S(1)}, u32[]{:S(2)}, u32[]{:S(2)}) collective-permute-start(bf16[256,2,4,128]{0,3,2,1:T(8,128)(2,1)S(1)} %get-tuple-element.300), channel_id=1, source_target_pairs={{0,128},{128,0},{1,129},{129,1},{2,130},{130,2},{3,131},{131,3},{4... | collective-permute-start | bytes 1572872 | tf_op jit(solution)/shard_map/ppermute | solution.py:30
  57.5 2.6 %fusion.147 = (f32[256]{0:T(256)S(1)}, f32[256]{0:T(256)S(1)}, f32[256]{0:T(256)S(1)}, f32[256]{0:T(256)S(1)}, f32[256]{0:T(256)S(1)}, /*index=5*/f32[256]{0:T(2...) fusion(bf16[256,2,4,128]{0,3,2,1:T(8,128)(2,1)S(1)} %get-tuple-, ...), kind=kLoop, calls=%fused_computation.301 | loop fusion | flops 12579072 | bytes 7879680 | tf_op jit(solution)/shard_map/reduce_sum | solution.py:79
  60.1 0.3 multiply_convert_fusion
  60.4 0.4 collective-permute-start.10
  61.5 0.6 copy-done.4
  62.1 10.8 %collective-permute-done.10 = bf16[256,2,4,128]{0,3,2,1:T(8,128)(2,1)S(1)} collective-permute-done((bf16[256,2,4,128]{0,3,2,1:T(8,128)(2,1)S(1)}, bf16[256,2,4,128]{0,3,2,1:T(8,128)(2,1)S(1)}, u32[]{:S(2)}, u32[]{:S(2)}) %collective-permute-start.10) | collective-permute-done | bytes 524320 | tf_op jit(solution)/shard_map/ppermute | solution.py:30
  72.9 0.1 pad_maximum_fusion.48
  73.0 9.4 %collective-permute-start.12 = (bf16[256,4,1,128]{0,3,2,1:T(8,128)(2,1)S(1)}, bf16[256,4,1,128]{0,3,2,1:T(8,128)(2,1)S(1)}, u32[]{:S(2)}, u32[]{:S(2)}) collective-permute-start(bf16[256,4,1,128]{0,3,2,1:T(8,128)(2,1)S(1)} %get-tuple-element.97), channel_id=1, source_target_pairs={{1,0},{2,1},{3,2},{4,3},{5,4},{6,5},{7,6},{8,7},{9,8},{10,9},{11,1... | collective-permute-start | bytes 786440 | tf_op jit(solution)/shard_map/ppermute | solution.py:35
  82.3 1.8 %collective-permute-start.11 = (bf16[256,4,1,128]{0,3,2,1:T(8,128)(2,1)S(1)}, bf16[256,4,1,128]{0,3,2,1:T(8,128)(2,1)S(1)}, u32[]{:S(2)}, u32[]{:S(2)}) collective-permute-start(bf16[256,4,1,128]{0,3,2,1:T(8,128)(2,1)S(1)} %get-tuple-element.96), channel_id=1, source_target_pairs={{0,1},{1,2},{2,3},{3,4},{4,5},{5,6},{6,7},{7,8},{8,9},{9,10},{10,1... | collective-permute-start | bytes 786440 | tf_op jit(solution)/shard_map/ppermute | solution.py:34
  84.2 0.8 pad_maximum_fusion.51
  85.0 7.7 %collective-permute-start.9 = (bf16[256,4,1,128]{0,3,2,1:T(8,128)(2,1)}, bf16[256,4,1,128]{0,3,2,1:T(8,128)(2,1)S(1)}, u32[]{:S(2)}, u32[]{:S(2)}) collective-permute-start(bf16[256,4,1,128]{0,3,2,1:T(8,128)(2,1)} %get-tuple-element.101), channel_id=1, source_target_pairs={{1,0},{2,1},{3,2},{4,3},{5,4},{6,5},{7,6},{8,7},{9,8},{10,9},{11,1... | collective-permute-start | bytes 786440 | tf_op jit(solution)/shard_map/ppermute | solution.py:35
  92.7 0.4 collective-permute-done.11
  93.1 0.2 maximum_maximum_fusion.3
  93.3 0.7 fusion.1
  94.0 1.3 fusion.104
  95.3 0.3 fusion
  95.9 2.6 %fusion.105 = (f32[256]{0:T(256)S(1)}, f32[256]{0:T(256)S(1)}, f32[256]{0:T(256)S(1)}, f32[256]{0:T(256)S(1)}, f32[256]{0:T(256)S(1)}, /*index=5*/f32[256]{0:T(2...) fusion(bf16[256,2,4,128]{0,3,2,1:T(8,128)(2,1)S(1)} %convolutio, ...), kind=kLoop, calls=%fused_computation.259 | loop fusion | flops 12579072 | bytes 7879680 | tf_op jit(solution)/shard_map/reduce_sum | solution.py:79
  98.6 5.2 %fusion.8 = f32[256,256]{1,0:T(8,128)S(1)} fusion(bf16[256,2,4,128]{0,3,2,1:T(8,128)(2,1)S(1)} %copy.11, bf16[256,2,4,128]{0,3,2,1:T(8,128)(2,1)S(1)} %multiply_convert_fusion, f32[256]{0:T(256)S(1)} %bitcast.242, f32[256]{0:T(256)S(1)} %bitcast.244, f32[256]{0:T(256)S(1)} %bitcast.240, f32[256]{0:T(256)S(1)} %bitcast.238, f32[256]{0:T(256)S(1)} %bitcast.236, ...), kind=kOutput, calls=%fused_computation.161 | convolution fusion | flops 156041216 | bytes 14445568 | tf_op jit(solution)/shard_map/dot_general | solution.py:97
  104.8 0.8 copy-done.1
  105.6 35.9 %shard_map.101 = f32[80,8,128]{2,1,0:T(8,128)} custom-call(f32[160,8,128]{2,1,0:T(8,128)} %copy-done.1), custom_call_target="tpu_custom_call" | custom-call | bytes 41943040 | tf_op jit(solution)/shard_map/pallas_call | solution.py:278
  141.5 0.8 slice_bitcast_fusion
  142.3 1.7 %fusion.294 = (f32[32,8,128]{2,1,0:T(8,128)}, f32[32,8,128]{2,1,0:T(8,128)}) fusion(f32[80,8,128]{2,1,0:T(8,128)} %shard_map.101), kind=kLoop, calls=%fused_computation.753 | loop fusion | bytes 524288 | tf_op jit(solution)/shard_map/slice | solution.py:324
  144.0 0.7 fusion.2
  144.7 0.2 pad_maximum_fusion.34
  145.2 0.3 fusion.3
  145.6 0.1 copy-done.9
  145.7 0.0 copy-done.25
  145.7 0.0 copy-done.29
  145.8 0.0 copy-done.39
  145.9 4.6 %fusion.148 = bf16[256,2,4,128]{0,3,2,1:T(8,128)(2,1)S(1)} fusion(bf16[256,2,4,128]{0,3,2,1:T(8,128)(2,1)S(1)} %get-tuple-element.300, bf16[256,2,4,128]{0,3,2,1:T(8,128)(2,1)S(1)} %copy.11, bf16[256,4,6,129]{0,3,2,1:T(8,128)(2,1)S(1)} %fusion.2, bf16[256,4,5,128]{0,3,2,1:T(8,128)(2,1)S(1)} %get-tuple-element.99, bf16[256,4,6,129]{0,3,2,1:T(8,128)(2,1)S(1)} %fusion.3, ...), kind=kLoop, calls=%fused_computation.304 | loop fusion | flops 22282240 | bytes 14707712 | tf_op jit(solution)/shard_map/convert_element_type | solution.py:357
  150.4 1.1 copy.22
  151.5 0.6 fusion.299
  (308 shorter events, 1.6 us)
Async XLA Ops:
  0.6 7.9 %copy-start = (bf16[256,2,4,128]{3,2,1,0:T(4,128)(2,1)S(1)}, bf16[256,2,4,128]{3,2,1,0:T(4,128)(2,1)}, u32[]{:S(2)}) copy-start(bf16[256,2,4,128]{3,2,1,0:T(4,128)(2,1)} %param.7) | copy-start | bytes 1572868
  3.2 6.3 %collective-permute-start = (bf16[72448]{0:T(1024)(128)(2,1)S(1)}, bf16[72448]{0:T(1024)(128)(2,1)S(1)}, u32[]{:S(2)}, u32[]{:S(2)}) collective-permute-start(bf16[72448]{0:T(1024)(128)(2,1)S(1)} %pad_maximum_fusion.58), channel_id=1, source_target_pairs={{0,128},{128,0},{1,129},{129,1},{2,130},{130,2},{3,131},{131,3},{4... | collective-permute-start | bytes 434696 | tf_op jit(solution)/shard_map/ppermute | solution.py:42
  8.4 14.2 %collective-permute-start.4 = (bf16[256,2,4,128]{0,3,2,1:T(8,128)(2,1)S(1)}, bf16[256,2,4,128]{0,3,2,1:T(8,128)(2,1)S(1)}, u32[]{:S(2)}, u32[]{:S(2)}) collective-permute-start(bf16[256,2,4,128]{0,3,2,1:T(8,128)(2,1)S(1)} %copy.13), channel_id=1, source_target_pairs={{0,128},{128,0},{1,129},{129,1},{2,130},{130,2},{3,131},{131,3},{4... | collective-permute-start | bytes 1572872 | tf_op jit(solution)/shard_map/ppermute | solution.py:30
  10.1 26.6 %collective-permute-start.1 = (bf16[256,2,4,128]{0,3,2,1:T(8,128)(2,1)S(1)}, bf16[256,2,4,128]{0,3,2,1:T(8,128)(2,1)S(1)}, u32[]{:S(2)}, u32[]{:S(2)}) collective-permute-start(bf16[256,2,4,128]{0,3,2,1:T(8,128)(2,1)S(1)} %convolution_convert_fusion.1), channel_id=1, source_target_pairs={{0,128},{128,0},{1,129},{129,1},{2,130},{130,2},{3,131},{131,3},{4... | collective-permute-start | bytes 1572872 | tf_op jit(solution)/shard_map/ppermute | solution.py:30
  13.8 33.6 %copy-start.54 = (f32[1,256]{1,0:T(1,128)}, f32[1,256]{1,0:T(1,128)S(1)}, u32[]{:S(2)}) copy-start(f32[1,256]{1,0:T(1,128)S(1)} %get-tuple-element.154) | copy-start | bytes 3076
  13.8 33.6 %copy-start.56 = (f32[1,256]{1,0:T(1,128)}, f32[1,256]{1,0:T(1,128)S(1)}, u32[]{:S(2)}) copy-start(f32[1,256]{1,0:T(1,128)S(1)} %get-tuple-element.155) | copy-start | bytes 3076
  13.9 33.6 %copy-start.58 = (f32[1,256]{1,0:T(1,128)}, f32[1,256]{1,0:T(1,128)S(1)}, u32[]{:S(2)}) copy-start(f32[1,256]{1,0:T(1,128)S(1)} %get-tuple-element.156) | copy-start | bytes 3076
  13.9 33.6 %copy-start.60 = (f32[1,256]{1,0:T(1,128)}, f32[1,256]{1,0:T(1,128)S(1)}, u32[]{:S(2)}) copy-start(f32[1,256]{1,0:T(1,128)S(1)} %get-tuple-element.157) | copy-start | bytes 3076
  13.9 33.6 %copy-start.62 = (f32[1,256]{1,0:T(1,128)}, f32[1,256]{1,0:T(1,128)S(1)}, u32[]{:S(2)}) copy-start(f32[1,256]{1,0:T(1,128)S(1)} %get-tuple-element.158) | copy-start | bytes 3076
  13.9 33.6 %copy-start.64 = (f32[1,256]{1,0:T(1,128)}, f32[1,256]{1,0:T(1,128)S(1)}, u32[]{:S(2)}) copy-start(f32[1,256]{1,0:T(1,128)S(1)} %get-tuple-element.159) | copy-start | bytes 3076
  13.9 33.6 %copy-start.66 = (f32[1,256]{1,0:T(1,128)}, f32[1,256]{1,0:T(1,128)S(1)}, u32[]{:S(2)}) copy-start(f32[1,256]{1,0:T(1,128)S(1)} %get-tuple-element.160) | copy-start | bytes 3076
  13.9 33.6 %copy-start.68 = (f32[1,256]{1,0:T(1,128)}, f32[1,256]{1,0:T(1,128)S(1)}, u32[]{:S(2)}) copy-start(f32[1,256]{1,0:T(1,128)S(1)} %get-tuple-element.161) | copy-start | bytes 3076
  13.9 33.6 %copy-start.70 = (f32[1,256]{1,0:T(1,128)}, f32[1,256]{1,0:T(1,128)S(1)}, u32[]{:S(2)}) copy-start(f32[1,256]{1,0:T(1,128)S(1)} %get-tuple-element.162) | copy-start | bytes 3076
  14.5 33.0 %copy-start.72 = (f32[1,256]{1,0:T(1,128)}, f32[1,256]{1,0:T(1,128)S(1)}, u32[]{:S(2)}) copy-start(f32[1,256]{1,0:T(1,128)S(1)} %get-tuple-element.145) | copy-start | bytes 3076
  14.5 33.0 %copy-start.74 = (f32[1,256]{1,0:T(1,128)}, f32[1,256]{1,0:T(1,128)S(1)}, u32[]{:S(2)}) copy-start(f32[1,256]{1,0:T(1,128)S(1)} %get-tuple-element.146) | copy-start | bytes 3076
  14.5 33.0 %copy-start.76 = (f32[1,256]{1,0:T(1,128)}, f32[1,256]{1,0:T(1,128)S(1)}, u32[]{:S(2)}) copy-start(f32[1,256]{1,0:T(1,128)S(1)} %get-tuple-element.147) | copy-start | bytes 3076
  14.5 33.0 %copy-start.78 = (f32[1,256]{1,0:T(1,128)}, f32[1,256]{1,0:T(1,128)S(1)}, u32[]{:S(2)}) copy-start(f32[1,256]{1,0:T(1,128)S(1)} %get-tuple-element.148) | copy-start | bytes 3076
  14.5 33.0 %copy-start.80 = (f32[1,256]{1,0:T(1,128)}, f32[1,256]{1,0:T(1,128)S(1)}, u32[]{:S(2)}) copy-start(f32[1,256]{1,0:T(1,128)S(1)} %get-tuple-element.149) | copy-start | bytes 3076
  14.5 33.0 %copy-start.82 = (f32[1,256]{1,0:T(1,128)}, f32[1,256]{1,0:T(1,128)S(1)}, u32[]{:S(2)}) copy-start(f32[1,256]{1,0:T(1,128)S(1)} %get-tuple-element.150) | copy-start | bytes 3076
  14.5 33.0 %copy-start.84 = (f32[1,256]{1,0:T(1,128)}, f32[1,256]{1,0:T(1,128)S(1)}, u32[]{:S(2)}) copy-start(f32[1,256]{1,0:T(1,128)S(1)} %get-tuple-element.151) | copy-start | bytes 3076
  15.2 26.2 %copy-start.8 = (f32[1,256]{1,0:T(1,128)}, f32[1,256]{1,0:T(1,128)S(1)}, u32[]{:S(2)}) copy-start(f32[1,256]{1,0:T(1,128)S(1)} %get-tuple-element.185) | copy-start | bytes 3076
  15.2 26.2 %copy-start.10 = (f32[1,256]{1,0:T(1,128)}, f32[1,256]{1,0:T(1,128)S(1)}, u32[]{:S(2)}) copy-start(f32[1,256]{1,0:T(1,128)S(1)} %get-tuple-element.186) | copy-start | bytes 3076
  15.2 26.2 %copy-start.12 = (f32[1,256]{1,0:T(1,128)}, f32[1,256]{1,0:T(1,128)S(1)}, u32[]{:S(2)}) copy-start(f32[1,256]{1,0:T(1,128)S(1)} %get-tuple-element.187) | copy-start | bytes 3076
  15.2 26.2 %copy-start.14 = (f32[1,256]{1,0:T(1,128)}, f32[1,256]{1,0:T(1,128)S(1)}, u32[]{:S(2)}) copy-start(f32[1,256]{1,0:T(1,128)S(1)} %get-tuple-element.188) | copy-start | bytes 3076
  15.2 26.2 %copy-start.16 = (f32[1,256]{1,0:T(1,128)}, f32[1,256]{1,0:T(1,128)S(1)}, u32[]{:S(2)}) copy-start(f32[1,256]{1,0:T(1,128)S(1)} %get-tuple-element.189) | copy-start | bytes 3076
  15.3 26.1 %copy-start.18 = (f32[1,256]{1,0:T(1,128)}, f32[1,256]{1,0:T(1,128)S(1)}, u32[]{:S(2)}) copy-start(f32[1,256]{1,0:T(1,128)S(1)} %get-tuple-element.172) | copy-start | bytes 3076
  15.3 26.1 %copy-start.20 = (f32[1,256]{1,0:T(1,128)}, f32[1,256]{1,0:T(1,128)S(1)}, u32[]{:S(2)}) copy-start(f32[1,256]{1,0:T(1,128)S(1)} %get-tuple-element.173) | copy-start | bytes 3076
  15.3 26.1 %copy-start.22 = (f32[1,256]{1,0:T(1,128)}, f32[1,256]{1,0:T(1,128)S(1)}, u32[]{:S(2)}) copy-start(f32[1,256]{1,0:T(1,128)S(1)} %get-tuple-element.174) | copy-start | bytes 3076
  15.3 26.1 %copy-start.24 = (f32[1,256]{1,0:T(1,128)}, f32[1,256]{1,0:T(1,128)S(1)}, u32[]{:S(2)}) copy-start(f32[1,256]{1,0:T(1,128)S(1)} %get-tuple-element.175) | copy-start | bytes 3076
  15.3 26.1 %copy-start.26 = (f32[1,256]{1,0:T(1,128)}, f32[1,256]{1,0:T(1,128)S(1)}, u32[]{:S(2)}) copy-start(f32[1,256]{1,0:T(1,128)S(1)} %get-tuple-element.176) | copy-start | bytes 3076
  15.3 26.1 %copy-start.28 = (f32[1,256]{1,0:T(1,128)}, f32[1,256]{1,0:T(1,128)S(1)}, u32[]{:S(2)}) copy-start(f32[1,256]{1,0:T(1,128)S(1)} %get-tuple-element.177) | copy-start | bytes 3076
  15.3 26.1 %copy-start.30 = (f32[1,256]{1,0:T(1,128)}, f32[1,256]{1,0:T(1,128)S(1)}, u32[]{:S(2)}) copy-start(f32[1,256]{1,0:T(1,128)S(1)} %get-tuple-element.178) | copy-start | bytes 3076
  15.3 26.1 %copy-start.32 = (f32[1,256]{1,0:T(1,128)}, f32[1,256]{1,0:T(1,128)S(1)}, u32[]{:S(2)}) copy-start(f32[1,256]{1,0:T(1,128)S(1)} %get-tuple-element.179) | copy-start | bytes 3076
  15.3 26.1 %copy-start.34 = (f32[1,256]{1,0:T(1,128)}, f32[1,256]{1,0:T(1,128)S(1)}, u32[]{:S(2)}) copy-start(f32[1,256]{1,0:T(1,128)S(1)} %get-tuple-element.180) | copy-start | bytes 3076
  15.4 26.0 %copy-start.36 = (f32[1,256]{1,0:T(1,128)}, f32[1,256]{1,0:T(1,128)S(1)}, u32[]{:S(2)}) copy-start(f32[1,256]{1,0:T(1,128)S(1)} %get-tuple-element.163) | copy-start | bytes 3076
  15.4 26.0 %copy-start.38 = (f32[1,256]{1,0:T(1,128)}, f32[1,256]{1,0:T(1,128)S(1)}, u32[]{:S(2)}) copy-start(f32[1,256]{1,0:T(1,128)S(1)} %get-tuple-element.164) | copy-start | bytes 3076
  15.5 26.0 %copy-start.40 = (f32[1,256]{1,0:T(1,128)}, f32[1,256]{1,0:T(1,128)S(1)}, u32[]{:S(2)}) copy-start(f32[1,256]{1,0:T(1,128)S(1)} %get-tuple-element.165) | copy-start | bytes 3076
  15.5 26.0 %copy-start.42 = (f32[1,256]{1,0:T(1,128)}, f32[1,256]{1,0:T(1,128)S(1)}, u32[]{:S(2)}) copy-start(f32[1,256]{1,0:T(1,128)S(1)} %get-tuple-element.166) | copy-start | bytes 3076
  15.5 26.0 %copy-start.44 = (f32[1,256]{1,0:T(1,128)}, f32[1,256]{1,0:T(1,128)S(1)}, u32[]{:S(2)}) copy-start(f32[1,256]{1,0:T(1,128)S(1)} %get-tuple-element.167) | copy-start | bytes 3076
  15.5 26.0 %copy-start.46 = (f32[1,256]{1,0:T(1,128)}, f32[1,256]{1,0:T(1,128)S(1)}, u32[]{:S(2)}) copy-start(f32[1,256]{1,0:T(1,128)S(1)} %get-tuple-element.168) | copy-start | bytes 3076
  15.5 26.0 %copy-start.48 = (f32[1,256]{1,0:T(1,128)}, f32[1,256]{1,0:T(1,128)S(1)}, u32[]{:S(2)}) copy-start(f32[1,256]{1,0:T(1,128)S(1)} %get-tuple-element.169) | copy-start | bytes 3076
  15.5 26.0 %copy-start.50 = (f32[1,256]{1,0:T(1,128)}, f32[1,256]{1,0:T(1,128)S(1)}, u32[]{:S(2)}) copy-start(f32[1,256]{1,0:T(1,128)S(1)} %get-tuple-element.170) | copy-start | bytes 3076
  15.5 26.0 %copy-start.52 = (f32[1,256]{1,0:T(1,128)}, f32[1,256]{1,0:T(1,128)S(1)}, u32[]{:S(2)}) copy-start(f32[1,256]{1,0:T(1,128)S(1)} %get-tuple-element.171) | copy-start | bytes 3076
  22.7 17.3 %collective-permute-start.5 = (bf16[256,4,1,128]{0,3,2,1:T(8,128)(2,1)S(1)}, bf16[256,4,1,128]{0,3,2,1:T(8,128)(2,1)S(1)}, u32[]{:S(2)}, u32[]{:S(2)}) collective-permute-start(bf16[256,4,1,128]{0,3,2,1:T(8,128)(2,1)S(1)} %get-tuple-element.108), channel_id=1, source_target_pairs={{0,1},{1,2},{2,3},{3,4},{4,5},{5,6},{6,7},{7,8},{8,9},{9,10},{10,1... | collective-permute-start | bytes 786440 | tf_op jit(solution)/shard_map/ppermute | solution.py:34
  26.3 13.8 %collective-permute-start.6 = (bf16[256,4,1,128]{0,3,2,1:T(8,128)(2,1)S(1)}, bf16[256,4,1,128]{0,3,2,1:T(8,128)(2,1)S(1)}, u32[]{:S(2)}, u32[]{:S(2)}) collective-permute-start(bf16[256,4,1,128]{0,3,2,1:T(8,128)(2,1)S(1)} %get-tuple-element.109), channel_id=1, source_target_pairs={{1,0},{2,1},{3,2},{4,3},{5,4},{6,5},{7,6},{8,7},{9,8},{10,9},{11,1... | collective-permute-start | bytes 786440 | tf_op jit(solution)/shard_map/ppermute | solution.py:35
  36.8 9.1 %collective-permute-start.3 = (bf16[256,4,1,128]{0,3,2,1:T(8,128)(2,1)S(1)}, bf16[256,4,1,128]{0,3,2,1:T(8,128)(2,1)S(1)}, u32[]{:S(2)}, u32[]{:S(2)}) collective-permute-start(bf16[256,4,1,128]{0,3,2,1:T(8,128)(2,1)S(1)} %get-tuple-element.105), channel_id=1, source_target_pairs={{1,0},{2,1},{3,2},{4,3},{5,4},{6,5},{7,6},{8,7},{9,8},{10,9},{11,1... | collective-permute-start | bytes 786440 | tf_op jit(solution)/shard_map/ppermute | solution.py:35
  40.0 6.1 %collective-permute-start.2 = (bf16[256,4,1,128]{0,3,2,1:T(8,128)(2,1)S(1)}, bf16[256,4,1,128]{0,3,2,1:T(8,128)(2,1)S(1)}, u32[]{:S(2)}, u32[]{:S(2)}) collective-permute-start(bf16[256,4,1,128]{0,3,2,1:T(8,128)(2,1)S(1)} %get-tuple-element.104), channel_id=1, source_target_pairs={{0,1},{1,2},{2,3},{3,4},{4,5},{5,6},{6,7},{7,8},{8,9},{9,10},{10,1... | collective-permute-start | bytes 786440 | tf_op jit(solution)/shard_map/ppermute | solution.py:34
  54.5 29.7 %collective-permute-start.7 = (bf16[256,2,4,128]{0,3,2,1:T(8,128)(2,1)S(1)}, bf16[256,2,4,128]{0,3,2,1:T(8,128)(2,1)S(1)}, u32[]{:S(2)}, u32[]{:S(2)}) collective-permute-start(bf16[256,2,4,128]{0,3,2,1:T(8,128)(2,1)S(1)} %get-tuple-element.300), channel_id=1, source_target_pairs={{0,128},{128,0},{1,129},{129,1},{2,130},{130,2},{3,131},{131,3},{4... | collective-permute-start | bytes 1572872 | tf_op jit(solution)/shard_map/ppermute | solution.py:30
  60.4 12.5 %collective-permute-start.10 = (bf16[256,2,4,128]{0,3,2,1:T(8,128)(2,1)S(1)}, bf16[256,2,4,128]{0,3,2,1:T(8,128)(2,1)S(1)}, u32[]{:S(2)}, u32[]{:S(2)}) collective-permute-start(bf16[256,2,4,128]{0,3,2,1:T(8,128)(2,1)S(1)} %multiply_convert_fusion), channel_id=1, source_target_pairs={{0,128},{128,0},{1,129},{129,1},{2,130},{130,2},{3,131},{131,3},{4... | collective-permute-start | bytes 1572872 | tf_op jit(solution)/shard_map/ppermute | solution.py:30
  73.0 19.7 %collective-permute-start.12 = (bf16[256,4,1,128]{0,3,2,1:T(8,128)(2,1)S(1)}, bf16[256,4,1,128]{0,3,2,1:T(8,128)(2,1)S(1)}, u32[]{:S(2)}, u32[]{:S(2)}) collective-permute-start(bf16[256,4,1,128]{0,3,2,1:T(8,128)(2,1)S(1)} %get-tuple-element.97), channel_id=1, source_target_pairs={{1,0},{2,1},{3,2},{4,3},{5,4},{6,5},{7,6},{8,7},{9,8},{10,9},{11,1... | collective-permute-start | bytes 786440 | tf_op jit(solution)/shard_map/ppermute | solution.py:35
  82.3 10.8 %collective-permute-start.11 = (bf16[256,4,1,128]{0,3,2,1:T(8,128)(2,1)S(1)}, bf16[256,4,1,128]{0,3,2,1:T(8,128)(2,1)S(1)}, u32[]{:S(2)}, u32[]{:S(2)}) collective-permute-start(bf16[256,4,1,128]{0,3,2,1:T(8,128)(2,1)S(1)} %get-tuple-element.96), channel_id=1, source_target_pairs={{0,1},{1,2},{2,3},{3,4},{4,5},{5,6},{6,7},{7,8},{8,9},{9,10},{10,1... | collective-permute-start | bytes 786440 | tf_op jit(solution)/shard_map/ppermute | solution.py:34
  85.0 59.1 %collective-permute-start.9 = (bf16[256,4,1,128]{0,3,2,1:T(8,128)(2,1)}, bf16[256,4,1,128]{0,3,2,1:T(8,128)(2,1)S(1)}, u32[]{:S(2)}, u32[]{:S(2)}) collective-permute-start(bf16[256,4,1,128]{0,3,2,1:T(8,128)(2,1)} %get-tuple-element.101), channel_id=1, source_target_pairs={{1,0},{2,1},{3,2},{4,3},{5,4},{6,5},{7,6},{8,7},{9,8},{10,9},{11,1... | collective-permute-start | bytes 786440 | tf_op jit(solution)/shard_map/ppermute | solution.py:35
  92.7 51.3 %collective-permute-start.8 = (bf16[256,4,1,128]{0,3,2,1:T(8,128)(2,1)S(1)}, bf16[256,4,1,128]{0,3,2,1:T(8,128)(2,1)S(1)}, u32[]{:S(2)}, u32[]{:S(2)}) collective-permute-start(bf16[256,4,1,128]{0,3,2,1:T(8,128)(2,1)S(1)} %get-tuple-element.100), channel_id=1, source_target_pairs={{0,1},{1,2},{2,3},{3,4},{4,5},{5,6},{6,7},{7,8},{8,9},{9,10},{10,1... | collective-permute-start | bytes 786440 | tf_op jit(solution)/shard_map/ppermute | solution.py:34
  95.7 2.7 %copy-start.55 = (f32[1,256]{1,0:T(1,128)S(1)}, f32[1,256]{1,0:T(1,128)}, u32[]{:S(2)}) copy-start(f32[1,256]{1,0:T(1,128)} %copy-done.54) | copy-start | bytes 3076
  95.7 2.7 %copy-start.57 = (f32[1,256]{1,0:T(1,128)S(1)}, f32[1,256]{1,0:T(1,128)}, u32[]{:S(2)}) copy-start(f32[1,256]{1,0:T(1,128)} %copy-done.56) | copy-start | bytes 3076
  95.7 2.7 %copy-start.59 = (f32[1,256]{1,0:T(1,128)S(1)}, f32[1,256]{1,0:T(1,128)}, u32[]{:S(2)}) copy-start(f32[1,256]{1,0:T(1,128)} %copy-done.58) | copy-start | bytes 3076
  95.7 2.7 %copy-start.61 = (f32[1,256]{1,0:T(1,128)S(1)}, f32[1,256]{1,0:T(1,128)}, u32[]{:S(2)}) copy-start(f32[1,256]{1,0:T(1,128)} %copy-done.60) | copy-start | bytes 3076
  95.7 2.7 %copy-start.63 = (f32[1,256]{1,0:T(1,128)S(1)}, f32[1,256]{1,0:T(1,128)}, u32[]{:S(2)}) copy-start(f32[1,256]{1,0:T(1,128)} %copy-done.62) | copy-start | bytes 3076
  95.7 2.7 %copy-start.65 = (f32[1,256]{1,0:T(1,128)S(1)}, f32[1,256]{1,0:T(1,128)}, u32[]{:S(2)}) copy-start(f32[1,256]{1,0:T(1,128)} %copy-done.64) | copy-start | bytes 3076
  95.8 2.7 %copy-start.67 = (f32[1,256]{1,0:T(1,128)S(1)}, f32[1,256]{1,0:T(1,128)}, u32[]{:S(2)}) copy-start(f32[1,256]{1,0:T(1,128)} %copy-done.66) | copy-start | bytes 3076
  95.8 2.7 %copy-start.69 = (f32[1,256]{1,0:T(1,128)S(1)}, f32[1,256]{1,0:T(1,128)}, u32[]{:S(2)}) copy-start(f32[1,256]{1,0:T(1,128)} %copy-done.68) | copy-start | bytes 3076
  95.8 2.7 %copy-start.71 = (f32[1,256]{1,0:T(1,128)S(1)}, f32[1,256]{1,0:T(1,128)}, u32[]{:S(2)}) copy-start(f32[1,256]{1,0:T(1,128)} %copy-done.70) | copy-start | bytes 3076
  98.6 5.6 %copy-start.5 = (f32[6912]{0:T(1024)S(1)}, f32[6912]{0:T(1024)}, u32[]{:S(2)}) copy-start(f32[6912]{0:T(1024)} %copy-done.4) | copy-start | bytes 82948
  98.6 5.6 %copy-start.7 = (f32[6912]{0:T(1024)S(1)}, f32[6912]{0:T(1024)}, u32[]{:S(2)}) copy-start(f32[6912]{0:T(1024)} %copy-done.6) | copy-start | bytes 82948
  (35 other events, 39.1 us)

commit v5 on v4

--- a/solution.py
+++ b/solution.py
@@ -338,13 +338,14 @@
     weight_one, weight_two, taps_one, taps_two = gather_weights(pw_one, pw_two, dw_one, dw_two)
     rim_width = 1
     wide_input = extended(density, (("own", 1), ("space", 2)), rim_width)
+    grad_second = backmap(weight_two, cotangent).astype(jnp.bfloat16)
+    second_padded = extended(grad_second, (("own", 1), ("space", 2)), 1)
     first = depthwise(wide_input, taps_one, extent_x, extent_y, 1).astype(jnp.bfloat16)
     pre = pointwise(weight_one, first)
+    second_padded, pre = lax.optimization_barrier((second_padded, pre))
     act = jax.nn.silu(pre).astype(jnp.bfloat16)
     act_padded = extended(act, (("own", 1), ("space", 2)), 1)
     second = depthwise(act_padded, taps_two, extent_x, extent_y, 1).astype(jnp.bfloat16)
-    grad_second = backmap(weight_two, cotangent).astype(jnp.bfloat16)
-    second_padded = extended(grad_second, (("own", 1), ("space", 2)), 1)
     sigma = jax.nn.sigmoid(pre)
     grad_pre = (
         depthwise(second_padded, taps_two, extent_x, extent_y, -1)

time: 153 us -> 165 us (1.078)
  other arithmetic: 23.9 us -> 32.4 us
  starting transfers between devices: 36.8 us -> 29.9 us
  local copies, waits for them, and re-layouts: 11.2 us -> 17.9 us
  waiting for transfers between devices: 29 us -> 33.8 us
  matrix products: 12.5 us -> 10.5 us
    ppermute x4, starting transfers between devices: 20.4 us -> 4.77 us  [extended(): after = lax.ppermute(first, axis, down)]
    ppermute x4, starting transfers between devices: 5.36 us -> 15 us  [extended(): before = lax.ppermute(last, axis, up)]
    convert_element_type x0 -> x1, other arithmetic: none -> 7.59 us  [shards(): grad_pre = (depthwise(second_padded, taps_two, extent_x, extent_y, -1) *...]
    dot_general x1, matrix products: 4.62 us -> 1.32 us  [pointwise(): jnp.dot(weights.T, flattened, preferred_element_type=jnp.float32)]
    ppermute x4, waiting for transfers between devices: 28.3 us -> 31 us  [extended(): theirs = lax.ppermute(jnp.concatenate([first, last], axis=dim), axis, up)]
    ppermute x4, waiting for transfers between devices: 0.01 us -> 2.75 us  [extended(): after = lax.ppermute(first, axis, down)]
    unnamed x235 -> x253, local copies, waits for them, and re-layouts: 7.14 us -> 9.76 us
    optimization_barrier x0 -> x1, local copies, waits for them, and re-layouts: none -> 2.6 us  [shards(): second_padded, pre = lax.optimization_barrier((second_padded, pre))]
  transfers between devices with their start and end apart: 13 -> 13, of which waited for: 6 -> 4; matrix products, arithmetic and copies ran while one was open for 18% -> 18% of each run, Pallas kernels for 24% -> 22%
where the time goes in v5:
time: 165 us; the launch traced here: 164 us
  Pallas kernels  36.6 us (22%)
  waiting for transfers between devices  33.8 us (20%)
  other arithmetic  32.4 us (20%)
  starting transfers between devices  29.9 us (18%)
  local copies, waits for them, and re-layouts  17.9 us (11%)
  matrix products  10.5 us (6%)
  between operations  3.15 us (2%)
    pallas_call x1, Pallas kernels, tree_reduce(): pl.pallas_call(functools.partial(reduce_kernel, plan), out_shape=jax.Shap...  36.6 us
    ppermute x4, waiting for transfers between devices, extended(): theirs = lax.ppermute(jnp.concatenate([first, last], axis=dim), axis, up)  31 us
    ppermute x4, starting transfers between devices, extended(): before = lax.ppermute(last, axis, up)  15 us
    unnamed x253, local copies, waits for them, and re-layouts  9.76 us
    convert_element_type x1, other arithmetic, shards(): grad_pre = (depthwise(second_padded, taps_two, extent_x, extent_y, -1) *...  7.59 us
    reduce_sum x3, other arithmetic, tap_sums(): jnp.sum(shifted.astype(jnp.float32) * grad_float, axis=(1, 2, 3))  6.46 us
    ppermute x4, starting transfers between devices, extended(): theirs = lax.ppermute(jnp.concatenate([first, last], axis=dim), axis, up)  6.26 us
    dot_general x2, matrix products, contract_cells(): lax.dot_general(left.reshape(channels, -1), right.reshape(channels, -1),...  4.78 us
  transfers between devices with their start and end apart: 13, of which 4 were waited for; matrix products, arithmetic and copies ran while one was open for 18% of the time, Pallas kernels for 22%

profile of v5, /device:TPU:1, one launch (start us, length us, event | category | flops | bytes accessed | tf_op | source)
XLA Modules:
  0.0 164.2 jit_solution(6967529456275650221)
XLA Ops:
  0.6 0.9 copy.54
  1.6 0.9 copy.55
  2.5 0.7 pad_maximum_fusion.50
  3.2 3.8 %collective-permute-start = (bf16[72448]{0:T(1024)(128)(2,1)S(1)}, bf16[72448]{0:T(1024)(128)(2,1)S(1)}, u32[]{:S(2)}, u32[]{:S(2)}) collective-permute-start(bf16[72448]{0:T(1024)(128)(2,1)S(1)} %pad_maximum_fusion.50), channel_id=1, source_target_pairs={{0,128},{128,0},{1,129},{129,1},{2,130},{130,2},{3,131},{131,3},{4... | collective-permute-start | bytes 434696 | tf_op jit(solution)/shard_map/ppermute | solution.py:42
  7.1 1.3 copy.31
  8.4 0.1 collective-permute-start.4
  8.5 1.1 copy.27
  9.7 0.4 reshape.544
  10.1 0.2 copy.30
  10.5 0.3 convolution_convert_fusion.1
  10.8 3.0 %collective-permute-start.1 = (bf16[256,2,4,128]{0,3,2,1:T(8,128)(2,1)S(1)}, bf16[256,2,4,128]{0,3,2,1:T(8,128)(2,1)S(1)}, u32[]{:S(2)}, u32[]{:S(2)}) collective-permute-start(bf16[256,2,4,128]{0,3,2,1:T(8,128)(2,1)S(1)} %convolution_convert_fusion.1), channel_id=1, source_target_pairs={{0,128},{128,0},{1,129},{129,1},{2,130},{130,2},{3,131},{131,3},{4... | collective-permute-start | bytes 1572872 | tf_op jit(solution)/shard_map/ppermute | solution.py:30
  13.8 0.6 fusion.264
  14.5 0.6 fusion.282
  15.1 0.6 fusion.273
  15.7 0.6 fusion.238
  16.3 0.6 fusion.256
  17.0 0.7 copy.28
  17.8 0.7 copy.29
  18.6 4.0 %collective-permute-done.4 = bf16[256,2,4,128]{0,3,2,1:T(8,128)(2,1)S(1)} collective-permute-done((bf16[256,2,4,128]{0,3,2,1:T(8,128)(2,1)S(1)}, bf16[256,2,4,128]{0,3,2,1:T(8,128)(2,1)S(1)}, u32[]{:S(2)}, u32[]{:S(2)}) %collective-permute-start.4) | collective-permute-done | bytes 524320 | tf_op jit(solution)/shard_map/ppermute | solution.py:30
  22.7 3.6 %collective-permute-start.5 = (bf16[256,4,1,128]{0,3,2,1:T(8,128)(2,1)S(1)}, bf16[256,4,1,128]{0,3,2,1:T(8,128)(2,1)S(1)}, u32[]{:S(2)}, u32[]{:S(2)}) collective-permute-start(bf16[256,4,1,128]{0,3,2,1:T(8,128)(2,1)S(1)} %get-tuple-element.115), channel_id=1, source_target_pairs={{0,1},{1,2},{2,3},{3,4},{4,5},{5,6},{6,7},{7,8},{8,9},{9,10},{10,1... | collective-permute-start | bytes 786440 | tf_op jit(solution)/shard_map/ppermute | solution.py:34
  26.3 10.4 %collective-permute-done.1 = bf16[256,2,4,128]{0,3,2,1:T(8,128)(2,1)S(1)} collective-permute-done((bf16[256,2,4,128]{0,3,2,1:T(8,128)(2,1)S(1)}, bf16[256,2,4,128]{0,3,2,1:T(8,128)(2,1)S(1)}, u32[]{:S(2)}, u32[]{:S(2)}) %collective-permute-start.1) | collective-permute-done | bytes 524320 | tf_op jit(solution)/shard_map/ppermute | solution.py:30
  36.8 2.1 %collective-permute-start.2 = (bf16[256,4,1,128]{0,3,2,1:T(8,128)(2,1)S(1)}, bf16[256,4,1,128]{0,3,2,1:T(8,128)(2,1)S(1)}, u32[]{:S(2)}, u32[]{:S(2)}) collective-permute-start(bf16[256,4,1,128]{0,3,2,1:T(8,128)(2,1)S(1)} %get-tuple-element.117), channel_id=1, source_target_pairs={{0,1},{1,2},{2,3},{3,4},{4,5},{5,6},{6,7},{7,8},{8,9},{9,10},{10,1... | collective-permute-start | bytes 786440 | tf_op jit(solution)/shard_map/ppermute | solution.py:34
  38.9 1.5 collective-permute-start.3
  40.3 0.3 fusion.4
  40.7 0.7 fusion.5
  41.5 0.2 maximum_maximum_fusion
  41.9 0.7 copy-done.2
  42.7 4.3 %fusion.34 = bf16[256,2,4,128]{0,3,2,1:T(8,128)(2,1)S(1)} fusion(bf16[256,2,4,128]{0,3,2,1:T(8,128)(2,1)S(1)} %copy.31, f32[256]{0:T(256)S(1)} %bitcast.184, f32[256]{0:T(256)S(1)} %bitcast.186, f32[256]{0:T(256)S(1)} %bitcast.182, f32[256]{0:T(256)S(1)} %bitcast.180, f32[256]{0:T(256)S(1)} %bitcast.178, f32[256]{0:T(256)S(1)} %bitcast.176, ...), kind=kLoop, calls=%fused_computation.194 | loop fusion | flops 21757952 | bytes 14183424 | tf_op jit(solution)/shard_map/convert_element_type | solution.py:343
  47.1 1.3 fusion.149
  48.5 0.2 pad_maximum_fusion.24
  48.7 2.6 %copy.36 = f32[256,2,4,128]{0,3,2,1:T(8,128)} copy(f32[256,2,4,128]{3,0,2,1:T(8,128)} %fusion.149) | data formatting | bytes 2097152 | tf_op jit(solution)/shard_map/optimization_barrier | solution.py:345
  51.4 7.6 %multiply_convert_fusion.1 = bf16[256,2,4,128]{0,3,2,1:T(8,128)(2,1)S(1)} fusion(f32[256,2,4,128]{0,3,2,1:T(8,128)} %copy.36, bf16[256,4,6,128]{0,3,2,1:T(8,128)(2,1)S(1)} %pad_maximum_fusion.24, bf16[256,4,6,1]{0,3,2,1:T(2,128)(2,1)S(1)} %get-tuple-element.104, bf16[256,4,6,1]{0,3,2,1:T(2,128)(2,1)S(1)} %get-tuple-element.103, f32[256]{0:T(256)} %bitcast.238, ...), kind=kLoop, calls=%fused_computation.292 | loop fusion | flops 37486592 | bytes 7941120 | tf_op jit(solution)/shard_map/convert_element_type | solution.py:353
  59.0 4.0 %fusion.129 = (f32[256]{0:T(256)S(1)}, f32[256]{0:T(256)S(1)}, f32[256]{0:T(256)S(1)}, f32[256]{0:T(256)S(1)}, f32[256]{0:T(256)S(1)}, /*index=5*/f32[256]{0:T(2...) fusion(bf16[256,4,5,128]{0,3,2,1:T(8,128)(2,1)} %copy-done.11, ...), kind=kOutput, calls=%fused_computation.289 | convolution fusion | flops 144438272 | bytes 7483392 | tf_op jit(solution)/shard_map/dot_general | solution.py:92
  63.1 0.3 fusion.7
  63.4 0.3 multiply_convert_fusion
  63.7 0.4 copy-done.1
  64.1 0.4 copy-done.4
  64.6 2.6 %fusion.130 = (f32[256]{0:T(256)S(1)}, f32[256]{0:T(256)S(1)}, f32[256]{0:T(256)S(1)}, f32[256]{0:T(256)S(1)}, f32[256]{0:T(256)S(1)}, /*index=5*/f32[256]{0:T(2...) fusion(bf16[256,2,4,128]{0,3,2,1:T(8,128)(2,1)S(1)} %get-tuple-, ...), kind=kLoop, calls=%fused_computation.290 | loop fusion | flops 12579072 | bytes 7879680 | tf_op jit(solution)/shard_map/reduce_sum | solution.py:79
  67.2 1.9 %collective-permute-start.7 = (bf16[256,2,4,128]{0,3,2,1:T(8,128)(2,1)S(1)}, bf16[256,2,4,128]{0,3,2,1:T(8,128)(2,1)S(1)}, u32[]{:S(2)}, u32[]{:S(2)}) collective-permute-start(bf16[256,2,4,128]{0,3,2,1:T(8,128)(2,1)S(1)} %get-tuple-element.307), channel_id=1, source_target_pairs={{0,128},{128,0},{1,129},{129,1},{2,130},{130,2},{3,131},{131,3},{4... | collective-permute-start | bytes 1572872 | tf_op jit(solution)/shard_map/ppermute | solution.py:30
  69.4 1.3 collective-permute-start.10
  71.1 16.6 %collective-permute-done.10 = bf16[256,2,4,128]{0,3,2,1:T(8,128)(2,1)S(1)} collective-permute-done((bf16[256,2,4,128]{0,3,2,1:T(8,128)(2,1)S(1)}, bf16[256,2,4,128]{0,3,2,1:T(8,128)(2,1)S(1)}, u32[]{:S(2)}, u32[]{:S(2)}) %collective-permute-start.10) | collective-permute-done | bytes 524320 | tf_op jit(solution)/shard_map/ppermute | solution.py:30
  87.8 7.6 %collective-permute-start.11 = (bf16[256,4,1,128]{0,3,2,1:T(8,128)(2,1)S(1)}, bf16[256,4,1,128]{0,3,2,1:T(8,128)(2,1)S(1)}, u32[]{:S(2)}, u32[]{:S(2)}) collective-permute-start(bf16[256,4,1,128]{0,3,2,1:T(8,128)(2,1)S(1)} %get-tuple-element.107), channel_id=1, source_target_pairs={{0,1},{1,2},{2,3},{3,4},{4,5},{5,6},{6,7},{7,8},{8,9},{9,10},{10,1... | collective-permute-start | bytes 786440 | tf_op jit(solution)/shard_map/ppermute | solution.py:34
  95.5 0.9 pad_maximum_fusion.43
  96.4 1.7 %collective-permute-start.8 = (bf16[256,4,1,128]{0,3,2,1:T(8,128)(2,1)}, bf16[256,4,1,128]{0,3,2,1:T(8,128)(2,1)S(1)}, u32[]{:S(2)}, u32[]{:S(2)}) collective-permute-start(bf16[256,4,1,128]{0,3,2,1:T(8,128)(2,1)} %get-tuple-element.111), channel_id=1, source_target_pairs={{0,1},{1,2},{2,3},{3,4},{4,5},{5,6},{6,7},{7,8},{8,9},{9,10},{10,1... | collective-permute-start | bytes 786440 | tf_op jit(solution)/shard_map/ppermute | solution.py:34
  98.1 3.3 %collective-permute-start.9 = (bf16[256,4,1,128]{0,3,2,1:T(8,128)(2,1)}, bf16[256,4,1,128]{0,3,2,1:T(8,128)(2,1)S(1)}, u32[]{:S(2)}, u32[]{:S(2)}) collective-permute-start(bf16[256,4,1,128]{0,3,2,1:T(8,128)(2,1)} %get-tuple-element.112), channel_id=1, source_target_pairs={{1,0},{2,1},{3,2},{4,3},{5,4},{6,5},{7,6},{8,7},{9,8},{10,9},{11,1... | collective-permute-start | bytes 786440 | tf_op jit(solution)/shard_map/ppermute | solution.py:35
  101.4 2.7 %collective-permute-done.12 = bf16[256,4,1,128]{0,3,2,1:T(8,128)(2,1)S(1)} collective-permute-done((bf16[256,4,1,128]{0,3,2,1:T(8,128)(2,1)S(1)}, bf16[256,4,1,128]{0,3,2,1:T(8,128)(2,1)S(1)}, u32[]{:S(2)}, u32[]{:S(2)}) %collective-permute-start.12) | collective-permute-done | bytes 262176 | tf_op jit(solution)/shard_map/ppermute | solution.py:35
  104.1 0.3 fusion
  104.5 0.2 maximum_maximum_fusion.2
  104.7 0.8 copy-done.7
  105.5 2.5 %fusion.88 = (f32[256]{0:T(256)S(1)}, f32[256]{0:T(256)S(1)}, f32[256]{0:T(256)S(1)}, f32[256]{0:T(256)S(1)}, f32[256]{0:T(256)S(1)}, /*index=5*/f32[256]{0:T(25...) fusion(bf16[256,2,4,128]{0,3,2,1:T(8,128)(2,1)S(1)} %copy-done., ...), kind=kLoop, calls=%fused_computation.248 | loop fusion | flops 12579072 | bytes 7879680 | tf_op jit(solution)/shard_map/reduce_sum | solution.py:79
  108.1 0.7 fusion.1
  109.1 1.3 fusion.87
  110.7 4.4 %fusion.6 = f32[256,256]{1,0:T(8,128)S(1)} fusion(bf16[256,2,4,128]{0,3,2,1:T(8,128)(2,1)S(1)} %copy-done.12, bf16[256,2,4,128]{0,3,2,1:T(8,128)(2,1)S(1)} %multiply_convert_fusion, f32[256]{0:T(256)S(1)} %bitcast.239, f32[256]{0:T(256)S(1)} %bitcast.241, f32[256]{0:T(256)S(1)} %bitcast.237, f32[256]{0:T(256)S(1)} %bitcast.235, f32[256]{0:T(256)S(1)} %bitcast.233, ...), kind=kOutput, calls=%fused_computation.165 | convolution fusion | flops 156041216 | bytes 14445568 | tf_op jit(solution)/shard_map/dot_general | solution.py:97
  116.0 0.8 copy-done.16
  116.8 36.6 %shard_map.101 = f32[80,8,128]{2,1,0:T(8,128)} custom-call(f32[160,8,128]{2,1,0:T(8,128)} %copy-done.16), custom_call_target="tpu_custom_call" | custom-call | bytes 41943040 | tf_op jit(solution)/shard_map/pallas_call | solution.py:278
  153.4 0.8 slice_bitcast_fusion
  154.3 1.7 %fusion.293 = (f32[32,8,128]{2,1,0:T(8,128)}, f32[32,8,128]{2,1,0:T(8,128)}) fusion(f32[80,8,128]{2,1,0:T(8,128)} %shard_map.101), kind=kLoop, calls=%fused_computation.775 | loop fusion | bytes 524288 | tf_op jit(solution)/shard_map/slice | solution.py:324
  156.0 0.7 fusion.2
  156.7 0.3 fusion.3
  157.3 0.2 pad_maximum_fusion.26
  157.5 0.2 copy-done.25
  157.9 4.6 %fusion.131 = bf16[256,2,4,128]{0,3,2,1:T(8,128)(2,1)S(1)} fusion(bf16[256,2,4,128]{0,3,2,1:T(8,128)(2,1)S(1)} %get-tuple-element.307, bf16[256,2,4,128]{0,3,2,1:T(8,128)(2,1)S(1)} %copy-done.12, bf16[256,4,6,129]{0,3,2,1:T(8,128)(2,1)S(1)} %fusion.2, bf16[256,4,5,128]{0,3,2,1:T(8,128)(2,1)S(1)} %get-tuple-element.110, ...), kind=kLoop, calls=%fused_computation.294 | loop fusion | flops 22282240 | bytes 14707712 | tf_op jit(solution)/shard_map/convert_element_type | solution.py:358
  162.5 1.1 copy.44
  163.6 0.6 fusion.298
  (329 shorter events, 1.9 us)
Async XLA Ops:
  0.6 7.9 %copy-start.15 = (bf16[256,2,4,128]{3,2,1,0:T(4,128)(2,1)S(1)}, bf16[256,2,4,128]{3,2,1,0:T(4,128)(2,1)}, u32[]{:S(2)}) copy-start(bf16[256,2,4,128]{3,2,1,0:T(4,128)(2,1)} %param.7) | copy-start | bytes 1572868
  3.2 7.1 %collective-permute-start = (bf16[72448]{0:T(1024)(128)(2,1)S(1)}, bf16[72448]{0:T(1024)(128)(2,1)S(1)}, u32[]{:S(2)}, u32[]{:S(2)}) collective-permute-start(bf16[72448]{0:T(1024)(128)(2,1)S(1)} %pad_maximum_fusion.50), channel_id=1, source_target_pairs={{0,128},{128,0},{1,129},{129,1},{2,130},{130,2},{3,131},{131,3},{4... | collective-permute-start | bytes 434696 | tf_op jit(solution)/shard_map/ppermute | solution.py:42
  8.4 33.4 %copy-start = (bf16[256,2,4,128]{0,3,2,1:T(8,128)(2,1)}, bf16[256,2,4,128]{0,3,2,1:T(8,128)(2,1)S(1)}, u32[]{:S(2)}) copy-start(bf16[256,2,4,128]{0,3,2,1:T(8,128)(2,1)S(1)} %copy.31) | copy-start | bytes 1572868
  8.4 1.9 %copy-start.21 = (bf16[27,128]{1,0:T(8,128)(2,1)S(1)}, bf16[27,128]{1,0:T(8,128)(2,1)}, u32[]{:S(2)}) copy-start(bf16[27,128]{1,0:T(8,128)(2,1)} %param.11) | copy-start | bytes 20740
  8.4 1.9 %copy-start.22 = (bf16[27,128]{1,0:T(8,128)(2,1)S(1)}, bf16[27,128]{1,0:T(8,128)(2,1)}, u32[]{:S(2)}) copy-start(bf16[27,128]{1,0:T(8,128)(2,1)} %param.10) | copy-start | bytes 20740
  8.4 14.2 %collective-permute-start.4 = (bf16[256,2,4,128]{0,3,2,1:T(8,128)(2,1)S(1)}, bf16[256,2,4,128]{0,3,2,1:T(8,128)(2,1)S(1)}, u32[]{:S(2)}, u32[]{:S(2)}) collective-permute-start(bf16[256,2,4,128]{0,3,2,1:T(8,128)(2,1)S(1)} %copy.31), channel_id=1, source_target_pairs={{0,128},{128,0},{1,129},{129,1},{2,130},{130,2},{3,131},{131,3},{4... | collective-permute-start | bytes 1572872 | tf_op jit(solution)/shard_map/ppermute | solution.py:30
  10.8 25.9 %copy-start.5 = (bf16[256,2,4,128]{0,3,2,1:T(8,128)(2,1)}, bf16[256,2,4,128]{0,3,2,1:T(8,128)(2,1)S(1)}, u32[]{:S(2)}) copy-start(bf16[256,2,4,128]{0,3,2,1:T(8,128)(2,1)S(1)} %convolution_convert_fusion.1) | copy-start | bytes 1572868
  10.8 25.8 %collective-permute-start.1 = (bf16[256,2,4,128]{0,3,2,1:T(8,128)(2,1)S(1)}, bf16[256,2,4,128]{0,3,2,1:T(8,128)(2,1)S(1)}, u32[]{:S(2)}, u32[]{:S(2)}) collective-permute-start(bf16[256,2,4,128]{0,3,2,1:T(8,128)(2,1)S(1)} %convolution_convert_fusion.1), channel_id=1, source_target_pairs={{0,128},{128,0},{1,129},{129,1},{2,130},{130,2},{3,131},{131,3},{4... | collective-permute-start | bytes 1572872 | tf_op jit(solution)/shard_map/ppermute | solution.py:30
  18.5 23.3 %copy-start.50 = (f32[1,256]{1,0:T(1,128)}, f32[1,256]{1,0:T(1,128)S(1)}, u32[]{:S(2)}) copy-start(f32[1,256]{1,0:T(1,128)S(1)} %get-tuple-element.181) | copy-start | bytes 3076
  18.5 23.3 %copy-start.52 = (f32[1,256]{1,0:T(1,128)}, f32[1,256]{1,0:T(1,128)S(1)}, u32[]{:S(2)}) copy-start(f32[1,256]{1,0:T(1,128)S(1)} %get-tuple-element.182) | copy-start | bytes 3076
  18.5 23.3 %copy-start.54 = (f32[1,256]{1,0:T(1,128)}, f32[1,256]{1,0:T(1,128)S(1)}, u32[]{:S(2)}) copy-start(f32[1,256]{1,0:T(1,128)S(1)} %get-tuple-element.183) | copy-start | bytes 3076
  18.5 23.3 %copy-start.56 = (f32[1,256]{1,0:T(1,128)}, f32[1,256]{1,0:T(1,128)S(1)}, u32[]{:S(2)}) copy-start(f32[1,256]{1,0:T(1,128)S(1)} %get-tuple-element.184) | copy-start | bytes 3076
  18.5 23.3 %copy-start.58 = (f32[1,256]{1,0:T(1,128)}, f32[1,256]{1,0:T(1,128)S(1)}, u32[]{:S(2)}) copy-start(f32[1,256]{1,0:T(1,128)S(1)} %get-tuple-element.185) | copy-start | bytes 3076
  18.5 23.3 %copy-start.60 = (f32[1,256]{1,0:T(1,128)}, f32[1,256]{1,0:T(1,128)S(1)}, u32[]{:S(2)}) copy-start(f32[1,256]{1,0:T(1,128)S(1)} %get-tuple-element.186) | copy-start | bytes 3076
  18.6 23.3 %copy-start.62 = (f32[1,256]{1,0:T(1,128)}, f32[1,256]{1,0:T(1,128)S(1)}, u32[]{:S(2)}) copy-start(f32[1,256]{1,0:T(1,128)S(1)} %get-tuple-element.187) | copy-start | bytes 3076
  18.6 23.3 %copy-start.64 = (f32[1,256]{1,0:T(1,128)}, f32[1,256]{1,0:T(1,128)S(1)}, u32[]{:S(2)}) copy-start(f32[1,256]{1,0:T(1,128)S(1)} %get-tuple-element.188) | copy-start | bytes 3076
  18.6 23.3 %copy-start.66 = (f32[1,256]{1,0:T(1,128)}, f32[1,256]{1,0:T(1,128)S(1)}, u32[]{:S(2)}) copy-start(f32[1,256]{1,0:T(1,128)S(1)} %get-tuple-element.189) | copy-start | bytes 3076
  22.7 19.2 %copy-start.8 = (bf16[256,1,4,128]{0,3,2,1:T(8,128)(2,1)}, bf16[256,1,4,128]{0,3,2,1:T(8,128)(2,1)S(1)}, u32[]{:S(2)}) copy-start(bf16[256,1,4,128]{0,3,2,1:T(8,128)(2,1)S(1)} %get-tuple-element.124) | copy-start | bytes 786436
  22.7 17.6 %collective-permute-start.5 = (bf16[256,4,1,128]{0,3,2,1:T(8,128)(2,1)S(1)}, bf16[256,4,1,128]{0,3,2,1:T(8,128)(2,1)S(1)}, u32[]{:S(2)}, u32[]{:S(2)}) collective-permute-start(bf16[256,4,1,128]{0,3,2,1:T(8,128)(2,1)S(1)} %get-tuple-element.115), channel_id=1, source_target_pairs={{0,1},{1,2},{2,3},{3,4},{4,5},{5,6},{6,7},{7,8},{8,9},{9,10},{10,1... | collective-permute-start | bytes 786440 | tf_op jit(solution)/shard_map/ppermute | solution.py:34
  26.3 14.0 %collective-permute-start.6 = (bf16[256,4,1,128]{0,3,2,1:T(8,128)(2,1)S(1)}, bf16[256,4,1,128]{0,3,2,1:T(8,128)(2,1)S(1)}, u32[]{:S(2)}, u32[]{:S(2)}) collective-permute-start(bf16[256,4,1,128]{0,3,2,1:T(8,128)(2,1)S(1)} %get-tuple-element.116), channel_id=1, source_target_pairs={{1,0},{2,1},{3,2},{4,3},{5,4},{6,5},{7,6},{8,7},{9,8},{10,9},{11,1... | collective-permute-start | bytes 786440 | tf_op jit(solution)/shard_map/ppermute | solution.py:35
  36.8 11.7 %collective-permute-start.2 = (bf16[256,4,1,128]{0,3,2,1:T(8,128)(2,1)S(1)}, bf16[256,4,1,128]{0,3,2,1:T(8,128)(2,1)S(1)}, u32[]{:S(2)}, u32[]{:S(2)}) collective-permute-start(bf16[256,4,1,128]{0,3,2,1:T(8,128)(2,1)S(1)} %get-tuple-element.117), channel_id=1, source_target_pairs={{0,1},{1,2},{2,3},{3,4},{4,5},{5,6},{6,7},{7,8},{8,9},{9,10},{10,1... | collective-permute-start | bytes 786440 | tf_op jit(solution)/shard_map/ppermute | solution.py:34
  38.9 9.6 %collective-permute-start.3 = (bf16[256,4,1,128]{0,3,2,1:T(8,128)(2,1)S(1)}, bf16[256,4,1,128]{0,3,2,1:T(8,128)(2,1)S(1)}, u32[]{:S(2)}, u32[]{:S(2)}) collective-permute-start(bf16[256,4,1,128]{0,3,2,1:T(8,128)(2,1)S(1)} %get-tuple-element.118), channel_id=1, source_target_pairs={{1,0},{2,1},{3,2},{4,3},{5,4},{6,5},{7,6},{8,7},{9,8},{10,9},{11,1... | collective-permute-start | bytes 786440 | tf_op jit(solution)/shard_map/ppermute | solution.py:35
  41.7 5.3 %copy-start.3 = (bf16[256,4,5,128]{0,3,2,1:T(8,128)(2,1)}, bf16[256,4,5,128]{0,3,2,1:T(8,128)(2,1)S(1)}, u32[]{:S(2)}) copy-start(bf16[256,4,5,128]{0,3,2,1:T(8,128)(2,1)S(1)} %get-tuple-element.113) | copy-start | bytes 3932164
  41.8 5.3 %copy-start.11 = (bf16[256,4,5,128]{0,3,2,1:T(8,128)(2,1)}, bf16[256,4,5,128]{0,3,2,1:T(8,128)(2,1)S(1)}, u32[]{:S(2)}) copy-start(bf16[256,4,5,128]{0,3,2,1:T(8,128)(2,1)S(1)} %get-tuple-element.114) | copy-start | bytes 3932164
  42.7 4.4 %copy-start.17 = (bf16[128,256]{0,1:T(8,128)(2,1)S(1)}, bf16[128,256]{0,1:T(8,128)(2,1)}, u32[]{:S(2)}) copy-start(bf16[128,256]{0,1:T(8,128)(2,1)} %copy.28) | copy-start | bytes 196612
  42.7 4.4 %copy-start.19 = (bf16[128,256]{0,1:T(8,128)(2,1)S(1)}, bf16[128,256]{0,1:T(8,128)(2,1)}, u32[]{:S(2)}) copy-start(bf16[128,256]{0,1:T(8,128)(2,1)} %copy.29) | copy-start | bytes 196612
  51.4 7.6 %copy-start.18 = (bf16[128,256]{0,1:T(8,128)(2,1)S(1)}, bf16[128,256]{0,1:T(8,128)(2,1)}, u32[]{:S(2)}) copy-start(bf16[128,256]{0,1:T(8,128)(2,1)} %copy.28) | copy-start | bytes 196612
  51.4 7.6 %copy-start.20 = (bf16[128,256]{0,1:T(8,128)(2,1)S(1)}, bf16[128,256]{0,1:T(8,128)(2,1)}, u32[]{:S(2)}) copy-start(bf16[128,256]{0,1:T(8,128)(2,1)} %copy.29) | copy-start | bytes 196612
  59.0 4.1 %copy-start.14 = (bf16[256,2,4,128]{0,3,2,1:T(8,128)(2,1)S(1)}, bf16[256,2,4,128]{0,3,2,1:T(8,128)(2,1)}, u32[]{:S(2)}) copy-start(bf16[256,2,4,128]{0,3,2,1:T(8,128)(2,1)} %copy-done.13) | copy-start | bytes 1572868
  59.0 4.4 %copy-start.10 = (f32[256,2,4,128]{0,3,2,1:T(8,128)S(1)}, f32[256,2,4,128]{0,3,2,1:T(8,128)}, u32[]{:S(2)}) copy-start(f32[256,2,4,128]{0,3,2,1:T(8,128)} %copy.36) | copy-start | bytes 3145732
  64.6 6.1 %copy-start.23 = (f32[6912]{0:T(1024)S(1)}, f32[6912]{0:T(1024)}, u32[]{:S(2)}) copy-start(f32[6912]{0:T(1024)} %custom-call.1) | copy-start | bytes 82948
  67.2 28.3 %collective-permute-start.7 = (bf16[256,2,4,128]{0,3,2,1:T(8,128)(2,1)S(1)}, bf16[256,2,4,128]{0,3,2,1:T(8,128)(2,1)S(1)}, u32[]{:S(2)}, u32[]{:S(2)}) collective-permute-start(bf16[256,2,4,128]{0,3,2,1:T(8,128)(2,1)S(1)} %get-tuple-element.307), channel_id=1, source_target_pairs={{0,128},{128,0},{1,129},{129,1},{2,130},{130,2},{3,131},{131,3},{4... | collective-permute-start | bytes 1572872 | tf_op jit(solution)/shard_map/ppermute | solution.py:30
  69.4 18.4 %collective-permute-start.10 = (bf16[256,2,4,128]{0,3,2,1:T(8,128)(2,1)S(1)}, bf16[256,2,4,128]{0,3,2,1:T(8,128)(2,1)S(1)}, u32[]{:S(2)}, u32[]{:S(2)}) collective-permute-start(bf16[256,2,4,128]{0,3,2,1:T(8,128)(2,1)S(1)} %multiply_convert_fusion), channel_id=1, source_target_pairs={{0,128},{128,0},{1,129},{129,1},{2,130},{130,2},{3,131},{131,3},{4... | collective-permute-start | bytes 1572872 | tf_op jit(solution)/shard_map/ppermute | solution.py:30
  87.8 13.6 %collective-permute-start.11 = (bf16[256,4,1,128]{0,3,2,1:T(8,128)(2,1)S(1)}, bf16[256,4,1,128]{0,3,2,1:T(8,128)(2,1)S(1)}, u32[]{:S(2)}, u32[]{:S(2)}) collective-permute-start(bf16[256,4,1,128]{0,3,2,1:T(8,128)(2,1)S(1)} %get-tuple-element.107), channel_id=1, source_target_pairs={{0,1},{1,2},{2,3},{3,4},{4,5},{5,6},{6,7},{7,8},{8,9},{9,10},{10,1... | collective-permute-start | bytes 786440 | tf_op jit(solution)/shard_map/ppermute | solution.py:34
  95.4 8.7 %collective-permute-start.12 = (bf16[256,4,1,128]{0,3,2,1:T(8,128)(2,1)S(1)}, bf16[256,4,1,128]{0,3,2,1:T(8,128)(2,1)S(1)}, u32[]{:S(2)}, u32[]{:S(2)}) collective-permute-start(bf16[256,4,1,128]{0,3,2,1:T(8,128)(2,1)S(1)} %get-tuple-element.108), channel_id=1, source_target_pairs={{1,0},{2,1},{3,2},{4,3},{5,4},{6,5},{7,6},{8,7},{9,8},{10,9},{11,1... | collective-permute-start | bytes 786440 | tf_op jit(solution)/shard_map/ppermute | solution.py:35
  96.4 59.6 %collective-permute-start.8 = (bf16[256,4,1,128]{0,3,2,1:T(8,128)(2,1)}, bf16[256,4,1,128]{0,3,2,1:T(8,128)(2,1)S(1)}, u32[]{:S(2)}, u32[]{:S(2)}) collective-permute-start(bf16[256,4,1,128]{0,3,2,1:T(8,128)(2,1)} %get-tuple-element.111), channel_id=1, source_target_pairs={{0,1},{1,2},{2,3},{3,4},{4,5},{5,6},{6,7},{7,8},{8,9},{9,10},{10,1... | collective-permute-start | bytes 786440 | tf_op jit(solution)/shard_map/ppermute | solution.py:34
  98.1 57.9 %collective-permute-start.9 = (bf16[256,4,1,128]{0,3,2,1:T(8,128)(2,1)}, bf16[256,4,1,128]{0,3,2,1:T(8,128)(2,1)S(1)}, u32[]{:S(2)}, u32[]{:S(2)}) collective-permute-start(bf16[256,4,1,128]{0,3,2,1:T(8,128)(2,1)} %get-tuple-element.112), channel_id=1, source_target_pairs={{1,0},{2,1},{3,2},{4,3},{5,4},{6,5},{7,6},{8,7},{9,8},{10,9},{11,1... | collective-permute-start | bytes 786440 | tf_op jit(solution)/shard_map/ppermute | solution.py:35
  108.8 1.6 copy-start.12
  108.8 1.6 copy-start.68
  108.8 1.6 copy-start.69
  108.8 1.6 copy-start.70
  108.8 1.6 copy-start.71
  108.8 1.6 copy-start.72
  108.8 1.6 copy-start.73
  108.8 1.6 copy-start.74
  108.9 1.6 copy-start.75
  108.9 1.6 copy-start.76
  108.9 1.6 copy-start.77
  108.9 1.6 copy-start.78
  108.9 1.6 copy-start.79
  108.9 1.6 copy-start.80
  108.9 1.6 copy-start.81
  108.9 1.6 copy-start.82
  108.9 1.6 copy-start.83
  108.9 1.6 copy-start.84
  109.0 1.6 copy-start.85
  109.0 1.6 copy-start.86
  109.0 1.6 copy-start.87
  109.0 1.6 copy-start.88
  109.0 1.6 copy-start.89
  109.0 1.6 copy-start.90
  109.0 1.6 copy-start.91
  109.0 1.6 copy-start.92
  109.0 1.6 copy-start.93
  (44 other events, 41.7 us)

commit v6 on v5

--- a/solution.py
+++ b/solution.py
@@ -339,6 +339,7 @@
     rim_width = 1
     wide_input = extended(density, (("own", 1), ("space", 2)), rim_width)
     grad_second = backmap(weight_two, cotangent).astype(jnp.bfloat16)
+    grad_second, wide_input = lax.optimization_barrier((grad_second, wide_input))
     second_padded = extended(grad_second, (("own", 1), ("space", 2)), 1)
     first = depthwise(wide_input, taps_one, extent_x, extent_y, 1).astype(jnp.bfloat16)
     pre = pointwise(weight_one, first)

time: 165 us -> 173 us (1.048)
  starting transfers between devices: 29.9 us -> 38.1 us
  other arithmetic: 32.4 us -> 40 us
  matrix products: 10.5 us -> 8.26 us
  waiting for transfers between devices: 33.8 us -> 31.6 us
  local copies, waits for them, and re-layouts: 17.9 us -> 16 us
    ppermute x4, starting transfers between devices: 4.77 us -> 26.8 us  [extended(): after = lax.ppermute(first, axis, down)]
    ppermute x4, starting transfers between devices: 15 us -> 0.3 us  [extended(): before = lax.ppermute(last, axis, up)]
    ppermute x4, waiting for transfers between devices: 31 us -> 21.1 us  [extended(): theirs = lax.ppermute(jnp.concatenate([first, last], axis=dim), axis, up)]
    ppermute x4, waiting for transfers between devices: 0.01 us -> 7.29 us  [extended(): before = lax.ppermute(last, axis, up)]
    optimization_barrier x1 -> x0, local copies, waits for them, and re-layouts: 2.6 us -> none  [shards(): second_padded, pre = lax.optimization_barrier((second_padded, pre))]
    convert_element_type x1, other arithmetic: 4.33 us -> 6.52 us  [shards(): depthwise(wide_input, taps_one, extent_x, extent_y, 1).astype(jnp.bfloat16)]
    dot_general x2, matrix products: 4.36 us -> 2.43 us  [backmap(): jnp.dot(weights, flattened, preferred_element_type=jnp.float32)]
    reduce_sum x3 -> x4, other arithmetic: 6.46 us -> 8.17 us  [tap_sums(): jnp.sum(shifted.astype(jnp.float32) * grad_float, axis=(1, 2, 3))]
  transfers between devices with their start and end apart: 13 -> 13, of which waited for: 4 -> 7; matrix products, arithmetic and copies ran while one was open for 18% -> 21% of each run, Pallas kernels for 22% -> 20%
where the time goes in v6:
time: 173 us; the launch traced here: 172 us
  other arithmetic  40 us (23%)
  starting transfers between devices  38.1 us (22%)
  Pallas kernels  35 us (20%)
  waiting for transfers between devices  31.6 us (18%)
  local copies, waits for them, and re-layouts  16 us (9%)
  matrix products  8.26 us (5%)
  between operations  3.34 us (2%)
    pallas_call x1, Pallas kernels, tree_reduce(): pl.pallas_call(functools.partial(reduce_kernel, plan), out_shape=jax.Shap...  35 us
    ppermute x4, starting transfers between devices, extended(): after = lax.ppermute(first, axis, down)  26.8 us
    ppermute x4, waiting for transfers between devices, extended(): theirs = lax.ppermute(jnp.concatenate([first, last], axis=dim), axis, up)  21.1 us
    unnamed x287, local copies, waits for them, and re-layouts  8.34 us
    reduce_sum x4, other arithmetic, tap_sums(): jnp.sum(shifted.astype(jnp.float32) * grad_float, axis=(1, 2, 3))  8.17 us
    convert_element_type x1, other arithmetic, shards(): grad_pre = (depthwise(second_padded, taps_two, extent_x, extent_y, -1) *...  7.86 us
    ppermute x4, waiting for transfers between devices, extended(): before = lax.ppermute(last, axis, up)  7.29 us
    ppermute x4, starting transfers between devices, extended(): theirs = lax.ppermute(jnp.concatenate([first, last], axis=dim), axis, up)  7.16 us
  transfers between devices with their start and end apart: 13, of which 7 were waited for; matrix products, arithmetic and copies ran while one was open for 21% of the time, Pallas kernels for 20%

profile of v6, /device:TPU:1, one launch (start us, length us, event | category | flops | bytes accessed | tf_op | source)
XLA Modules:
  0.0 172.4 jit_solution(4319159460357090831)
XLA Ops:
  0.6 0.9 copy.38
  1.6 0.9 copy.37
  2.5 0.7 pad_maximum_fusion.36
  3.2 3.8 %collective-permute-start = (bf16[72448]{0:T(1024)(128)(2,1)S(1)}, bf16[72448]{0:T(1024)(128)(2,1)S(1)}, u32[]{:S(2)}, u32[]{:S(2)}) collective-permute-start(bf16[72448]{0:T(1024)(128)(2,1)S(1)} %pad_maximum_fusion.36), channel_id=1, source_target_pairs={{0,128},{128,0},{1,129},{129,1},{2,130},{130,2},{3,131},{131,3},{4... | collective-permute-start | bytes 434696 | tf_op jit(solution)/shard_map/ppermute | solution.py:42
  7.1 1.3 copy.23
  8.5 0.4 reshape.544
  8.9 1.1 copy.19
  10.0 0.2 copy.22
  10.4 0.6 fusion.250
  11.0 0.6 fusion.259
  11.6 0.6 fusion.268
  12.2 0.6 fusion.276
  12.9 0.6 fusion.285
  13.5 9.2 %collective-permute-done.1 = bf16[256,2,4,128]{0,3,2,1:T(8,128)(2,1)} collective-permute-done((bf16[256,2,4,128]{0,3,2,1:T(8,128)(2,1)S(1)}, bf16[256,2,4,128]{0,3,2,1:T(8,128)(2,1)}, u32[]{:S(2)}, u32[]{:S(2)}) %collective-permute-start.1) | collective-permute-done | bytes 524320 | tf_op jit(solution)/shard_map/ppermute | solution.py:30
  22.7 1.1 fusion.306
  23.9 1.9 %collective-permute-start.3 = (bf16[256,4,1,128]{0,3,2,1:T(8,128)(2,1)S(1)}, bf16[256,4,1,128]{0,3,2,1:T(8,128)(2,1)S(1)}, u32[]{:S(2)}, u32[]{:S(2)}) collective-permute-start(bf16[256,4,1,128]{0,3,2,1:T(8,128)(2,1)S(1)} %get-tuple-element.114), channel_id=1, source_target_pairs={{1,0},{2,1},{3,2},{4,3},{5,4},{6,5},{7,6},{8,7},{9,8},{10,9},{11,1... | collective-permute-start | bytes 786440 | tf_op jit(solution)/shard_map/ppermute | solution.py:35
  25.7 0.3 collective-permute-start.2
  26.0 0.6 fusion.294
  26.8 0.1 copy.21
  26.9 0.1 copy.20
  27.0 0.3 convolution_convert_fusion.1
  27.6 2.4 %collective-permute-done.3 = bf16[256,4,1,128]{0,3,2,1:T(8,128)(2,1)S(1)} collective-permute-done((bf16[256,4,1,128]{0,3,2,1:T(8,128)(2,1)S(1)}, bf16[256,4,1,128]{0,3,2,1:T(8,128)(2,1)S(1)}, u32[]{:S(2)}, u32[]{:S(2)}) %collective-permute-start.3) | collective-permute-done | bytes 262176 | tf_op jit(solution)/shard_map/ppermute | solution.py:35
  30.0 3.2 %collective-permute-done.2 = bf16[256,4,1,128]{0,3,2,1:T(8,128)(2,1)} collective-permute-done((bf16[256,4,1,128]{0,3,2,1:T(8,128)(2,1)S(1)}, bf16[256,4,1,128]{0,3,2,1:T(8,128)(2,1)}, u32[]{:S(2)}, u32[]{:S(2)}) %collective-permute-start.2) | collective-permute-done | bytes 262176 | tf_op jit(solution)/shard_map/ppermute | solution.py:34
  33.2 1.2 pad_maximum_fusion.9
  34.5 3.1 %collective-permute-start.4 = (bf16[256,2,4,128]{3,0,2,1:T(8,128)(2,1)S(1)}, bf16[256,2,4,128]{3,0,2,1:T(8,128)(2,1)S(1)}, u32[]{:S(2)}, u32[]{:S(2)}) collective-permute-start(bf16[256,2,4,128]{3,0,2,1:T(8,128)(2,1)S(1)} %convolution_convert_fusion.1), channel_id=1, source_target_pairs={{0,128},{128,0},{1,129},{129,1},{2,130},{130,2},{3,131},{131,3},{4... | collective-permute-start | bytes 1572872 | tf_op jit(solution)/shard_map/ppermute | solution.py:30
  37.8 6.5 %fusion.30 = (bf16[256,2,4,128]{0,3,2,1:T(8,128)(2,1)S(1)}, bf16[256,2,4,128]{0,3,2,1:T(8,128)(2,1)}, bf16[256,2,4,128]{0,3,2,1:T(8,128)(2,1)}) fusion(f32[256]{0:T(256)S(1)} %bitcast.184, f32[256]{0:T(256)S(1)} %bitcast.186, f32[256]{0:T(256)S(1)} %bitcast.182, f32[256]{0:T(256)S(1)} %bitcast.180, f32[256]{0:T(256)S(1)} %bitcast.178, f32[256]{0:T(256)S(1)} %bitcast.176, ...), kind=kLoop, calls=%fused_computation.208 | loop fusion | flops 35913728 | bytes 7941120 | tf_op jit(solution)/shard_map/convert_element_type | solution.py:344
  44.5 12.2 %collective-permute-start.6 = (bf16[256,4,1,128]{3,0,2,1:T(8,128)(2,1)S(1)}, bf16[256,4,1,128]{3,0,2,1:T(8,128)(2,1)S(1)}, u32[]{:S(2)}, u32[]{:S(2)}) collective-permute-start(bf16[256,4,1,128]{3,0,2,1:T(8,128)(2,1)S(1)} %get-tuple-element.112), channel_id=1, source_target_pairs={{1,0},{2,1},{3,2},{4,3},{5,4},{6,5},{7,6},{8,7},{9,8},{10,9},{11,1... | collective-permute-start | bytes 786440 | tf_op jit(solution)/shard_map/ppermute | solution.py:35
  56.7 0.3 fusion.161
  57.0 0.8 collective-permute-done.6
  57.8 2.2 %collective-permute-done.5 = bf16[256,4,1,128]{3,0,2,1:T(8,128)(2,1)S(1)} collective-permute-done((bf16[256,4,1,128]{3,0,2,1:T(8,128)(2,1)S(1)}, bf16[256,4,1,128]{3,0,2,1:T(8,128)(2,1)S(1)}, u32[]{:S(2)}, u32[]{:S(2)}) %collective-permute-start.5) | collective-permute-done | bytes 262176 | tf_op jit(solution)/shard_map/ppermute | solution.py:34
  60.0 0.2 pad_maximum_fusion.10
  60.5 0.7 fusion.301
  61.5 7.9 %multiply_convert_fusion.1 = bf16[256,2,4,128]{3,0,2,1:T(8,128)(2,1)S(1)} fusion(f32[256,2,4,128]{3,0,2,1:T(8,128)S(1)} %fusion.161, bf16[256,4,6,1]{3,0,2,1:T(8,128)(2,1)S(1)} %get-tuple-element.100, bf16[256,4,6,128]{3,0,2,1:T(8,128)(2,1)S(1)} %pad_maximum_fusion.10, bf16[256,4,6,1]{3,0,2,1:T(8,128)(2,1)S(1)} %get-tuple-element.99, f32[256]{0:T(256)S(1)} %bitcast.238, ...), kind=kLoop, calls=%fused_computation.306 | loop fusion | flops 37486592 | bytes 11037696 | tf_op jit(solution)/shard_map/convert_element_type | solution.py:354
  69.3 1.0 copy.25
  70.3 0.3 fusion.3
  70.7 0.9 copy-done.1
  71.6 0.3 multiply_convert_fusion
  71.9 2.1 %fusion.121 = (f32[256]{0:T(256)S(1)}, f32[256]{0:T(256)S(1)}, f32[256]{0:T(256)S(1)}, f32[256]{0:T(256)S(1)}, f32[256]{0:T(256)S(1)}, /*index=5*/f32[256]{0:T(2...) fusion(bf16[256,4,6,128]{0,3,2,1:T(8,128)(2,1)S(1)} %pad_maximum_fusion.9, ...), kind=kOutput, calls=%fused_computation.299 | convolution fusion | flops 148371200 | bytes 3298304 | tf_op jit(solution)/shard_map/dot_general | solution.py:92
  74.0 3.8 %collective-permute-start.7 = (bf16[256,2,4,128]{0,3,2,1:T(8,128)(2,1)S(1)}, bf16[256,2,4,128]{0,3,2,1:T(8,128)(2,1)S(1)}, u32[]{:S(2)}, u32[]{:S(2)}) collective-permute-start(bf16[256,2,4,128]{0,3,2,1:T(8,128)(2,1)S(1)} %get-tuple-element.303), channel_id=1, source_target_pairs={{0,128},{128,0},{1,129},{129,1},{2,130},{130,2},{3,131},{131,3},{4... | collective-permute-start | bytes 1572872 | tf_op jit(solution)/shard_map/ppermute | solution.py:30
  77.8 2.7 %fusion.123 = (f32[256]{0:T(256)S(1)}, f32[256]{0:T(256)S(1)}, f32[256]{0:T(256)S(1)}, f32[256]{0:T(256)S(1)}, f32[256]{0:T(256)S(1)}, /*index=5*/f32[256]{0:T(256)S(1)}, f32[256]{0:T(256)S(1)}, f32[256]{0:T(256)S(1)}) fusion(bf16[256,2,4,128]{0,3,2,1:T(8,128)(2,1)S(1)} %get-tuple-element.303, bf16[256,4,6,1]{0,3,2,1:T(2,128)(2,1)S(1)} %get-tuple-element.101, ...), kind=kLoop, calls=%fused_computation.301 | loop fusion | flops 12843008 | bytes 2117632 | tf_op jit(solution)/shard_map/reduce_sum | solution.py:79
  80.5 0.1 collective-permute-start.10
  80.6 0.9 fusion.125
  82.3 11.9 %collective-permute-done.10 = bf16[256,2,4,128]{3,0,2,1:T(8,128)(2,1)S(1)} collective-permute-done((bf16[256,2,4,128]{3,0,2,1:T(8,128)(2,1)S(1)}, bf16[256,2,4,128]{3,0,2,1:T(8,128)(2,1)S(1)}, u32[]{:S(2)}, u32[]{:S(2)}) %collective-permute-start.10) | collective-permute-done | bytes 524320 | tf_op jit(solution)/shard_map/ppermute | solution.py:30
  94.3 9.9 %collective-permute-start.12 = (bf16[256,4,1,128]{3,0,2,1:T(8,128)(2,1)S(1)}, bf16[256,4,1,128]{3,0,2,1:T(8,128)(2,1)S(1)}, u32[]{:S(2)}, u32[]{:S(2)}) collective-permute-start(bf16[256,4,1,128]{3,0,2,1:T(8,128)(2,1)S(1)} %get-tuple-element.106), channel_id=1, source_target_pairs={{1,0},{2,1},{3,2},{4,3},{5,4},{6,5},{7,6},{8,7},{9,8},{10,9},{11,1... | collective-permute-start | bytes 786440 | tf_op jit(solution)/shard_map/ppermute | solution.py:35
  104.2 0.8 pad_maximum_fusion.29
  105.0 2.9 %collective-permute-start.9 = (bf16[256,4,1,128]{0,3,2,1:T(8,128)(2,1)}, bf16[256,4,1,128]{0,3,2,1:T(8,128)(2,1)S(1)}, u32[]{:S(2)}, u32[]{:S(2)}) collective-permute-start(bf16[256,4,1,128]{0,3,2,1:T(8,128)(2,1)} %get-tuple-element.110), channel_id=1, source_target_pairs={{1,0},{2,1},{3,2},{4,3},{5,4},{6,5},{7,6},{8,7},{9,8},{10,9},{11,1... | collective-permute-start | bytes 786440 | tf_op jit(solution)/shard_map/ppermute | solution.py:35
  107.9 1.9 %collective-permute-done.11 = bf16[256,4,1,128]{3,0,2,1:T(8,128)(2,1)S(1)} collective-permute-done((bf16[256,4,1,128]{3,0,2,1:T(8,128)(2,1)S(1)}, bf16[256,4,1,128]{3,0,2,1:T(8,128)(2,1)S(1)}, u32[]{:S(2)}, u32[]{:S(2)}) %collective-permute-start.11) | collective-permute-done | bytes 262176 | tf_op jit(solution)/shard_map/ppermute | solution.py:34
  109.8 0.2 pad_maximum_fusion.11
  110.0 0.7 fusion.300
  110.7 0.2 maximum_maximum_fusion.2
  110.9 3.5 %maximum_maximum_fusion = (bf16[256,4,6,129]{3,0,2,1:T(8,128)(2,1)S(1)}, bf16[256,4,6,129]{3,0,2,1:T(8,128)(2,1)S(1)}) fusion(bf16[256,4,1,128]{3,0,2,1:T(8,128)(2,1)S(1)} %collective-permute-done.12, bf16[256,1,4,128]{3,0,2,1:T(8,128)(2,1)S(1)} %get-tuple-element.115, bf16[256,2,4,128]{3,0,2,1:T(8,128)(2,1)S(1)} %multiply_convert_fusion, ...), kind=kLoop, calls=%fused_computation.103 | loop fusion | flops 19021824 | bytes 4767744 | tf_op jit(solution)/shard_map/concatenate | solution.py:56
  114.4 1.5 fusion.83
  116.3 3.1 %fusion.84 = (f32[256]{0:T(256)S(1)}, f32[256]{0:T(256)S(1)}, f32[256]{0:T(256)S(1)}, f32[256]{0:T(256)S(1)}, f32[256]{0:T(256)S(1)}, /*index=5*/f32[256]{0:T(25...) fusion(bf16[256,2,4,128]{3,0,2,1:T(8,128)(2,1)S(1)} %convolutio, ...), kind=kLoop, calls=%fused_computation.262 | loop fusion | flops 12579072 | bytes 7879680 | tf_op jit(solution)/shard_map/reduce_sum | solution.py:79
  119.6 5.2 %fusion.2 = f32[256,256]{1,0:T(8,128)S(1)} fusion(bf16[256,2,4,128]{0,3,2,1:T(8,128)(2,1)S(1)} %copy-done.2, bf16[256,2,4,128]{3,0,2,1:T(8,128)(2,1)S(1)} %multiply_convert_fusion, f32[256]{0:T(256)S(1)} %bitcast.239, f32[256]{0:T(256)S(1)} %bitcast.241, f32[256]{0:T(256)S(1)} %bitcast.237, f32[256]{0:T(256)S(1)} %bitcast.235, f32[256]{0:T(256)S(1)} %bitcast.233, ...), kind=kOutput, calls=%fused_computation.179 | convolution fusion | flops 156041216 | bytes 14445568 | tf_op jit(solution)/shard_map/dot_general | solution.py:97
  125.6 0.9 copy-done.5
  126.5 35.0 %shard_map.101 = f32[80,8,128]{2,1,0:T(8,128)} custom-call(f32[160,8,128]{2,1,0:T(8,128)} %copy-done.5), custom_call_target="tpu_custom_call" | custom-call | bytes 41943040 | tf_op jit(solution)/shard_map/pallas_call | solution.py:278
  161.5 0.8 slice_bitcast_fusion
  162.3 1.7 fusion.307
  164.0 0.7 fusion
  164.7 0.2 pad_maximum_fusion.12
  165.2 0.3 fusion.1
  165.8 4.8 %fusion.127 = bf16[256,2,4,128]{0,3,2,1:T(8,128)(2,1)S(1)} fusion(bf16[256,2,4,128]{0,3,2,1:T(8,128)(2,1)S(1)} %get-tuple-element.303, bf16[256,2,4,128]{0,3,2,1:T(8,128)(2,1)S(1)} %copy-done.2, bf16[256,4,6,129]{0,3,2,1:T(8,128)(2,1)S(1)} %fusion, bf16[256,4,5,128]{0,3,2,1:T(8,128)(2,1)S(1)} %get-tuple-element.108, bf16[256,4,6,129]{0,3,2,1:T(8,128)(2,1)S(1)} %fusion.1, ...), kind=kLoop, calls=%fused_computation.308 | loop fusion | flops 22282240 | bytes 14707712 | tf_op jit(solution)/shard_map/convert_element_type | solution.py:359
  170.7 1.1 copy.29
  171.8 0.6 fusion.312
  (364 shorter events, 2.1 us)
Async XLA Ops:
  0.6 7.9 %copy-start.3 = (bf16[256,2,4,128]{3,2,1,0:T(4,128)(2,1)S(1)}, bf16[256,2,4,128]{3,2,1,0:T(4,128)(2,1)}, u32[]{:S(2)}) copy-start(bf16[256,2,4,128]{3,2,1,0:T(4,128)(2,1)} %param.7) | copy-start | bytes 1572868
  3.2 7.0 %collective-permute-start = (bf16[72448]{0:T(1024)(128)(2,1)S(1)}, bf16[72448]{0:T(1024)(128)(2,1)S(1)}, u32[]{:S(2)}, u32[]{:S(2)}) collective-permute-start(bf16[72448]{0:T(1024)(128)(2,1)S(1)} %pad_maximum_fusion.36), channel_id=1, source_target_pairs={{0,128},{128,0},{1,129},{129,1},{2,130},{130,2},{3,131},{131,3},{4... | collective-permute-start | bytes 434696 | tf_op jit(solution)/shard_map/ppermute | solution.py:42
  8.4 14.3 %collective-permute-start.1 = (bf16[256,2,4,128]{0,3,2,1:T(8,128)(2,1)S(1)}, bf16[256,2,4,128]{0,3,2,1:T(8,128)(2,1)}, u32[]{:S(2)}, u32[]{:S(2)}) collective-permute-start(bf16[256,2,4,128]{0,3,2,1:T(8,128)(2,1)S(1)} %copy.23), channel_id=1, source_target_pairs={{0,128},{128,0},{1,129},{129,1},{2,130},{130,2},{3,131},{131,3},{4... | collective-permute-start | bytes 1572872 | tf_op jit(solution)/shard_map/ppermute | solution.py:30
  23.9 6.1 %collective-permute-start.3 = (bf16[256,4,1,128]{0,3,2,1:T(8,128)(2,1)S(1)}, bf16[256,4,1,128]{0,3,2,1:T(8,128)(2,1)S(1)}, u32[]{:S(2)}, u32[]{:S(2)}) collective-permute-start(bf16[256,4,1,128]{0,3,2,1:T(8,128)(2,1)S(1)} %get-tuple-element.114), channel_id=1, source_target_pairs={{1,0},{2,1},{3,2},{4,3},{5,4},{6,5},{7,6},{8,7},{9,8},{10,9},{11,1... | collective-permute-start | bytes 786440 | tf_op jit(solution)/shard_map/ppermute | solution.py:35
  25.7 7.5 %collective-permute-start.2 = (bf16[256,4,1,128]{0,3,2,1:T(8,128)(2,1)S(1)}, bf16[256,4,1,128]{0,3,2,1:T(8,128)(2,1)}, u32[]{:S(2)}, u32[]{:S(2)}) collective-permute-start(bf16[256,4,1,128]{0,3,2,1:T(8,128)(2,1)S(1)} %get-tuple-element.113), channel_id=1, source_target_pairs={{0,1},{1,2},{2,3},{3,4},{4,5},{5,6},{6,7},{7,8},{8,9},{9,10},{10,1... | collective-permute-start | bytes 786440 | tf_op jit(solution)/shard_map/ppermute | solution.py:34
  27.4 10.3 %copy-start.12 = (f32[1,256]{1,0:T(1,128)S(1)}, f32[1,256]{1,0:T(1,128)}, u32[]{:S(2)}) copy-start(f32[1,256]{1,0:T(1,128)} %get-tuple-element.190) | copy-start | bytes 3076
  27.4 10.2 %copy-start.14 = (f32[1,256]{1,0:T(1,128)S(1)}, f32[1,256]{1,0:T(1,128)}, u32[]{:S(2)}) copy-start(f32[1,256]{1,0:T(1,128)} %get-tuple-element.191) | copy-start | bytes 3076
  27.4 10.2 %copy-start.16 = (f32[1,256]{1,0:T(1,128)S(1)}, f32[1,256]{1,0:T(1,128)}, u32[]{:S(2)}) copy-start(f32[1,256]{1,0:T(1,128)} %get-tuple-element.192) | copy-start | bytes 3076
  27.4 10.2 %copy-start.18 = (f32[1,256]{1,0:T(1,128)S(1)}, f32[1,256]{1,0:T(1,128)}, u32[]{:S(2)}) copy-start(f32[1,256]{1,0:T(1,128)} %get-tuple-element.193) | copy-start | bytes 3076
  27.4 10.2 %copy-start.20 = (f32[1,256]{1,0:T(1,128)S(1)}, f32[1,256]{1,0:T(1,128)}, u32[]{:S(2)}) copy-start(f32[1,256]{1,0:T(1,128)} %get-tuple-element.194) | copy-start | bytes 3076
  27.4 10.2 %copy-start.22 = (f32[1,256]{1,0:T(1,128)S(1)}, f32[1,256]{1,0:T(1,128)}, u32[]{:S(2)}) copy-start(f32[1,256]{1,0:T(1,128)} %get-tuple-element.177) | copy-start | bytes 3076
  27.4 10.2 %copy-start.24 = (f32[1,256]{1,0:T(1,128)S(1)}, f32[1,256]{1,0:T(1,128)}, u32[]{:S(2)}) copy-start(f32[1,256]{1,0:T(1,128)} %get-tuple-element.178) | copy-start | bytes 3076
  27.4 10.2 %copy-start.26 = (f32[1,256]{1,0:T(1,128)S(1)}, f32[1,256]{1,0:T(1,128)}, u32[]{:S(2)}) copy-start(f32[1,256]{1,0:T(1,128)} %get-tuple-element.179) | copy-start | bytes 3076
  27.5 10.2 %copy-start.28 = (f32[1,256]{1,0:T(1,128)S(1)}, f32[1,256]{1,0:T(1,128)}, u32[]{:S(2)}) copy-start(f32[1,256]{1,0:T(1,128)} %get-tuple-element.180) | copy-start | bytes 3076
  27.5 10.2 %copy-start.30 = (f32[1,256]{1,0:T(1,128)S(1)}, f32[1,256]{1,0:T(1,128)}, u32[]{:S(2)}) copy-start(f32[1,256]{1,0:T(1,128)} %get-tuple-element.181) | copy-start | bytes 3076
  27.5 10.2 %copy-start.32 = (f32[1,256]{1,0:T(1,128)S(1)}, f32[1,256]{1,0:T(1,128)}, u32[]{:S(2)}) copy-start(f32[1,256]{1,0:T(1,128)} %get-tuple-element.182) | copy-start | bytes 3076
  27.5 10.2 %copy-start.34 = (f32[1,256]{1,0:T(1,128)S(1)}, f32[1,256]{1,0:T(1,128)}, u32[]{:S(2)}) copy-start(f32[1,256]{1,0:T(1,128)} %get-tuple-element.183) | copy-start | bytes 3076
  27.5 10.2 %copy-start.36 = (f32[1,256]{1,0:T(1,128)S(1)}, f32[1,256]{1,0:T(1,128)}, u32[]{:S(2)}) copy-start(f32[1,256]{1,0:T(1,128)} %get-tuple-element.184) | copy-start | bytes 3076
  27.5 10.2 %copy-start.38 = (f32[1,256]{1,0:T(1,128)S(1)}, f32[1,256]{1,0:T(1,128)}, u32[]{:S(2)}) copy-start(f32[1,256]{1,0:T(1,128)} %get-tuple-element.185) | copy-start | bytes 3076
  27.5 10.2 %copy-start.40 = (f32[1,256]{1,0:T(1,128)S(1)}, f32[1,256]{1,0:T(1,128)}, u32[]{:S(2)}) copy-start(f32[1,256]{1,0:T(1,128)} %get-tuple-element.168) | copy-start | bytes 3076
  27.5 10.2 %copy-start.42 = (f32[1,256]{1,0:T(1,128)S(1)}, f32[1,256]{1,0:T(1,128)}, u32[]{:S(2)}) copy-start(f32[1,256]{1,0:T(1,128)} %get-tuple-element.169) | copy-start | bytes 3076
  27.5 10.2 %copy-start.44 = (f32[1,256]{1,0:T(1,128)S(1)}, f32[1,256]{1,0:T(1,128)}, u32[]{:S(2)}) copy-start(f32[1,256]{1,0:T(1,128)} %get-tuple-element.170) | copy-start | bytes 3076
  27.5 10.2 %copy-start.46 = (f32[1,256]{1,0:T(1,128)S(1)}, f32[1,256]{1,0:T(1,128)}, u32[]{:S(2)}) copy-start(f32[1,256]{1,0:T(1,128)} %get-tuple-element.171) | copy-start | bytes 3076
  27.6 10.2 %copy-start.48 = (f32[1,256]{1,0:T(1,128)S(1)}, f32[1,256]{1,0:T(1,128)}, u32[]{:S(2)}) copy-start(f32[1,256]{1,0:T(1,128)} %get-tuple-element.172) | copy-start | bytes 3076
  27.6 10.2 %copy-start.50 = (f32[1,256]{1,0:T(1,128)S(1)}, f32[1,256]{1,0:T(1,128)}, u32[]{:S(2)}) copy-start(f32[1,256]{1,0:T(1,128)} %get-tuple-element.173) | copy-start | bytes 3076
  27.6 10.2 %copy-start.52 = (f32[1,256]{1,0:T(1,128)S(1)}, f32[1,256]{1,0:T(1,128)}, u32[]{:S(2)}) copy-start(f32[1,256]{1,0:T(1,128)} %get-tuple-element.174) | copy-start | bytes 3076
  27.6 10.2 %copy-start.54 = (f32[1,256]{1,0:T(1,128)S(1)}, f32[1,256]{1,0:T(1,128)}, u32[]{:S(2)}) copy-start(f32[1,256]{1,0:T(1,128)} %get-tuple-element.175) | copy-start | bytes 3076
  27.6 10.2 %copy-start.56 = (f32[1,256]{1,0:T(1,128)S(1)}, f32[1,256]{1,0:T(1,128)}, u32[]{:S(2)}) copy-start(f32[1,256]{1,0:T(1,128)} %get-tuple-element.176) | copy-start | bytes 3076
  34.5 9.9 %collective-permute-start.4 = (bf16[256,2,4,128]{3,0,2,1:T(8,128)(2,1)S(1)}, bf16[256,2,4,128]{3,0,2,1:T(8,128)(2,1)S(1)}, u32[]{:S(2)}, u32[]{:S(2)}) collective-permute-start(bf16[256,2,4,128]{3,0,2,1:T(8,128)(2,1)S(1)} %convolution_convert_fusion.1), channel_id=1, source_target_pairs={{0,128},{128,0},{1,129},{129,1},{2,130},{130,2},{3,131},{131,3},{4... | collective-permute-start | bytes 1572872 | tf_op jit(solution)/shard_map/ppermute | solution.py:30
  44.5 13.4 %collective-permute-start.6 = (bf16[256,4,1,128]{3,0,2,1:T(8,128)(2,1)S(1)}, bf16[256,4,1,128]{3,0,2,1:T(8,128)(2,1)S(1)}, u32[]{:S(2)}, u32[]{:S(2)}) collective-permute-start(bf16[256,4,1,128]{3,0,2,1:T(8,128)(2,1)S(1)} %get-tuple-element.112), channel_id=1, source_target_pairs={{1,0},{2,1},{3,2},{4,3},{5,4},{6,5},{7,6},{8,7},{9,8},{10,9},{11,1... | collective-permute-start | bytes 786440 | tf_op jit(solution)/shard_map/ppermute | solution.py:35
  56.7 3.3 %collective-permute-start.5 = (bf16[256,4,1,128]{3,0,2,1:T(8,128)(2,1)S(1)}, bf16[256,4,1,128]{3,0,2,1:T(8,128)(2,1)S(1)}, u32[]{:S(2)}, u32[]{:S(2)}) collective-permute-start(bf16[256,4,1,128]{3,0,2,1:T(8,128)(2,1)S(1)} %get-tuple-element.111), channel_id=1, source_target_pairs={{0,1},{1,2},{2,3},{3,4},{4,5},{5,6},{6,7},{7,8},{8,9},{9,10},{10,1... | collective-permute-start | bytes 786440 | tf_op jit(solution)/shard_map/ppermute | solution.py:34
  57.0 4.2 %copy-start = (f32[256,2,4,128]{3,0,2,1:T(8,128)}, f32[256,2,4,128]{3,0,2,1:T(8,128)S(1)}, u32[]{:S(2)}) copy-start(f32[256,2,4,128]{3,0,2,1:T(8,128)S(1)} %fusion.161) | copy-start | bytes 3145732
  74.0 6.6 %copy-start.4 = (bf16[256,2,4,128]{0,3,2,1:T(8,128)(2,1)S(1)}, bf16[256,2,4,128]{0,3,2,1:T(8,128)(2,1)}, u32[]{:S(2)}) copy-start(bf16[256,2,4,128]{0,3,2,1:T(8,128)(2,1)} %get-tuple-element.93) | copy-start | bytes 1572868
  74.0 30.2 %collective-permute-start.7 = (bf16[256,2,4,128]{0,3,2,1:T(8,128)(2,1)S(1)}, bf16[256,2,4,128]{0,3,2,1:T(8,128)(2,1)S(1)}, u32[]{:S(2)}, u32[]{:S(2)}) collective-permute-start(bf16[256,2,4,128]{0,3,2,1:T(8,128)(2,1)S(1)} %get-tuple-element.303), channel_id=1, source_target_pairs={{0,128},{128,0},{1,129},{129,1},{2,130},{130,2},{3,131},{131,3},{4... | collective-permute-start | bytes 1572872 | tf_op jit(solution)/shard_map/ppermute | solution.py:30
  80.5 13.7 %collective-permute-start.10 = (bf16[256,2,4,128]{3,0,2,1:T(8,128)(2,1)S(1)}, bf16[256,2,4,128]{3,0,2,1:T(8,128)(2,1)S(1)}, u32[]{:S(2)}, u32[]{:S(2)}) collective-permute-start(bf16[256,2,4,128]{3,0,2,1:T(8,128)(2,1)S(1)} %multiply_convert_fusion), channel_id=1, source_target_pairs={{0,128},{128,0},{1,129},{129,1},{2,130},{130,2},{3,131},{131,3},{4... | collective-permute-start | bytes 1572872 | tf_op jit(solution)/shard_map/ppermute | solution.py:30
  94.3 13.6 %collective-permute-start.12 = (bf16[256,4,1,128]{3,0,2,1:T(8,128)(2,1)S(1)}, bf16[256,4,1,128]{3,0,2,1:T(8,128)(2,1)S(1)}, u32[]{:S(2)}, u32[]{:S(2)}) collective-permute-start(bf16[256,4,1,128]{3,0,2,1:T(8,128)(2,1)S(1)} %get-tuple-element.106), channel_id=1, source_target_pairs={{1,0},{2,1},{3,2},{4,3},{5,4},{6,5},{7,6},{8,7},{9,8},{10,9},{11,1... | collective-permute-start | bytes 786440 | tf_op jit(solution)/shard_map/ppermute | solution.py:35
  104.2 5.6 %collective-permute-start.11 = (bf16[256,4,1,128]{3,0,2,1:T(8,128)(2,1)S(1)}, bf16[256,4,1,128]{3,0,2,1:T(8,128)(2,1)S(1)}, u32[]{:S(2)}, u32[]{:S(2)}) collective-permute-start(bf16[256,4,1,128]{3,0,2,1:T(8,128)(2,1)S(1)} %get-tuple-element.105), channel_id=1, source_target_pairs={{0,1},{1,2},{2,3},{3,4},{4,5},{5,6},{6,7},{7,8},{8,9},{9,10},{10,1... | collective-permute-start | bytes 786440 | tf_op jit(solution)/shard_map/ppermute | solution.py:34
  105.0 59.0 %collective-permute-start.9 = (bf16[256,4,1,128]{0,3,2,1:T(8,128)(2,1)}, bf16[256,4,1,128]{0,3,2,1:T(8,128)(2,1)S(1)}, u32[]{:S(2)}, u32[]{:S(2)}) collective-permute-start(bf16[256,4,1,128]{0,3,2,1:T(8,128)(2,1)} %get-tuple-element.110), channel_id=1, source_target_pairs={{1,0},{2,1},{3,2},{4,3},{5,4},{6,5},{7,6},{8,7},{9,8},{10,9},{11,1... | collective-permute-start | bytes 786440 | tf_op jit(solution)/shard_map/ppermute | solution.py:35
  107.8 56.2 %collective-permute-start.8 = (bf16[256,4,1,128]{0,3,2,1:T(8,128)(2,1)S(1)}, bf16[256,4,1,128]{0,3,2,1:T(8,128)(2,1)S(1)}, u32[]{:S(2)}, u32[]{:S(2)}) collective-permute-start(bf16[256,4,1,128]{0,3,2,1:T(8,128)(2,1)S(1)} %get-tuple-element.109), channel_id=1, source_target_pairs={{0,1},{1,2},{2,3},{3,4},{4,5},{5,6},{6,7},{7,8},{8,9},{9,10},{10,1... | collective-permute-start | bytes 786440 | tf_op jit(solution)/shard_map/ppermute | solution.py:34
  116.0 3.4 %copy-start.2 = (bf16[256,2,4,128]{0,3,2,1:T(8,128)(2,1)S(1)}, bf16[256,2,4,128]{0,3,2,1:T(8,128)(2,1)}, u32[]{:S(2)}) copy-start(bf16[256,2,4,128]{0,3,2,1:T(8,128)(2,1)} %copy.19) | copy-start | bytes 1572868
  116.0 3.4 %copy-start.59 = (f32[1,256]{1,0:T(1,128)S(1)}, f32[1,256]{1,0:T(1,128)}, u32[]{:S(2)}) copy-start(f32[1,256]{1,0:T(1,128)} %get-tuple-element.159) | copy-start | bytes 3076
  116.0 3.4 %copy-start.61 = (f32[1,256]{1,0:T(1,128)S(1)}, f32[1,256]{1,0:T(1,128)}, u32[]{:S(2)}) copy-start(f32[1,256]{1,0:T(1,128)} %get-tuple-element.160) | copy-start | bytes 3076
  116.0 3.4 %copy-start.63 = (f32[1,256]{1,0:T(1,128)S(1)}, f32[1,256]{1,0:T(1,128)}, u32[]{:S(2)}) copy-start(f32[1,256]{1,0:T(1,128)} %get-tuple-element.161) | copy-start | bytes 3076
  116.0 3.4 %copy-start.65 = (f32[1,256]{1,0:T(1,128)S(1)}, f32[1,256]{1,0:T(1,128)}, u32[]{:S(2)}) copy-start(f32[1,256]{1,0:T(1,128)} %get-tuple-element.162) | copy-start | bytes 3076
  116.0 3.4 %copy-start.67 = (f32[1,256]{1,0:T(1,128)S(1)}, f32[1,256]{1,0:T(1,128)}, u32[]{:S(2)}) copy-start(f32[1,256]{1,0:T(1,128)} %get-tuple-element.163) | copy-start | bytes 3076
  116.0 3.4 %copy-start.69 = (f32[1,256]{1,0:T(1,128)S(1)}, f32[1,256]{1,0:T(1,128)}, u32[]{:S(2)}) copy-start(f32[1,256]{1,0:T(1,128)} %get-tuple-element.164) | copy-start | bytes 3076
  116.1 3.4 %copy-start.71 = (f32[1,256]{1,0:T(1,128)S(1)}, f32[1,256]{1,0:T(1,128)}, u32[]{:S(2)}) copy-start(f32[1,256]{1,0:T(1,128)} %get-tuple-element.165) | copy-start | bytes 3076
  116.1 3.4 %copy-start.73 = (f32[1,256]{1,0:T(1,128)S(1)}, f32[1,256]{1,0:T(1,128)}, u32[]{:S(2)}) copy-start(f32[1,256]{1,0:T(1,128)} %get-tuple-element.166) | copy-start | bytes 3076
  116.1 3.4 %copy-start.75 = (f32[1,256]{1,0:T(1,128)S(1)}, f32[1,256]{1,0:T(1,128)}, u32[]{:S(2)}) copy-start(f32[1,256]{1,0:T(1,128)} %get-tuple-element.167) | copy-start | bytes 3076
  116.1 3.4 %copy-start.77 = (f32[1,256]{1,0:T(1,128)S(1)}, f32[1,256]{1,0:T(1,128)}, u32[]{:S(2)}) copy-start(f32[1,256]{1,0:T(1,128)} %get-tuple-element.150) | copy-start | bytes 3076
  116.1 3.4 %copy-start.79 = (f32[1,256]{1,0:T(1,128)S(1)}, f32[1,256]{1,0:T(1,128)}, u32[]{:S(2)}) copy-start(f32[1,256]{1,0:T(1,128)} %get-tuple-element.151) | copy-start | bytes 3076
  116.1 3.4 %copy-start.81 = (f32[1,256]{1,0:T(1,128)S(1)}, f32[1,256]{1,0:T(1,128)}, u32[]{:S(2)}) copy-start(f32[1,256]{1,0:T(1,128)} %get-tuple-element.152) | copy-start | bytes 3076
  116.1 3.4 %copy-start.83 = (f32[1,256]{1,0:T(1,128)S(1)}, f32[1,256]{1,0:T(1,128)}, u32[]{:S(2)}) copy-start(f32[1,256]{1,0:T(1,128)} %get-tuple-element.153) | copy-start | bytes 3076
  116.1 3.4 %copy-start.85 = (f32[1,256]{1,0:T(1,128)S(1)}, f32[1,256]{1,0:T(1,128)}, u32[]{:S(2)}) copy-start(f32[1,256]{1,0:T(1,128)} %get-tuple-element.154) | copy-start | bytes 3076
  116.1 3.4 %copy-start.87 = (f32[1,256]{1,0:T(1,128)S(1)}, f32[1,256]{1,0:T(1,128)}, u32[]{:S(2)}) copy-start(f32[1,256]{1,0:T(1,128)} %get-tuple-element.155) | copy-start | bytes 3076
  116.1 3.4 %copy-start.89 = (f32[1,256]{1,0:T(1,128)S(1)}, f32[1,256]{1,0:T(1,128)}, u32[]{:S(2)}) copy-start(f32[1,256]{1,0:T(1,128)} %get-tuple-element.156) | copy-start | bytes 3076
  116.2 3.4 %copy-start.91 = (f32[1,256]{1,0:T(1,128)S(1)}, f32[1,256]{1,0:T(1,128)}, u32[]{:S(2)}) copy-start(f32[1,256]{1,0:T(1,128)} %get-tuple-element.157) | copy-start | bytes 3076
  116.2 3.4 %copy-start.93 = (f32[1,256]{1,0:T(1,128)S(1)}, f32[1,256]{1,0:T(1,128)}, u32[]{:S(2)}) copy-start(f32[1,256]{1,0:T(1,128)} %get-tuple-element.158) | copy-start | bytes 3076
  116.2 3.4 %copy-start.95 = (f32[1,256]{1,0:T(1,128)S(1)}, f32[1,256]{1,0:T(1,128)}, u32[]{:S(2)}) copy-start(f32[1,256]{1,0:T(1,128)} %get-tuple-element.141) | copy-start | bytes 3076
  116.2 3.4 %copy-start.97 = (f32[1,256]{1,0:T(1,128)S(1)}, f32[1,256]{1,0:T(1,128)}, u32[]{:S(2)}) copy-start(f32[1,256]{1,0:T(1,128)} %get-tuple-element.142) | copy-start | bytes 3076
  116.2 3.4 %copy-start.99 = (f32[1,256]{1,0:T(1,128)S(1)}, f32[1,256]{1,0:T(1,128)}, u32[]{:S(2)}) copy-start(f32[1,256]{1,0:T(1,128)} %get-tuple-element.143) | copy-start | bytes 3076
  116.2 3.4 %copy-start.101 = (f32[1,256]{1,0:T(1,128)S(1)}, f32[1,256]{1,0:T(1,128)}, u32[]{:S(2)}) copy-start(f32[1,256]{1,0:T(1,128)} %get-tuple-element.144) | copy-start | bytes 3076
  116.2 3.4 %copy-start.103 = (f32[1,256]{1,0:T(1,128)S(1)}, f32[1,256]{1,0:T(1,128)}, u32[]{:S(2)}) copy-start(f32[1,256]{1,0:T(1,128)} %get-tuple-element.145) | copy-start | bytes 3076
  116.2 3.4 %copy-start.105 = (f32[1,256]{1,0:T(1,128)S(1)}, f32[1,256]{1,0:T(1,128)}, u32[]{:S(2)}) copy-start(f32[1,256]{1,0:T(1,128)} %get-tuple-element.146) | copy-start | bytes 3076
  (61 other events, 62.5 us)
